TPU v7x, 128 devices: a whole 4x4x4 slice. The times are simulated.
128 devices in a mesh: depth: 8 (over x_lo, z), probe: 16 (over x_hi, y, core).
Axes of the slice: x: 4 (x_hi: 2, x_lo: 2; x = x_hi * 2 + x_lo), y: 4, z: 4, core: 2. Of those that a mesh axis runs over, the one named last changes fastest.
Arguments:
- residual: bfloat16 [64, 2, 256, 256], P('probe'), may hold values from -4 to 4
- saved_waves: bfloat16 [16, 64, 2, 256, 256], P('depth', 'probe'), may hold values from -4 to 4
- object_phase: float32 [16, 384, 384], P('depth'), may hold values from -3.140625 to 3.140625
- object_amp: float32 [16, 384, 384], P('depth'), may hold values from 0.25 to 1.75
- prop_phase: float32 [256, 256], replicated, may hold values from -3.140625 to 3.140625
- offsets: int32 [64, 2], P('probe'), may hold values from 0 to 128
Outputs:
- object_grad: float32 [16, 2, 384, 384], P('depth', None, 'probe')
- probe_grad: float32 [2, 256, 256], P(None, 'probe', 'depth')
Inputs may be any that keep to these rules, and one draw needn't show every extreme that they name: `offsets`: every window lies inside the patch.
All inputs are finite; a program needn't handle non-finite values.
Results may differ from a plain program's by a relative error of at most 0.025.
The roundings to bfloat16 on the way count: a program that leaves them out, or rounds other values in their place, can miss the bound.
Values may be sent and summed in bfloat16 or wider, within the bound.
No kernel may reach another device: no remote copies, remote signals or barrier semaphores. Data moves between devices by JAX's collectives and lax.ppermute only.
A program may use at most 128 MiB of HBM per device.

v0:
```python
import math

import jax
import jax.numpy as jnp
from jax import lax
from jax.sharding import PartitionSpec as P

MB_POS = 2


def passed_along(block, axis, distance):
    devices = range(lax.axis_size(axis))
    route = [(i - distance, i) for i in devices if i - distance in devices]
    return lax.ppermute(block, axis, route)


def split_up(array, dim, length):
    dims = array.shape
    blocks = array.reshape(*dims[:dim], length, dims[dim] // length, *dims[dim + 1 :])
    return jnp.moveaxis(blocks, dim, 0)


def sent_and_summed(array, axis, dim):
    length = lax.axis_size(axis)
    blocks = lax.all_to_all(split_up(array, dim, length), axis, 0, 0, tiled=True)
    return jnp.sum(blocks, axis=0)


def picked(array, axis, root):
    return lax.dynamic_index_in_dim(lax.all_gather(array, axis), root, 0, keepdims=False)


def tables(width):
    rows = lax.broadcasted_iota(jnp.int32, (width, width), 0)
    cols = lax.broadcasted_iota(jnp.int32, (width, width), 1)
    phase = 2.0 * math.pi / width * (rows * cols % width).astype(jnp.float32)
    factor = 1.0 / math.sqrt(width)
    return (
        (jnp.cos(phase) * factor).astype(jnp.bfloat16),
        (jnp.sin(phase) * factor).astype(jnp.bfloat16),
    )


def left_first(real_part, imag_part, waves):
    block = jnp.concatenate(
        [jnp.concatenate([real_part, -imag_part], 1), jnp.concatenate([imag_part, real_part], 1)], 0
    )
    batch, _, width, _ = waves.shape
    flat = waves.reshape(batch, 2 * width, width)
    result = jnp.einsum("jk,bkl->bjl", block, flat, preferred_element_type=jnp.float32)
    return result.reshape(batch, 2, width, width)


def left_apply(real_part, imag_part, waves):
    block = jnp.concatenate(
        [jnp.concatenate([real_part, -imag_part], 1), jnp.concatenate([imag_part, real_part], 1)], 0
    )
    batch, _, width, _ = waves.shape
    flat = waves.reshape(batch, 2 * width, width)
    result = jnp.einsum(
        "jk,bkl->bjl", block.astype(jnp.float32), flat, precision=lax.Precision.HIGHEST
    )
    return result.reshape(batch, 2, width, width)


def right_apply(real_part, imag_part, waves):
    batch, _, width, _ = waves.shape
    real_table = real_part.astype(jnp.float32)
    imag_table = imag_part.astype(jnp.float32)
    wave_real = waves[:, 0].reshape(batch * width, width)
    wave_imag = waves[:, 1].reshape(batch * width, width)
    high = lax.Precision.HIGHEST
    out_real = jnp.dot(wave_real, real_table, precision=high) - jnp.dot(
        wave_imag, imag_table, precision=high
    )
    out_imag = jnp.dot(wave_real, imag_table, precision=high) + jnp.dot(
        wave_imag, real_table, precision=high
    )
    return jnp.stack([out_real, out_imag], 1).reshape(batch, 2, width, width)


def back_propagate(chi, cosine, sine, kernel_cos, kernel_sin):
    first = left_first(cosine, -sine, chi)
    spectrum = right_apply(cosine, -sine, first)
    spec_real = spectrum[:, 0]
    spec_imag = spectrum[:, 1]
    filtered = jnp.stack(
        [
            kernel_cos * spec_real + kernel_sin * spec_imag,
            kernel_cos * spec_imag - kernel_sin * spec_real,
        ],
        1,
    )
    second = left_apply(cosine, sine, filtered)
    return right_apply(cosine, sine, second)


def shards(residual, saved_waves, object_phase, object_amp, prop_phase, offsets):
    pos_count, _, width, _ = residual.shape
    section_count = lax.axis_size("depth")
    section_index = lax.axis_index("depth")
    cosine, sine = tables(width)
    kernel_cos = jnp.cos(prop_phase)
    kernel_sin = jnp.sin(prop_phase)
    transmission = jnp.stack(
        [object_amp * jnp.cos(object_phase), object_amp * jnp.sin(object_phase)], 1
    )
    zero_index = jnp.zeros((), jnp.int32)
    group_count = pos_count // MB_POS
    group_size = pos_count // group_count
    tick_count = section_count + group_count - 1

    def work(operands):
        incoming, grads, probe_sum, first = operands
        chi = incoming
        places = lax.dynamic_slice_in_dim(offsets, first, group_size, 0)
        row_starts = places[:, 0]
        col_starts = places[:, 1]
        for layer in (1, 0):
            arrived = back_propagate(chi, cosine, sine, kernel_cos, kernel_sin)
            chi_real = arrived[:, 0]
            chi_imag = arrived[:, 1]
            waves = lax.dynamic_slice_in_dim(saved_waves[layer], first, group_size, 0).astype(
                jnp.float32
            )
            psi_real = waves[:, 0]
            psi_imag = waves[:, 1]
            terms = jnp.stack(
                [
                    psi_real * chi_real + psi_imag * chi_imag,
                    psi_real * chi_imag - psi_imag * chi_real,
                ],
                1,
            )

            def deposit(position, layer_grad):
                corner = (zero_index, row_starts[position], col_starts[position])
                window = lax.dynamic_slice(layer_grad, corner, (2, width, width))
                return lax.dynamic_update_slice(layer_grad, window + terms[position], corner)

            layer_grad = lax.fori_loop(0, group_size, deposit, grads[layer])
            grads = grads.at[layer].set(layer_grad)
            layer_trans = transmission[layer]
            windows = jax.vmap(
                lambda row_at, col_at: lax.dynamic_slice(
                    layer_trans, (zero_index, row_at, col_at), (2, width, width)
                )
            )(row_starts, col_starts)
            trans_real = windows[:, 0]
            trans_imag = windows[:, 1]
            chi = jnp.stack(
                [
                    trans_real * chi_real + trans_imag * chi_imag,
                    trans_real * chi_imag - trans_imag * chi_real,
                ],
                1,
            ).astype(jnp.bfloat16)
        probe_sum = probe_sum + jnp.sum(chi.astype(jnp.float32), axis=0)
        return (chi, grads, probe_sum)

    def skip(operands):
        incoming, grads, probe_sum, first = operands
        return (jnp.zeros_like(incoming), grads, probe_sum)

    def tick(tick_now, carry):
        inbox, grads, probe_sum = carry
        group_now = tick_now - (section_count - 1 - section_index)
        active = (group_now >= 0) & (group_now < group_count)
        first = jnp.clip(group_now, 0, group_count - 1) * group_size
        fresh = lax.dynamic_slice_in_dim(residual, first, group_size, 0)
        incoming = jnp.where(section_index == section_count - 1, fresh, inbox)
        outgoing, grads, probe_sum = lax.cond(
            active, work, skip, (incoming, grads, probe_sum, first)
        )
        inbox = passed_along(outgoing, "depth", -1)
        return (inbox, grads, probe_sum)

    patch = object_phase.shape[-1]
    start_inbox = jnp.zeros((group_size, 2, width, width), jnp.bfloat16)
    start_grads = jnp.zeros((object_phase.shape[0], 2, patch, patch), jnp.float32)
    start_probe = jnp.zeros((2, width, width), jnp.float32)
    _, grads, probe_sum = lax.fori_loop(
        0, tick_count, tick, (start_inbox, start_grads, start_probe)
    )
    object_grad = sent_and_summed(grads, "probe", 2)
    total = lax.psum(probe_sum, "probe")
    rows_each = width // lax.axis_size("probe")
    own_rows = lax.dynamic_slice_in_dim(total, lax.axis_index("probe") * rows_each, rows_each, 1)
    spread_rows = picked(own_rows, "depth", 0)
    cols_each = width // section_count
    probe_grad = lax.dynamic_slice_in_dim(spread_rows, section_index * cols_each, cols_each, 2)
    return (object_grad, probe_grad)


def solution(mesh):
    return jax.shard_map(
        shards,
        mesh=mesh,
        in_specs=(
            P("probe", None, None, None),
            P("depth", "probe", None, None, None),
            P("depth", None, None),
            P("depth", None, None),
            P(),
            P("probe", None),
        ),
        out_specs=(P("depth", None, "probe", None), P(None, "probe", "depth")),
        check_vma=False,
    )
```

profile of v0, /device:TPU:0, one launch (start us, length us, event | category | flops | bytes accessed | tf_op | source)
XLA Modules:
  0.0 1384.8 jit_solution(6627573080066078283)
XLA Ops:
  7.9 2.5 fusion.36
  10.5 6.7 multiply_bitcast_fusion.1
  21.4 1126.4 %while.61 = (s32[]{:T(128)}, bf16[2,2,256,256]{3,2,1,0:T(8,128)(2,1)S(1)}, f32[2,2,384,384]{3,2,1,0:T(8,128)}, f32[2,256,256]{2,1,0:T(8,128)}, s32[]{:T(128)}, /...) while((s32[]{:T(128)}, ...), condition=%wide.region_8.9_spmd.clone.clone, body=%wide.region_0.8_spmd.clone.clone.sunk | while | flops 10220994560 | bytes 174329680 | solution.py:182
  24.6 14.8 %collective-permute-done = bf16[2,2,256,256]{3,2,1,0:T(8,128)(2,1)S(1)} collective-permute-done((bf16[2,2,256,256]{3,2,1,0:T(8,128)(2,1)}, bf16[2,2,256,256]{3,2,1,0:T(8,128)(2,1)S(1)}, u32[]{:S(2)}, u32[]{:S(2)}) %collective-permute-start) | collective-permute-done | bytes 524320 | tf_op jit(solution)/shard_map/while/body/eval_jaxpr/ppermute | solution.py:14
  42.6 14.0 %collective-permute-done = bf16[2,2,256,256]{3,2,1,0:T(8,128)(2,1)S(1)} collective-permute-done((bf16[2,2,256,256]{3,2,1,0:T(8,128)(2,1)}, bf16[2,2,256,256]{3,2,1,0:T(8,128)(2,1)S(1)}, u32[]{:S(2)}, u32[]{:S(2)}) %collective-permute-start) | collective-permute-done | bytes 524320 | tf_op jit(solution)/shard_map/while/body/eval_jaxpr/ppermute | solution.py:14
  59.9 13.1 collective-permute-done
  76.3 14.2 %collective-permute-done = bf16[2,2,256,256]{3,2,1,0:T(8,128)(2,1)S(1)} collective-permute-done((bf16[2,2,256,256]{3,2,1,0:T(8,128)(2,1)}, bf16[2,2,256,256]{3,2,1,0:T(8,128)(2,1)S(1)}, u32[]{:S(2)}, u32[]{:S(2)}) %collective-permute-start) | collective-permute-done | bytes 524320 | tf_op jit(solution)/shard_map/while/body/eval_jaxpr/ppermute | solution.py:14
  93.7 13.2 collective-permute-done
  110.1 12.3 collective-permute-done
  125.7 769.9 %collective-permute-done = bf16[2,2,256,256]{3,2,1,0:T(8,128)(2,1)S(1)} collective-permute-done((bf16[2,2,256,256]{3,2,1,0:T(8,128)(2,1)}, bf16[2,2,256,256]{3,2,1,0:T(8,128)(2,1)S(1)}, u32[]{:S(2)}, u32[]{:S(2)}) %collective-permute-start) | collective-permute-done | bytes 524320 | tf_op jit(solution)/shard_map/while/body/eval_jaxpr/ppermute | solution.py:14
  896.7 112.0 %conditional.4 = (bf16[2,2,256,256]{3,2,1,0:T(8,128)(2,1)}, f32[2,2,384,384]{3,2,1,0:T(8,128)}, f32[2,256,256]{2,1,0:T(8,128)}) conditional(s32[]{:T(128)} %convert_element_type.187, (f32[2,2,384,384]{3,2,1,0:T(8,128)}, f32[2,256,256]{2,1,0:T(8,128)}) %tuple.175, (f32[2,2,384,384]{3,2,1,0:T(8,128)}, s32[]{:T(128)}, s32[4,2]{1,0:T(4,128)S(1)}, ...), branch_computations={%region_1.1_spmd, %region_2.7_spmd} | conditional | flops 10219814912 | bytes 171969856 | solution.py:172
  911.5 3.3 slice_bitcast_fusion.2
  915.8 7.9 while.60
  916.4 3.3 bitcast_dynamic-update-slice_fusion.7
  920.3 3.3 bitcast_dynamic-update-slice_fusion.7
  924.8 6.0 while.59
  925.5 2.3 bitcast_dynamic-update-slice_fusion.6
  928.4 2.3 bitcast_dynamic-update-slice_fusion.6
  934.8 24.0 %while.57 = (s32[]{:T(128)}, f32[2,384,384]{2,1,0:T(8,128)S(1)}, s32[2]{0:T(128)S(1)}, s32[2]{0:T(128)S(1)}, f32[2,2,256,256]{3,2,1,0:T(8,128)S(1)}, /*index=5*/s32[]{:T(128)}, s32[]{:T(128)}, s32[]{:T(128)}) while((s32[]{:T(128)}, f32[2,384,384]{2,1,0:T(8,128)S(1)}, s32[2]{0:T(128)S(1)}, s32[2]{0:T(128)S(1)}, ...), condition=%wide.region_4.3_spmd, body=%wide.region_3.2_spmd.sunk | while | flops 131080 | bytes 2621641 | solution.py:141
  939.4 7.8 dynamic_update_slice.16
  951.8 6.9 dynamic_update_slice.16
  978.8 1.9 add.240
  982.2 25.3 %while.58 = (s32[]{:T(128)}, f32[2,384,384]{2,1,0:T(8,128)S(1)}, s32[2]{0:T(128)S(1)}, s32[2]{0:T(128)S(1)}, f32[2,2,256,256]{3,2,1,0:T(8,128)S(1)}, /*index=5*/s32[]{:T(128)}, s32[]{:T(128)}, s32[]{:T(128)}) while((s32[]{:T(128)}, f32[2,384,384]{2,1,0:T(8,128)S(1)}, s32[2]{0:T(128)S(1)}, s32[2]{0:T(128)S(1)}, ...), condition=%wide.region_6.5_spmd, body=%wide.region_5.4_spmd.sunk | while | flops 131080 | bytes 2621641 | solution.py:141
  987.5 7.8 dynamic_update_slice.17
  1000.6 6.9 dynamic_update_slice.17
  1010.0 13.1 collective-permute-done
  1024.2 112.3 %conditional.4 = (bf16[2,2,256,256]{3,2,1,0:T(8,128)(2,1)}, f32[2,2,384,384]{3,2,1,0:T(8,128)}, f32[2,256,256]{2,1,0:T(8,128)}) conditional(s32[]{:T(128)} %convert_element_type.187, (f32[2,2,384,384]{3,2,1,0:T(8,128)}, f32[2,256,256]{2,1,0:T(8,128)}) %tuple.175, (f32[2,2,384,384]{3,2,1,0:T(8,128)}, s32[]{:T(128)}, s32[4,2]{1,0:T(4,128)S(1)}, ...), branch_computations={%region_1.1_spmd, %region_2.7_spmd} | conditional | flops 10219814912 | bytes 171969856 | solution.py:172
  1030.7 1.9 convolution_bitcast_fusion.2
  1039.0 3.3 slice_bitcast_fusion.2
  1043.3 7.9 while.60
  1043.9 3.3 bitcast_dynamic-update-slice_fusion.7
  1047.8 3.3 bitcast_dynamic-update-slice_fusion.7
  1052.3 6.0 while.59
  1052.9 2.3 bitcast_dynamic-update-slice_fusion.6
  1055.9 2.3 bitcast_dynamic-update-slice_fusion.6
  1062.3 24.2 %while.57 = (s32[]{:T(128)}, f32[2,384,384]{2,1,0:T(8,128)S(1)}, s32[2]{0:T(128)S(1)}, s32[2]{0:T(128)S(1)}, f32[2,2,256,256]{3,2,1,0:T(8,128)S(1)}, /*index=5*/s32[]{:T(128)}, s32[]{:T(128)}, s32[]{:T(128)}) while((s32[]{:T(128)}, f32[2,384,384]{2,1,0:T(8,128)S(1)}, s32[2]{0:T(128)S(1)}, s32[2]{0:T(128)S(1)}, ...), condition=%wide.region_4.3_spmd, body=%wide.region_3.2_spmd.sunk | while | flops 131080 | bytes 2621641 | solution.py:141
  1066.9 7.7 dynamic_update_slice.16
  1079.2 7.3 dynamic_update_slice.16
  1106.5 1.9 add.240
  1109.9 25.5 %while.58 = (s32[]{:T(128)}, f32[2,384,384]{2,1,0:T(8,128)S(1)}, s32[2]{0:T(128)S(1)}, s32[2]{0:T(128)S(1)}, f32[2,2,256,256]{3,2,1,0:T(8,128)S(1)}, /*index=5*/s32[]{:T(128)}, s32[]{:T(128)}, s32[]{:T(128)}) while((s32[]{:T(128)}, f32[2,384,384]{2,1,0:T(8,128)S(1)}, s32[2]{0:T(128)S(1)}, s32[2]{0:T(128)S(1)}, ...), condition=%wide.region_6.5_spmd, body=%wide.region_5.4_spmd.sunk | while | flops 131080 | bytes 2621641 | solution.py:141
  1115.2 7.7 dynamic_update_slice.17
  1128.1 7.3 dynamic_update_slice.17
  1137.8 10.0 collective-permute-done
  1147.8 3.4 copy.54
  1151.1 49.1 %all-to-all-start = ((f32[16,2,2,24,384]{4,3,2,1,0:T(8,128)}), f32[16,2,2,24,384]{4,3,2,1,0:T(8,128)}, u32[]{:S(2)}, u32[]{:S(2)}) async-start(f32[16,2,2,24,384]{4,3,2,1,0:T(8,128)} %copy.54), calls=%async_computation | async-start | bytes 4718592 | tf_op jit(solution)/shard_map/all_to_all | solution.py:25
  1201.0 144.5 %all-reduce.2.cloned.1.call-done = f32[2,256,256]{2,1,0:T(8,128)} async-done(((f32[2,256,256]{2,1,0:T(8,128)}), f32[2,256,256]{2,1,0:T(8,128)}) %all-reduce.2.cloned.1.call-update) | async-done | bytes 524304 | tf_op jit(solution)/shard_map/psum | solution.py:186
  1346.3 28.6 %all-gather = f32[16,16,256]{2,1,0:T(8,128)S(1)} all-gather(f32[2,16,256]{2,1,0:T(8,128)S(1)} %constant_dynamic-slice_fusion.3), channel_id=2, replica_groups=mesh['depth'=8,'probe'=16] {'depth'}, dimensions={0}, use_global_device_ids=true | all-gather | bytes 294912 | tf_op jit(solution)/shard_map/all_gather | solution.py:30
  1375.6 2.4 reduce_sum.20
  (252 shorter events, 140.6 us)
Async XLA Ops:
  23.3 16.1 %collective-permute-start = (bf16[2,2,256,256]{3,2,1,0:T(8,128)(2,1)}, bf16[2,2,256,256]{3,2,1,0:T(8,128)(2,1)S(1)}, u32[]{:S(2)}, u32[]{:S(2)}) collective-permute-start(bf16[2,2,256,256]{3,2,1,0:T(8,128)(2,1)} %get-tuple-element.1207), channel_id=1, source_target_pairs={{16,0},{32,16},{48,32},{64,48},{80,64},{96,80},{112,96},{17,1},{33... | collective-permute-start | bytes 1572872 | tf_op jit(solution)/shard_map/while/body/eval_jaxpr/ppermute | solution.py:14
  41.3 15.3 %collective-permute-start = (bf16[2,2,256,256]{3,2,1,0:T(8,128)(2,1)}, bf16[2,2,256,256]{3,2,1,0:T(8,128)(2,1)S(1)}, u32[]{:S(2)}, u32[]{:S(2)}) collective-permute-start(bf16[2,2,256,256]{3,2,1,0:T(8,128)(2,1)} %get-tuple-element.1207), channel_id=1, source_target_pairs={{16,0},{32,16},{48,32},{64,48},{80,64},{96,80},{112,96},{17,1},{33... | collective-permute-start | bytes 1572872 | tf_op jit(solution)/shard_map/while/body/eval_jaxpr/ppermute | solution.py:14
  58.6 14.4 %collective-permute-start = (bf16[2,2,256,256]{3,2,1,0:T(8,128)(2,1)}, bf16[2,2,256,256]{3,2,1,0:T(8,128)(2,1)S(1)}, u32[]{:S(2)}, u32[]{:S(2)}) collective-permute-start(bf16[2,2,256,256]{3,2,1,0:T(8,128)(2,1)} %get-tuple-element.1207), channel_id=1, source_target_pairs={{16,0},{32,16},{48,32},{64,48},{80,64},{96,80},{112,96},{17,1},{33... | collective-permute-start | bytes 1572872 | tf_op jit(solution)/shard_map/while/body/eval_jaxpr/ppermute | solution.py:14
  75.0 15.5 %collective-permute-start = (bf16[2,2,256,256]{3,2,1,0:T(8,128)(2,1)}, bf16[2,2,256,256]{3,2,1,0:T(8,128)(2,1)S(1)}, u32[]{:S(2)}, u32[]{:S(2)}) collective-permute-start(bf16[2,2,256,256]{3,2,1,0:T(8,128)(2,1)} %get-tuple-element.1207), channel_id=1, source_target_pairs={{16,0},{32,16},{48,32},{64,48},{80,64},{96,80},{112,96},{17,1},{33... | collective-permute-start | bytes 1572872 | tf_op jit(solution)/shard_map/while/body/eval_jaxpr/ppermute | solution.py:14
  92.4 14.4 %collective-permute-start = (bf16[2,2,256,256]{3,2,1,0:T(8,128)(2,1)}, bf16[2,2,256,256]{3,2,1,0:T(8,128)(2,1)S(1)}, u32[]{:S(2)}, u32[]{:S(2)}) collective-permute-start(bf16[2,2,256,256]{3,2,1,0:T(8,128)(2,1)} %get-tuple-element.1207), channel_id=1, source_target_pairs={{16,0},{32,16},{48,32},{64,48},{80,64},{96,80},{112,96},{17,1},{33... | collective-permute-start | bytes 1572872 | tf_op jit(solution)/shard_map/while/body/eval_jaxpr/ppermute | solution.py:14
  108.8 13.6 collective-permute-start
  124.4 771.2 %collective-permute-start = (bf16[2,2,256,256]{3,2,1,0:T(8,128)(2,1)}, bf16[2,2,256,256]{3,2,1,0:T(8,128)(2,1)S(1)}, u32[]{:S(2)}, u32[]{:S(2)}) collective-permute-start(bf16[2,2,256,256]{3,2,1,0:T(8,128)(2,1)} %get-tuple-element.1207), channel_id=1, source_target_pairs={{16,0},{32,16},{48,32},{64,48},{80,64},{96,80},{112,96},{17,1},{33... | collective-permute-start | bytes 1572872 | tf_op jit(solution)/shard_map/while/body/eval_jaxpr/ppermute | solution.py:14
  897.0 1.7 copy-start.7
  897.1 6.2 copy-start.5
  932.5 1.6 copy-start.3
  932.5 1.9 copy-start.4
  966.8 0.9 copy-start.6
  974.2 1.7 copy-start.2
  977.8 2.9 copy-start
  980.8 1.4 copy-start.1
  1008.7 14.4 %collective-permute-start = (bf16[2,2,256,256]{3,2,1,0:T(8,128)(2,1)}, bf16[2,2,256,256]{3,2,1,0:T(8,128)(2,1)S(1)}, u32[]{:S(2)}, u32[]{:S(2)}) collective-permute-start(bf16[2,2,256,256]{3,2,1,0:T(8,128)(2,1)} %get-tuple-element.1207), channel_id=1, source_target_pairs={{16,0},{32,16},{48,32},{64,48},{80,64},{96,80},{112,96},{17,1},{33... | collective-permute-start | bytes 1572872 | tf_op jit(solution)/shard_map/while/body/eval_jaxpr/ppermute | solution.py:14
  1024.5 1.7 copy-start.7
  1024.6 6.2 copy-start.5
  1060.0 1.6 copy-start.3
  1060.0 1.9 copy-start.4
  1094.4 0.9 copy-start.6
  1101.9 1.7 copy-start.2
  1105.5 2.9 copy-start
  1108.4 1.4 copy-start.1
  1136.5 11.3 collective-permute-start
  1151.1 224.4 %all-to-all-start = ((f32[16,2,2,24,384]{4,3,2,1,0:T(8,128)}), f32[16,2,2,24,384]{4,3,2,1,0:T(8,128)}, u32[]{:S(2)}, u32[]{:S(2)}) async-start(f32[16,2,2,24,384]{4,3,2,1,0:T(8,128)} %copy.54), calls=%async_computation | async-start | bytes 4718592 | tf_op jit(solution)/shard_map/all_to_all | solution.py:25
  1200.2 145.3 %all-reduce.2.cloned.1.call-start = ((), (), s32[]{:S(2)}) async-start(), calls=%async_computation.1 | async-start | bytes 1048576 | tf_op jit(solution)/shard_map/psum | solution.py:186
Sparse Core Ops, SparseCore 0:
  1203.5 141.9 all-reduce.1
where the time goes:
time: 1380 us
  waiting for transfers between devices  1020 us (74%)
  local copies, waits for them, and re-layouts  165 us (12%)
  starting transfers between devices  60.7 us (4%)
  other arithmetic  43.4 us (3%)
  loops' own time  30.4 us (2%)
  blocking collectives  28.6 us (2%)
  matrix products  23.4 us (2%)
  between operations  14.1 us (1%)
    ppermute x9, waiting for transfers between devices, passed_along(): return lax.ppermute(block, axis, route)  874 us
    psum x1, waiting for transfers between devices, shards(): total = lax.psum(probe_sum, 'probe')  145 us
    dynamic_update_slice x8, local copies, waits for them, and re-layouts, deposit(): lax.dynamic_update_slice(layer_grad, window + terms[position], corner)  59.3 us
    all_to_all x1, starting transfers between devices, sent_and_summed(): lax.all_to_all(split_up(array, dim, length), axis, 0, 0, tiled=True)  49.1 us
    another operation x4, loops' own time, work(): layer_grad = lax.fori_loop(0, group_size, deposit, grads[layer])  28.8 us
    all_gather x1, blocking collectives, picked(): lax.all_gather(array, axis)  28.6 us
    gather x24, local copies, waits for them, and re-layouts  27.7 us
  transfers between devices with their start and end apart: 11, of which 10 were waited for; matrix products, arithmetic and copies ran while one was open for 0% of the time, Pallas kernels for 0%

commit v1 on v0

v1 whole, which is shorter than its diff:
```python
import functools
import math

import jax
import jax.numpy as jnp
from jax import lax
from jax.experimental import pallas as pl
from jax.experimental.pallas import tpu as pltpu
from jax.sharding import PartitionSpec as P

BF = jnp.bfloat16
F32 = jnp.float32
RING = 4
N = 256
HALF = 128
PATCH = 384
ANY = pl.BlockSpec(memory_space=pl.ANY)
VM = pl.BlockSpec(memory_space=pltpu.VMEM)
SM = pl.BlockSpec(memory_space=pltpu.SMEM)
VMEM_LIMIT = 48 * 1024 * 1024


def half(index):
    return slice(index * HALF, (index + 1) * HALF)


def transform_tables(width):
    span = width // 2
    shape = (2, width, width)
    parity = lax.broadcasted_iota(jnp.int32, shape, 0)

    def build(spread_dim, sign):
        rows = lax.broadcasted_iota(jnp.int32, shape, 1)
        cols = lax.broadcasted_iota(jnp.int32, shape, 2)
        spread, other = (rows, cols) if spread_dim == 1 else (cols, rows)
        order = (2 * (spread % span) + parity) * (other % span) % width
        phase = 2.0 * math.pi / width * order.astype(F32)
        factor = 1.0 / math.sqrt(width)
        low = rows < span
        left = cols < span
        value = jnp.where(low == left, jnp.cos(phase), jnp.where(low, sign, -sign) * jnp.sin(phase))
        return (value * factor).astype(BF)

    return build(2, 1.0), build(1, 1.0), build(2, -1.0)


def split_order(array):
    span = array.shape[0] // 2
    return array.reshape(span, 2, span, 2).transpose(1, 0, 3, 2).reshape(array.shape)


def dot(a, b):
    return jnp.dot(a, b, preferred_element_type=F32)


def back_step(source, tables, mixed, filtered, second, finish):
    inward, table, flipped, kernel_cos, kernel_sin = tables
    for part in (0, 1):
        even = dot(inward[0, half(part), :], source[0])
        odd = dot(inward[1, half(part), :], source[1])
        for row, value in ((0, even + odd), (1, even - odd)):
            left, right = value[:, :HALF], value[:, HALF:]
            mixed[0, half(row), half(part)] = (left + right).astype(BF)
            mixed[1, half(row), half(part)] = (left - right).astype(BF)
    for col in (0, 1):
        upper = dot(mixed[col, half(0), :], flipped[col])
        lower = dot(mixed[col, half(1), :], flipped[col])
        for parity in (0, 1):
            real = upper[:, half(parity)]
            imag = lower[:, half(parity)]
            kc = kernel_cos[half(parity), half(col)]
            ks = kernel_sin[half(parity), half(col)]
            filtered[parity, half(0), half(col)] = (kc * real + ks * imag).astype(BF)
            filtered[parity, half(1), half(col)] = (kc * imag - ks * real).astype(BF)
    for part in (0, 1):
        even = dot(flipped[0, half(part), :], filtered[0])
        odd = dot(flipped[1, half(part), :], filtered[1])
        total = (even + odd).astype(BF)
        diff = (even - odd).astype(BF)
        for col in (0, 1):
            second[col, half(0), half(part)] = total[:, half(col)]
            second[col, half(1), half(part)] = diff[:, half(col)]
    totals, diffs = [], []
    for row in (0, 1):
        even = dot(second[0, half(row), :], table[0])
        odd = dot(second[1, half(row), :], table[1])
        totals.append(even + odd)
        diffs.append(even - odd)
    for parity in (0, 1):
        finish(
            parity,
            (totals[0][:, half(parity)], diffs[0][:, half(parity)]),
            (totals[1][:, half(parity)], diffs[1][:, half(parity)]),
        )


def step_scratch():
    return [pltpu.VMEM((2, N, N), BF), pltpu.VMEM((2, N, N), BF), pltpu.VMEM((2, N, N), BF)]


def sine_and_cosine(angle):
    half_angle = 0.5 * angle
    square = half_angle * half_angle

    def series(first):
        value = jnp.full_like(square, (-1.0) ** 6 / math.factorial(12 + first))
        for term in range(5, -1, -1):
            value = value * square + (-1.0) ** term / math.factorial(2 * term + first)
        return value

    low_sine = half_angle * series(1)
    low_cosine = series(0)
    return 2.0 * low_sine * low_cosine, 1.0 - 2.0 * low_sine * low_sine


def window_kernel(where, offsets, phase, amp, *rest):
    outs, field = rest[:RING], rest[RING]
    rank = where[0]
    for layer in (0, 1):
        for col in range(3):
            for block in range(3):
                sine, cosine = sine_and_cosine(phase[layer, half(block), half(col)])
                size = amp[layer, half(block), half(col)]
                field[layer, 0, col, half(block), :] = size * cosine
                field[layer, 1, col, half(block), :] = size * sine
    lane = lax.broadcasted_iota(jnp.int32, (HALF, HALF), 1)
    for distance in range(RING):
        position = (rank + distance) % RING
        col_at = offsets[position, 1]
        turn = (HALF - col_at) % HALF
        inside = lane < HALF - col_at
        for parity in (0, 1):
            rows = pl.ds(offsets[position, 0] + parity, HALF, stride=2)
            for layer in (0, 1):
                for part in (0, 1):
                    turned = [
                        pltpu.roll(field[layer, part, col, rows, :], turn, 1) for col in range(3)
                    ]
                    for col in (0, 1):
                        outs[distance][layer, parity, half(part), half(col)] = jnp.where(
                            inside, turned[col], turned[col + 1]
                        ).astype(BF)


def transmission_windows(where, offsets, phase, amp):
    shape = jax.ShapeDtypeStruct((2, 2, N, N), BF)
    return pl.pallas_call(
        window_kernel,
        name="windows",
        out_shape=[shape] * RING,
        in_specs=[SM, SM, VM, VM],
        out_specs=[VM] * RING,
        scratch_shapes=[pltpu.VMEM((2, 2, 3, PATCH, HALF), F32)],
        compiler_params=pltpu.CompilerParams(vmem_limit_bytes=VMEM_LIMIT),
    )(where, offsets, phase, amp)


def chain_kernel(first, where, start, *rest):
    windows = rest[:RING]
    earlier = () if first else rest[RING : 2 * RING]
    rest = rest[RING + len(earlier) :]
    tables = rest[:5]
    count = RING + 1 if first else RING
    outs = rest[5 : 5 + count]
    trans, waves, middle, mixed, filtered, second, in_sems, out_sems = rest[5 + count :]
    rank = where[0]
    active = where[1] == 1 if first else where[1] == 0

    def loads():
        copies = []
        for distance in range(RING):
            slot = (rank + RING - distance) % RING
            copies.append(
                pltpu.make_async_copy(windows[distance], trans.at[slot], in_sems.at[distance])
            )
        copies.append(
            pltpu.make_async_copy(start, waves.at[(2 * RING - 1 - rank) % RING], in_sems.at[RING])
        )
        return copies

    def stores():
        return [
            pltpu.make_async_copy(waves.at[k], outs[k], out_sems.at[k]) for k in range(count)
        ]

    @pl.when(active)
    def _():
        for copy in loads():
            copy.start()
        for copy in loads():
            copy.wait()

        def pair(step, carry):
            pair_at = RING - 1 - step
            source = waves.at[(pair_at + RING - rank) % RING]
            target = waves.at[
                jnp.where(pair_at == 0, RING, (pair_at + 2 * RING - 1 - rank) % RING)
            ]
            for layer, begin, end in ((1, source, middle), (0, middle, target)):

                def finish(parity, reals, imags, layer=layer, end=end):
                    for col in (0, 1):
                        tr = trans[pair_at, layer, parity, half(0), half(col)].astype(F32)
                        ti = trans[pair_at, layer, parity, half(1), half(col)].astype(F32)
                        qr, qi = reals[col], imags[col]
                        end[parity, half(0), half(col)] = (tr * qr + ti * qi).astype(BF)
                        end[parity, half(1), half(col)] = (tr * qi - ti * qr).astype(BF)

                back_step(begin, tables, mixed, filtered, second, finish)
            return carry

        lax.fori_loop(0, RING, pair, 0)
        for copy in stores():
            copy.start()
        for copy in stores():
            copy.wait()

    if not first:

        @pl.when(jnp.logical_not(active))
        def _():
            copies = [
                pltpu.make_async_copy(earlier[k], outs[k], out_sems.at[k]) for k in range(RING)
            ]
            for copy in copies:
                copy.start()
            for copy in copies:
                copy.wait()


def run_chain(first, where, start, windows, earlier, tables):
    count = RING + 1 if first else RING
    wave = jax.ShapeDtypeStruct((2, N, N), BF)
    return pl.pallas_call(
        functools.partial(chain_kernel, first),
        name="chain_deep" if first else "chain_top",
        out_shape=[wave] * count,
        in_specs=[SM, ANY] + [ANY] * RING + [ANY] * len(earlier) + [VM] * 5,
        out_specs=[ANY] * count,
        scratch_shapes=[
            pltpu.VMEM((RING, 2, 2, N, N), BF),
            pltpu.VMEM((RING + 1, 2, N, N), BF),
            pltpu.VMEM((2, N, N), BF),
            *step_scratch(),
            pltpu.SemaphoreType.DMA((RING + 1,)),
            pltpu.SemaphoreType.DMA((RING + 1,)),
        ],
        compiler_params=pltpu.CompilerParams(vmem_limit_bytes=VMEM_LIMIT),
    )(where, start, *windows, *earlier, *tables)


def terms_kernel(where, offsets, saved, *rest):
    windows = rest[:RING]
    entries = rest[RING : 2 * RING]
    tables = rest[2 * RING : 2 * RING + 5]
    payload = rest[2 * RING + 5]
    trans, waves, psi, grads, ending, final, middle, mixed, filtered, second, sems = rest[
        2 * RING + 6 :
    ]
    rank = where[0]

    def loads(index):
        position = (rank + RING - index) % RING
        return [
            pltpu.make_async_copy(entries[index], waves.at[index], sems.at[0, index]),
            pltpu.make_async_copy(
                windows[(RING - index) % RING], trans.at[index], sems.at[1, index]
            ),
            pltpu.make_async_copy(saved.at[position], psi.at[index], sems.at[2, index]),
        ]

    for index in range(RING):
        for copy in loads(index):
            copy.start()
    grads[...] = jnp.zeros_like(grads)
    ending[...] = jnp.zeros_like(ending)
    for index in range(RING):
        for copy in loads(index):
            copy.wait()
    lane = lax.broadcasted_iota(jnp.int32, (HALF, HALF), 1)

    def visit(index, carry):
        position = (rank + RING - index) % RING
        col_at = offsets[position, 1]
        turn = col_at % HALF
        inside = lane >= col_at

        for layer in (1, 0):

            def finish(parity, reals, imags, layer=layer):
                terms = ([], [])
                for col in (0, 1):
                    wr = psi[index, layer, parity, half(0), half(col)].astype(F32)
                    wi = psi[index, layer, parity, half(1), half(col)].astype(F32)
                    tr = trans[index, layer, parity, half(0), half(col)].astype(F32)
                    ti = trans[index, layer, parity, half(1), half(col)].astype(F32)
                    qr, qi = reals[col], imags[col]
                    terms[0].append(pltpu.roll(wr * qr + wi * qi, turn, 1))
                    terms[1].append(pltpu.roll(wr * qi - wi * qr, turn, 1))
                    next_real = (tr * qr + ti * qi).astype(BF)
                    next_imag = (tr * qi - ti * qr).astype(BF)
                    if layer == 1:
                        middle[parity, half(0), half(col)] = next_real
                        middle[parity, half(1), half(col)] = next_imag
                    else:
                        ending[parity, half(0), half(col)] += next_real.astype(F32)
                        ending[parity, half(1), half(col)] += next_imag.astype(F32)
                rows = pl.ds(offsets[position, 0] + parity, HALF, stride=2)
                zero = jnp.zeros((HALF, HALF), F32)
                for part in (0, 1):
                    left, right = terms[part]
                    placed = (
                        jnp.where(inside, left, zero),
                        jnp.where(inside, right, left),
                        jnp.where(inside, zero, right),
                    )
                    for col in range(3):
                        grads[layer, part, col, rows, :] += placed[col]

            begin = waves.at[index] if layer == 1 else middle
            back_step(begin, tables, mixed, filtered, second, finish)
        return carry

    lax.fori_loop(0, RING, visit, 0)
    chunks = payload.shape[0]
    rows_each = PATCH // chunks
    probe_each = N // chunks

    for parity in (0, 1):
        for part in (0, 1):
            for col in (0, 1):
                final[part, col, pl.ds(parity, HALF, stride=2), :] = ending[
                    parity, half(part), half(col)
                ]

    def pack(chunk, carry):
        rows = pl.ds(pl.multiple_of(chunk * rows_each, 8), rows_each)
        probe_rows = pl.ds(pl.multiple_of(chunk * probe_each, 8), probe_each)
        for col in range(3):
            pieces = [grads[layer, part, col, rows, :] for layer in (0, 1) for part in (0, 1)]
            if col < 2:
                pieces += [final[part, col, probe_rows, :] for part in (0, 1)]
            else:
                pieces += [jnp.zeros((2 * probe_each, HALF), F32)]
            payload[chunk, :, half(col)] = jnp.concatenate(pieces, 0).astype(BF)
        return carry

    lax.fori_loop(0, chunks, pack, 0)


def slice_terms(chunks, where, offsets, saved, windows, entries, tables):
    rows = 4 * (PATCH // chunks) + 2 * (N // chunks)
    return pl.pallas_call(
        terms_kernel,
        name="terms",
        out_shape=jax.ShapeDtypeStruct((chunks, rows, PATCH), BF),
        in_specs=[SM, SM, ANY] + [ANY] * (2 * RING) + [VM] * 5,
        out_specs=VM,
        scratch_shapes=[
            pltpu.VMEM((RING, 2, 2, N, N), BF),
            pltpu.VMEM((RING, 2, N, N), BF),
            pltpu.VMEM((RING, 2, 2, N, N), BF),
            pltpu.VMEM((2, 2, 3, PATCH, HALF), F32),
            pltpu.VMEM((2, N, N), F32),
            pltpu.VMEM((2, 2, N, HALF), F32),
            pltpu.VMEM((2, N, N), BF),
            *step_scratch(),
            pltpu.SemaphoreType.DMA((3, RING)),
        ],
        compiler_params=pltpu.CompilerParams(vmem_limit_bytes=VMEM_LIMIT),
    )(where, offsets, saved, *windows, *entries, *tables)


def order_kernel(where, residual, saved, start, waves):
    rows = lax.broadcasted_iota(jnp.int32, (N, N), 0)
    cols = lax.broadcasted_iota(jnp.int32, (N, N), 1)
    take = (cols == 2 * (rows % HALF) + rows // HALF).astype(F32).astype(BF)

    def reorder(source, target):
        for part in (0, 1):
            ordered = dot(take, source[part]).astype(BF)
            for parity in (0, 1):
                target[parity, half(part), :] = ordered[half(parity), :]

    for layer in (0, 1):
        reorder(saved.at[layer, 0], waves.at[0, layer])

    @pl.when(pl.program_id(0) == where[0])
    def _():
        reorder(residual.at[0], start)


def row_parity_first(where, residual, saved):
    wave = (2, N, N)
    return pl.pallas_call(
        order_kernel,
        name="reorder",
        out_shape=[
            jax.ShapeDtypeStruct(wave, BF),
            jax.ShapeDtypeStruct((RING, 2, *wave), BF),
        ],
        grid=(RING,),
        in_specs=[
            SM,
            pl.BlockSpec((1, *wave), lambda i: (i, 0, 0, 0)),
            pl.BlockSpec((2, 1, *wave), lambda i: (0, i, 0, 0, 0)),
        ],
        out_specs=[
            pl.BlockSpec(wave, lambda i: (0, 0, 0)),
            pl.BlockSpec((1, 2, *wave), lambda i: (i, 0, 0, 0, 0)),
        ],
        compiler_params=pltpu.CompilerParams(vmem_limit_bytes=VMEM_LIMIT),
    )(where, residual, saved)


def turned(array, distance):
    route = [
        (RING * ring + i, RING * ring + (i + distance) % RING)
        for ring in range(2)
        for i in range(RING)
    ]
    return lax.ppermute(array, "depth", route)


def exchanged(arrays):
    return [arrays[0]] + [turned(arrays[k], k) for k in range(1, RING)]


def shards(residual, saved_waves, object_phase, object_amp, prop_phase, offsets):
    depth_at = lax.axis_index("depth")
    chunks = lax.axis_size("probe")
    where = jnp.stack([depth_at % RING, depth_at // RING]).astype(jnp.int32)
    own = transmission_windows(where, offsets, object_phase, object_amp)
    ordered = split_order(prop_phase)
    tables = (*transform_tables(N), jnp.cos(ordered), jnp.sin(ordered))
    start, waves = row_parity_first(where, residual, saved_waves)
    foreign = exchanged(own)
    *deep, leaving = run_chain(True, where, start, foreign, (), tables)
    arrived = lax.ppermute(leaving, "depth", [(RING + i, i) for i in range(RING)])
    entries = run_chain(False, where, arrived, foreign, deep, tables)
    payload = slice_terms(chunks, where, offsets, waves, own, exchanged(entries), tables)
    received = lax.all_to_all(payload, "probe", 0, 0, tiled=True)
    total = jnp.sum(received.astype(F32), axis=0)
    rows_each = PATCH // chunks
    object_grad = total[: 4 * rows_each].reshape(2, 2, rows_each, PATCH)
    probe_rows = total[4 * rows_each :, :N].reshape(2, N // chunks, 8, N // 8)
    spread = lax.all_to_all(jnp.moveaxis(probe_rows, 2, 0), "depth", 0, 0, tiled=True)
    return (object_grad, spread[0])


def solution(mesh):
    return jax.shard_map(
        shards,
        mesh=mesh,
        in_specs=(
            P("probe", None, None, None),
            P("depth", "probe", None, None, None),
            P("depth", None, None),
            P("depth", None, None),
            P(),
            P("probe", None),
        ),
        out_specs=(P("depth", None, "probe", None), P(None, "probe", "depth")),
        check_vma=False,
    )
```

time: 1380 us -> 177 us (0.13)
  waiting for transfers between devices: 1020 us -> 31.4 us
  local copies, waits for them, and re-layouts: 165 us -> 65.2 us
  starting transfers between devices: 60.7 us -> 15.7 us
  other arithmetic: 43.4 us -> 5.94 us
  loops' own time: 30.4 us -> 0 us
  Pallas kernels: 0 us -> 27.5 us
  matrix products: 23.4 us -> 0 us
    ppermute x9 -> x7, waiting for transfers between devices: 874 us -> 25.8 us  [the longest x1 15.5 us: shards(): lax.ppermute(leaving, 'depth', [(RING + i, i) for i in range(RING)])]
    psum x1 -> x0, waiting for transfers between devices: 145 us -> none  [shards(): total = lax.psum(probe_sum, 'probe')]
    dynamic_update_slice x8 -> x0, local copies, waits for them, and re-layouts: 59.3 us -> none  [deposit(): lax.dynamic_update_slice(layer_grad, window + terms[position], corner)]
    all_to_all x1, starting transfers between devices: 49.1 us -> 3.91 us  [shards(): lax.all_to_all(jnp.moveaxis(probe_rows, 2, 0), 'depth', 0, 0, tiled=True)]
    another operation x18 -> x0, loops' own time: 30.4 us -> none  [the longest x4 28.8 us: work(): layer_grad = lax.fori_loop(0, group_size, deposit, grads[layer])]
    all_to_all x0 -> x1, blocking collectives: none -> 30.1 us  [shards(): received = lax.all_to_all(payload, 'probe', 0, 0, tiled=True)]
    all_gather x1 -> x0, blocking collectives: 28.6 us -> none  [picked(): lax.all_gather(array, axis)]
    cos x0 -> x2, local copies, waits for them, and re-layouts: none -> 28 us  [shards(): tables = (*transform_tables(N), jnp.cos(ordered), jnp.sin(ordered))]
  transfers between devices with their start and end apart: 11 -> 8, of which waited for: 10 -> 4; matrix products, arithmetic and copies ran while one was open for 0% -> 35% of each run, Pallas kernels for 0% -> 1%
where the time goes in v1:
time: 177 us
  local copies, waits for them, and re-layouts  65.2 us (37%)
  waiting for transfers between devices  31.4 us (18%)
  blocking collectives  30.1 us (17%)
  Pallas kernels  27.5 us (16%)
  starting transfers between devices  15.7 us (9%)
  other arithmetic  5.94 us (3%)
    all_to_all x1, blocking collectives, shards(): received = lax.all_to_all(payload, 'probe', 0, 0, tiled=True)  30.1 us
    sin x4, local copies, waits for them, and re-layouts, shards(): tables = (*transform_tables(N), jnp.cos(ordered), jnp.sin(ordered))  28.6 us
    cos x2, local copies, waits for them, and re-layouts, shards(): tables = (*transform_tables(N), jnp.cos(ordered), jnp.sin(ordered))  28 us
    ppermute x1, waiting for transfers between devices, shards(): lax.ppermute(leaving, 'depth', [(RING + i, i) for i in range(RING)])  15.5 us
    pallas_call x1, Pallas kernels, slice_terms(): pl.pallas_call(terms_kernel, name='terms', out_shape=jax.ShapeDtypeStruct...  11.6 us
    ppermute x6, starting transfers between devices, turned(): return lax.ppermute(array, 'depth', route)  10.5 us
    ppermute x6, waiting for transfers between devices, turned(): return lax.ppermute(array, 'depth', route)  10.3 us
    pallas_call x2, Pallas kernels, run_chain(): pl.pallas_call(functools.partial(chain_kernel, first), name='chain_deep'...  10 us
  transfers between devices with their start and end apart: 8, of which 4 were waited for; matrix products, arithmetic and copies ran while one was open for 35% of the time, Pallas kernels for 1%

profile of v1, /device:TPU:0, one launch (start us, length us, event | category | flops | bytes accessed | tf_op | source)
XLA Modules:
  0.0 176.6 jit_solution(8248199852886123908)
XLA Ops:
  0.6 0.8 copy.19.offsets
  1.4 0.1 pad_add_fusion.where
  1.5 0.0 copy-start.2
  1.5 1.3 copy-done.2
  2.8 1.3 copy-done.3
  4.0 0.0 copy-start.6
  4.0 3.7 %windows.1 = (bf16[2,2,256,256]{3,2,1,0:T(8,128)(2,1)S(1)}, bf16[2,2,256,256]{3,2,1,0:T(8,128)(2,1)}, bf16[2,2,256,256]{3,2,1,0:T(8,128)(2,1)}, bf16[2,2,256,256]{3,2,1,0:T(8,128)(2,1)}) custom-call(s32[2]{0:T(128)S(1)} %pad_add_fusion.where, s32[4,2]{1,0:T(4,128)S(1)} %copy.19.offsets, f32[2,384,384]{2,1,0:T(8,128)S(1)} %copy-done.2, ...), custom_call_target="tpu_custom_call" | custom-call | tf_op jit(solution)/shard_map/windows/pallas_call | solution.py:147
  7.7 2.0 %collective-permute-start = (bf16[2,2,256,256]{3,2,1,0:T(8,128)(2,1)}, bf16[2,2,256,256]{3,2,1,0:T(8,128)(2,1)S(1)}, u32[]{:S(2)}, u32[]{:S(2)}) collective-permute-start(bf16[2,2,256,256]{3,2,1,0:T(8,128)(2,1)} %get-tuple-element.19.rest_1_), channel_id=1, source_target_pairs={{0,16},{16,32},{32,48},{48,0},{64,80},{80,96},{96,112},{112,64},{1... | collective-permute-start | bytes 1572872 | tf_op jit(solution)/shard_map/ppermute | solution.py:422
  9.7 3.6 %collective-permute-start.1 = (bf16[2,2,256,256]{3,2,1,0:T(8,128)(2,1)}, bf16[2,2,256,256]{3,2,1,0:T(8,128)(2,1)}, u32[]{:S(2)}, u32[]{:S(2)}) collective-permute-start(bf16[2,2,256,256]{3,2,1,0:T(8,128)(2,1)} %get-tuple-element.20.rest_2_), channel_id=1, source_target_pairs={{0,32},{16,48},{32,0},{48,16},{64,96},{80,112},{96,64},{112,80},{1... | collective-permute-start | bytes 1572872 | tf_op jit(solution)/shard_map/ppermute | solution.py:422
  13.3 1.0 collective-permute-start.2
  14.3 0.0 copy-done.6
  14.4 1.0 fusion.17
  15.3 18.1 %sin.33 = f32[128,2,128,2]{3,2,1,0:T(8,128)} reshape(f32[256,256]{1,0:T(8,128)S(1)} %get-tuple-element.32) | data formatting | bytes 524288 | tf_op jit(solution)/shard_map/sin | solution.py:435
  33.4 9.5 %copy.18 = f32[2,128,2,128]{3,2,1,0:T(2,128)S(1)} copy(f32[2,128,2,128]{2,3,0,1:T(8,128)} %bitcast.16) | data formatting | bytes 524288 | tf_op jit(solution)/shard_map/sin | solution.py:435
  42.9 18.1 %cos.33 = f32[128,2,128,2]{3,2,1,0:T(8,128)} reshape(f32[256,256]{1,0:T(8,128)S(1)} %get-tuple-element.33) | data formatting | bytes 524288 | tf_op jit(solution)/shard_map/cos | solution.py:435
  61.0 9.9 %copy.17 = f32[2,128,2,128]{3,2,1,0:T(2,128)} copy(f32[2,128,2,128]{2,3,0,1:T(8,128)} %bitcast.17) | data formatting | bytes 524288 | tf_op jit(solution)/shard_map/cos | solution.py:435
  70.9 0.0 copy-done.1
  70.9 1.2 copy-done.4
  72.2 2.2 %reorder.1 = (bf16[2,256,256]{2,1,0:T(8,128)(2,1)S(1)}, bf16[4,2,2,256,256]{4,3,2,1,0:T(8,128)(2,1)S(1)}) custom-call(s32[2]{0:T(128)S(1)} %pad_add_fusion.where, bf16[4,2,256,256]{3,2,1,0:T(8,128)(2,1)S(1)} %copy-done.4, bf16[2,4,2,256,256]{4,3,2,1,0:T(8,128)(2,1)S(1)} %copy-done.1), custom_call_target="tpu_custom_call" | custom-call | tf_op jit(solution)/shard_map/reorder/pallas_call | solution.py:395
  74.3 0.0 copy-start
  74.3 1.3 copy-done
  75.7 0.0 copy-done.5
  75.7 4.9 %fusion.11 = (bf16[2,256,256]{2,1,0:T(8,128)(2,1)S(1)}, bf16[2,256,256]{2,1,0:T(8,128)(2,1)S(1)}, bf16[2,256,256]{2,1,0:T(8,128)(2,1)S(1)}) fusion(f32[256]{0:T(256)S(1)} %get-tuple-element.42, s32[256]{0:T(256)S(1)} %get-tuple-element.39, s32[256]{0:T(256)S(1)} %get-tuple-element.40, pred[256]{0:T(512)(128)(4,1)S(1)} %get-tuple-element.37, ...), kind=kLoop, calls=%fused_computation.25 | loop fusion | flops 6160384 | bytes 791040 | tf_op jit(solution)/shard_map/convert_element_type | solution.py:42
  80.6 0.0 collective-permute-done.rest_1_
  80.6 0.0 collective-permute-done.1.rest_2_
  80.7 0.0 collective-permute-done.2.rest_3_
  80.7 0.6 chain_deep.1
  81.3 1.3 collective-permute-start.3
  82.6 15.5 %collective-permute-done.3.start = bf16[2,256,256]{2,1,0:T(8,128)(2,1)S(1)} collective-permute-done((bf16[2,256,256]{2,1,0:T(8,128)(2,1)S(1)}, bf16[2,256,256]{2,1,0:T(8,128)(2,1)S(1)}, u32[]{:S(2)}, u32[]{:S(2)}) %collective-permute-start.3) | collective-permute-done | bytes 262176 | tf_op jit(solution)/shard_map/ppermute | solution.py:439
  98.1 9.4 %chain_top.1 = (bf16[2,256,256]{2,1,0:T(8,128)(2,1)S(1)}, bf16[2,256,256]{2,1,0:T(8,128)(2,1)S(1)}, bf16[2,256,256]{2,1,0:T(8,128)(2,1)S(1)}, bf16[2,256,256]{2,1,0:T(8,128)(2,1)S(1)}) custom-call(s32[2]{0:T(128)S(1)} %pad_add_fusion.where, bf16[2,256,256]{2,1,0:T(8,128)(2,1)S(1)} %collective-permute-done.3.start, ...), custom_call_target="tpu_custom_call" | custom-call | tf_op jit(solution)/shard_map/chain_top/pallas_call | solution.py:234
  107.5 1.1 collective-permute-start.4
  108.5 0.7 collective-permute-start.5
  109.3 2.0 %collective-permute-start.6 = (bf16[2,256,256]{2,1,0:T(8,128)(2,1)S(1)}, bf16[2,256,256]{2,1,0:T(8,128)(2,1)S(1)}, u32[]{:S(2)}, u32[]{:S(2)}) collective-permute-start(bf16[2,256,256]{2,1,0:T(8,128)(2,1)S(1)} %get-tuple-element.31), channel_id=1, source_target_pairs={{0,48},{16,0},{32,16},{48,32},{64,112},{80,64},{96,80},{112,96},{1... | collective-permute-start | bytes 786440 | tf_op jit(solution)/shard_map/ppermute | solution.py:422
  111.3 9.7 %collective-permute-done.4.rest_5_ = bf16[2,256,256]{2,1,0:T(8,128)(2,1)S(1)} collective-permute-done((bf16[2,256,256]{2,1,0:T(8,128)(2,1)S(1)}, bf16[2,256,256]{2,1,0:T(8,128)(2,1)S(1)}, u32[]{:S(2)}, u32[]{:S(2)}) %collective-permute-start.4) | collective-permute-done | bytes 262176 | tf_op jit(solution)/shard_map/ppermute | solution.py:422
  121.0 0.0 collective-permute-done.5.rest_6_
  121.0 0.6 collective-permute-done.6.rest_7_
  121.6 11.6 %terms.1 = bf16[16,128,384]{2,1,0:T(8,128)(2,1)S(1)} custom-call(s32[2]{0:T(128)S(1)} %pad_add_fusion.where, s32[4,2]{1,0:T(4,128)S(1)} %copy.19.offsets, bf16[4,2,2,256,256]{4,3,2,1,0:T(8,128)(2,1)} %copy-done, bf16[2,2,256,256]{3,2,1,0:T(8,128)(2,1)S(1)} %get-tuple-element.18.rest_0_, bf16[2,2,256,256]{3,2,1,0:T(8,128)(2,1)} %get-tuple-element.19.rest_1_, ...), custom_call_target="tpu_custom_call" | custom-call | tf_op jit(solution)/shard_map/terms/pallas_call | solution.py:353
  133.3 30.1 %all_to_all.10 = bf16[16,128,384]{2,1,0:T(8,128)(2,1)S(1)} all-to-all(bf16[16,128,384]{2,1,0:T(8,128)(2,1)S(1)} %terms.1), channel_id=1, replica_groups=mesh['depth'=8,'probe'=16] {'probe'}, dimensions={0} | all-to-all | bytes 3145728 | tf_op jit(solution)/shard_map/all_to_all | solution.py:442
  163.4 0.2 convert_reduce_fusion
  163.6 0.1 reshape.17
  163.7 0.7 reshape.18
  164.5 3.9 %all-to-all-start.1 = ((f32[8,1,1024]{2,1,0:T(1,128)}), f32[8,1,1024]{2,1,0:T(1,128)S(1)}, u32[]{:S(2)}, u32[]{:S(2)}) async-start(f32[8,1,1024]{2,1,0:T(1,128)} %reshape.18), calls=%async_computation.1 | async-start | bytes 65536 | tf_op jit(solution)/shard_map/all_to_all | solution.py:447
  168.4 0.7 slice.12
  169.0 5.6 %all-to-all-done.1 = f32[8,1,1024]{2,1,0:T(1,128)S(1)} async-done(((f32[8,1,1024]{2,1,0:T(1,128)}), f32[8,1,1024]{2,1,0:T(1,128)S(1)}, u32[]{:S(2)}, u32[]{:S(2)}) %all-to-all-start.1) | async-done | bytes 32800 | tf_op jit(solution)/shard_map/all_to_all | solution.py:447
  174.6 0.5 broadcast.117
  175.1 0.7 reduce
  175.9 0.1 reshape.19
  176.0 0.6 slice_bitcast_fusion
  (10 shorter events, 0.1 us)
Async XLA Ops:
  1.5 1.3 copy-start.2
  2.8 1.3 copy-start.3
  4.0 10.3 %copy-start.6 = (f32[256,256]{1,0:T(8,128)S(1)}, f32[256,256]{1,0:T(8,128)}, u32[]{:S(2)}) copy-start(f32[256,256]{1,0:T(8,128)} %param.10) | copy-start | bytes 786436
  7.7 72.9 %collective-permute-start = (bf16[2,2,256,256]{3,2,1,0:T(8,128)(2,1)}, bf16[2,2,256,256]{3,2,1,0:T(8,128)(2,1)S(1)}, u32[]{:S(2)}, u32[]{:S(2)}) collective-permute-start(bf16[2,2,256,256]{3,2,1,0:T(8,128)(2,1)} %get-tuple-element.19.rest_1_), channel_id=1, source_target_pairs={{0,16},{16,32},{32,48},{48,0},{64,80},{80,96},{96,112},{112,64},{1... | collective-permute-start | bytes 1572872 | tf_op jit(solution)/shard_map/ppermute | solution.py:422
  9.7 70.9 %collective-permute-start.1 = (bf16[2,2,256,256]{3,2,1,0:T(8,128)(2,1)}, bf16[2,2,256,256]{3,2,1,0:T(8,128)(2,1)}, u32[]{:S(2)}, u32[]{:S(2)}) collective-permute-start(bf16[2,2,256,256]{3,2,1,0:T(8,128)(2,1)} %get-tuple-element.20.rest_2_), channel_id=1, source_target_pairs={{0,32},{16,48},{32,0},{48,16},{64,96},{80,112},{96,64},{112,80},{1... | collective-permute-start | bytes 1572872 | tf_op jit(solution)/shard_map/ppermute | solution.py:422
  13.3 67.3 %collective-permute-start.2 = (bf16[2,2,256,256]{3,2,1,0:T(8,128)(2,1)}, bf16[2,2,256,256]{3,2,1,0:T(8,128)(2,1)}, u32[]{:S(2)}, u32[]{:S(2)}) collective-permute-start(bf16[2,2,256,256]{3,2,1,0:T(8,128)(2,1)} %get-tuple-element.21.rest_3_), channel_id=1, source_target_pairs={{0,48},{16,0},{32,16},{48,32},{64,112},{80,64},{96,80},{112,96},{1... | collective-permute-start | bytes 1572872 | tf_op jit(solution)/shard_map/ppermute | solution.py:422
  61.0 9.9 %copy-start.1 = (bf16[2,4,2,256,256]{4,3,2,1,0:T(8,128)(2,1)S(1)}, bf16[2,4,2,256,256]{4,3,2,1,0:T(8,128)(2,1)}, u32[]{:S(2)}) copy-start(bf16[2,4,2,256,256]{4,3,2,1,0:T(8,128)(2,1)} %saved.1) | copy-start | bytes 6291460
  70.9 1.2 copy-start.4
  72.2 3.5 %copy-start.5 = (f32[2,128,2,128]{3,2,1,0:T(2,128)S(1)}, f32[2,128,2,128]{3,2,1,0:T(2,128)}, u32[]{:S(2)}) copy-start(f32[2,128,2,128]{3,2,1,0:T(2,128)} %copy.17) | copy-start | bytes 786436
  74.3 1.3 copy-start
  81.3 16.8 %collective-permute-start.3 = (bf16[2,256,256]{2,1,0:T(8,128)(2,1)S(1)}, bf16[2,256,256]{2,1,0:T(8,128)(2,1)S(1)}, u32[]{:S(2)}, u32[]{:S(2)}) collective-permute-start(bf16[2,256,256]{2,1,0:T(8,128)(2,1)S(1)} %get-tuple-element.23), channel_id=1, source_target_pairs={{64,0},{80,16},{96,32},{112,48},{65,1},{81,17},{97,33},{113,49},{6... | collective-permute-start | bytes 786440 | tf_op jit(solution)/shard_map/ppermute | solution.py:439
  107.5 13.5 %collective-permute-start.4 = (bf16[2,256,256]{2,1,0:T(8,128)(2,1)S(1)}, bf16[2,256,256]{2,1,0:T(8,128)(2,1)S(1)}, u32[]{:S(2)}, u32[]{:S(2)}) collective-permute-start(bf16[2,256,256]{2,1,0:T(8,128)(2,1)S(1)} %get-tuple-element.29), channel_id=1, source_target_pairs={{0,16},{16,32},{32,48},{48,0},{64,80},{80,96},{96,112},{112,64},{1... | collective-permute-start | bytes 786440 | tf_op jit(solution)/shard_map/ppermute | solution.py:422
  108.5 12.5 %collective-permute-start.5 = (bf16[2,256,256]{2,1,0:T(8,128)(2,1)S(1)}, bf16[2,256,256]{2,1,0:T(8,128)(2,1)S(1)}, u32[]{:S(2)}, u32[]{:S(2)}) collective-permute-start(bf16[2,256,256]{2,1,0:T(8,128)(2,1)S(1)} %get-tuple-element.30), channel_id=1, source_target_pairs={{0,32},{16,48},{32,0},{48,16},{64,96},{80,112},{96,64},{112,80},{1... | collective-permute-start | bytes 786440 | tf_op jit(solution)/shard_map/ppermute | solution.py:422
  109.3 12.3 %collective-permute-start.6 = (bf16[2,256,256]{2,1,0:T(8,128)(2,1)S(1)}, bf16[2,256,256]{2,1,0:T(8,128)(2,1)S(1)}, u32[]{:S(2)}, u32[]{:S(2)}) collective-permute-start(bf16[2,256,256]{2,1,0:T(8,128)(2,1)S(1)} %get-tuple-element.31), channel_id=1, source_target_pairs={{0,48},{16,0},{32,16},{48,32},{64,112},{80,64},{96,80},{112,96},{1... | collective-permute-start | bytes 786440 | tf_op jit(solution)/shard_map/ppermute | solution.py:422
  164.5 10.2 %all-to-all-start.1 = ((f32[8,1,1024]{2,1,0:T(1,128)}), f32[8,1,1024]{2,1,0:T(1,128)S(1)}, u32[]{:S(2)}, u32[]{:S(2)}) async-start(f32[8,1,1024]{2,1,0:T(1,128)} %reshape.18), calls=%async_computation.1 | async-start | bytes 65536 | tf_op jit(solution)/shard_map/all_to_all | solution.py:447

commit v2 on v1

--- a/solution.py
+++ b/solution.py
@@ -11,12 +11,16 @@
 BF = jnp.bfloat16
 F32 = jnp.float32
 RING = 4
+DEPTH = 8
 N = 256
 HALF = 128
 PATCH = 384
 ANY = pl.BlockSpec(memory_space=pl.ANY)
 VM = pl.BlockSpec(memory_space=pltpu.VMEM)
 SM = pl.BlockSpec(memory_space=pltpu.SMEM)
+HB = pl.BlockSpec(memory_space=pltpu.HBM)
+SINE = (0.999999995716, -0.166666579699, 0.00833305061733, -0.000198090463574, 2.60516627618e-06)
+COSINE = (0.99999999978, -0.49999999357, 0.0416666362089, -0.00138883608423, 2.47601355058e-05, -2.60510761786e-07)
 VMEM_LIMIT = 48 * 1024 * 1024
 
 
@@ -42,11 +46,6 @@
         return (value * factor).astype(BF)
 
     return build(2, 1.0), build(1, 1.0), build(2, -1.0)
-
-
-def split_order(array):
-    span = array.shape[0] // 2
-    return array.reshape(span, 2, span, 2).transpose(1, 0, 3, 2).reshape(array.shape)
 
 
 def dot(a, b):
@@ -102,23 +101,70 @@
     half_angle = 0.5 * angle
     square = half_angle * half_angle
 
-    def series(first):
-        value = jnp.full_like(square, (-1.0) ** 6 / math.factorial(12 + first))
-        for term in range(5, -1, -1):
-            value = value * square + (-1.0) ** term / math.factorial(2 * term + first)
+    def series(factors):
+        value = jnp.full_like(square, factors[-1])
+        for factor in factors[-2::-1]:
+            value = value * square + factor
         return value
 
-    low_sine = half_angle * series(1)
-    low_cosine = series(0)
+    low_sine = half_angle * series(SINE)
+    low_cosine = series(COSINE)
     return 2.0 * low_sine * low_cosine, 1.0 - 2.0 * low_sine * low_sine
 
 
-def window_kernel(where, offsets, phase, amp, *rest):
-    outs, field = rest[:RING], rest[RING]
+def filter_kernel(phase, kernel_cos, kernel_sin, plain):
+    rows = lax.broadcasted_iota(jnp.int32, (N, N), 0)
+    cols = lax.broadcasted_iota(jnp.int32, (N, N), 1)
+    take = (rows == 2 * (cols % HALF) + cols // HALF).astype(F32).astype(BF)
+    for col in (0, 1):
+        sine, cosine = sine_and_cosine(phase[:, half(col)])
+        plain[0, col] = cosine
+        plain[1, col] = sine
+    for index, out in ((0, kernel_cos), (1, kernel_sin)):
+        for parity in (0, 1):
+            picked = [plain[index, col, pl.ds(parity, HALF, stride=2), :] for col in (0, 1)]
+            rest = jnp.concatenate(picked, 1)
+            value = jnp.zeros((HALF, N), F32)
+            for _ in range(3):
+                term = rest.astype(BF)
+                value = value + dot(term, take)
+                rest = rest - term.astype(F32)
+            out[half(parity), :] = value
+
+
+def filters(phase):
+    shape = jax.ShapeDtypeStruct((N, N), F32)
+    return pl.pallas_call(
+        filter_kernel,
+        name="filters",
+        out_shape=[shape, shape],
+        scratch_shapes=[pltpu.VMEM((2, 2, N, HALF), F32)],
+        compiler_params=pltpu.CompilerParams(vmem_limit_bytes=VMEM_LIMIT),
+    )(phase)
+
+
+def window_kernel(where, offsets, phase_all, amp_all, *rest):
+    outs, (field, phase, amp, sems) = rest[:RING], rest[RING:]
     rank = where[0]
+
+    def loads(layer, block):
+        rows = half(block)
+        return [
+            pltpu.make_async_copy(
+                source.at[layer, rows, :], target.at[layer, rows, :], sems.at[kind, layer, block]
+            )
+            for kind, source, target in ((0, phase_all, phase), (1, amp_all, amp))
+        ]
+
     for layer in (0, 1):
-        for col in range(3):
-            for block in range(3):
+        for block in range(3):
+            for copy in loads(layer, block):
+                copy.start()
+    for layer in (0, 1):
+        for block in range(3):
+            for copy in loads(layer, block):
+                copy.wait()
+            for col in range(3):
                 sine, cosine = sine_and_cosine(phase[layer, half(block), half(col)])
                 size = amp[layer, half(block), half(col)]
                 field[layer, 0, col, half(block), :] = size * cosine
@@ -148,9 +194,14 @@
         window_kernel,
         name="windows",
         out_shape=[shape] * RING,
-        in_specs=[SM, SM, VM, VM],
+        in_specs=[SM, SM, HB, HB],
         out_specs=[VM] * RING,
-        scratch_shapes=[pltpu.VMEM((2, 2, 3, PATCH, HALF), F32)],
+        scratch_shapes=[
+            pltpu.VMEM((2, 2, 3, PATCH, HALF), F32),
+            pltpu.VMEM((2, PATCH, PATCH), F32),
+            pltpu.VMEM((2, PATCH, PATCH), F32),
+            pltpu.SemaphoreType.DMA((2, 2, 3)),
+        ],
         compiler_params=pltpu.CompilerParams(vmem_limit_bytes=VMEM_LIMIT),
     )(where, offsets, phase, amp)
 
@@ -160,7 +211,7 @@
     earlier = () if first else rest[RING : 2 * RING]
     rest = rest[RING + len(earlier) :]
     tables = rest[:5]
-    count = RING + 1 if first else RING
+    count = RING + 1
     outs = rest[5 : 5 + count]
     trans, waves, middle, mixed, filtered, second, in_sems, out_sems = rest[5 + count :]
     rank = where[0]
@@ -222,6 +273,8 @@
             copies = [
                 pltpu.make_async_copy(earlier[k], outs[k], out_sems.at[k]) for k in range(RING)
             ]
+            middle[...] = jnp.zeros_like(middle)
+            copies.append(pltpu.make_async_copy(middle, outs[RING], out_sems.at[RING]))
             for copy in copies:
                 copy.start()
             for copy in copies:
@@ -229,7 +282,7 @@
 
 
 def run_chain(first, where, start, windows, earlier, tables):
-    count = RING + 1 if first else RING
+    count = RING + 1
     wave = jax.ShapeDtypeStruct((2, N, N), BF)
     return pl.pallas_call(
         functools.partial(chain_kernel, first),
@@ -253,9 +306,9 @@
     windows = rest[:RING]
     entries = rest[RING : 2 * RING]
     tables = rest[2 * RING : 2 * RING + 5]
-    payload = rest[2 * RING + 5]
-    trans, waves, psi, grads, ending, final, middle, mixed, filtered, second, sems = rest[
-        2 * RING + 6 :
+    probe, payload = rest[2 * RING + 5 : 2 * RING + 7]
+    trans, waves, psi, grads, middle_sum, middle, mixed, filtered, second, sems = rest[
+        2 * RING + 7 :
     ]
     rank = where[0]
 
@@ -273,7 +326,6 @@
         for copy in loads(index):
             copy.start()
     grads[...] = jnp.zeros_like(grads)
-    ending[...] = jnp.zeros_like(ending)
     for index in range(RING):
         for copy in loads(index):
             copy.wait()
@@ -297,14 +349,9 @@
                     qr, qi = reals[col], imags[col]
                     terms[0].append(pltpu.roll(wr * qr + wi * qi, turn, 1))
                     terms[1].append(pltpu.roll(wr * qi - wi * qr, turn, 1))
-                    next_real = (tr * qr + ti * qi).astype(BF)
-                    next_imag = (tr * qi - ti * qr).astype(BF)
                     if layer == 1:
-                        middle[parity, half(0), half(col)] = next_real
-                        middle[parity, half(1), half(col)] = next_imag
-                    else:
-                        ending[parity, half(0), half(col)] += next_real.astype(F32)
-                        ending[parity, half(1), half(col)] += next_imag.astype(F32)
+                        middle[parity, half(0), half(col)] = (tr * qr + ti * qi).astype(BF)
+                        middle[parity, half(1), half(col)] = (tr * qi - ti * qr).astype(BF)
                 rows = pl.ds(offsets[position, 0] + parity, HALF, stride=2)
                 zero = jnp.zeros((HALF, HALF), F32)
                 for part in (0, 1):
@@ -324,51 +371,45 @@
     lax.fori_loop(0, RING, visit, 0)
     chunks = payload.shape[0]
     rows_each = PATCH // chunks
-    probe_each = N // chunks
-
-    for parity in (0, 1):
-        for part in (0, 1):
-            for col in (0, 1):
-                final[part, col, pl.ds(parity, HALF, stride=2), :] = ending[
-                    parity, half(part), half(col)
-                ]
+    whole = 4 * rows_each
+    total = jnp.zeros((HALF, HALF), F32)
+    for source in range(DEPTH):
+        total = total + probe[source].astype(F32)
+    middle_sum[...] = total
 
     def pack(chunk, carry):
         rows = pl.ds(pl.multiple_of(chunk * rows_each, 8), rows_each)
-        probe_rows = pl.ds(pl.multiple_of(chunk * probe_each, 8), probe_each)
+        own = pl.ds(pl.multiple_of(chunk * 8, 8), 8)
         for col in range(3):
             pieces = [grads[layer, part, col, rows, :] for layer in (0, 1) for part in (0, 1)]
-            if col < 2:
-                pieces += [final[part, col, probe_rows, :] for part in (0, 1)]
-            else:
-                pieces += [jnp.zeros((2 * probe_each, HALF), F32)]
+            pieces.append(middle_sum[own, :] if col == 0 else jnp.zeros((8, HALF), F32))
+            pieces.append(jnp.zeros((8, HALF), F32))
             payload[chunk, :, half(col)] = jnp.concatenate(pieces, 0).astype(BF)
         return carry
 
     lax.fori_loop(0, chunks, pack, 0)
 
 
-def slice_terms(chunks, where, offsets, saved, windows, entries, tables):
-    rows = 4 * (PATCH // chunks) + 2 * (N // chunks)
+def slice_terms(chunks, where, offsets, saved, windows, entries, tables, probe):
+    rows = 4 * (PATCH // chunks) + 16
     return pl.pallas_call(
         terms_kernel,
         name="terms",
         out_shape=jax.ShapeDtypeStruct((chunks, rows, PATCH), BF),
-        in_specs=[SM, SM, ANY] + [ANY] * (2 * RING) + [VM] * 5,
+        in_specs=[SM, SM, ANY] + [ANY] * (2 * RING) + [VM] * 6,
         out_specs=VM,
         scratch_shapes=[
             pltpu.VMEM((RING, 2, 2, N, N), BF),
             pltpu.VMEM((RING, 2, N, N), BF),
             pltpu.VMEM((RING, 2, 2, N, N), BF),
             pltpu.VMEM((2, 2, 3, PATCH, HALF), F32),
-            pltpu.VMEM((2, N, N), F32),
-            pltpu.VMEM((2, 2, N, HALF), F32),
+            pltpu.VMEM((HALF, HALF), F32),
             pltpu.VMEM((2, N, N), BF),
             *step_scratch(),
             pltpu.SemaphoreType.DMA((3, RING)),
         ],
         compiler_params=pltpu.CompilerParams(vmem_limit_bytes=VMEM_LIMIT),
-    )(where, offsets, saved, *windows, *entries, *tables)
+    )(where, offsets, saved, *windows, *entries, *tables, probe)
 
 
 def order_kernel(where, residual, saved, start, waves):
@@ -411,6 +452,57 @@
         ],
         compiler_params=pltpu.CompilerParams(vmem_limit_bytes=VMEM_LIMIT),
     )(where, residual, saved)
+
+
+def pieces_kernel(wave, pieces):
+    width = N // DEPTH
+    lane = lax.broadcasted_iota(jnp.int32, (HALF, HALF), 1) // width
+    for piece in range(DEPTH):
+        per_tile = HALF // width
+        value = jnp.zeros((HALF, HALF), F32)
+        for parity in (0, 1):
+            for part in (0, 1):
+                place = 2 * parity + part
+                source = wave[parity, half(part), half(piece // per_tile)].astype(F32)
+                shift = (place - piece % per_tile) * width % HALF
+                moved = pltpu.roll(source, shift, 1) if shift else source
+                value = jnp.where(lane == place, moved, value)
+        pieces[piece] = value.astype(BF)
+
+
+def column_pieces(wave):
+    return pl.pallas_call(
+        pieces_kernel,
+        name="pieces",
+        out_shape=jax.ShapeDtypeStruct((DEPTH, HALF, HALF), BF),
+        compiler_params=pltpu.CompilerParams(vmem_limit_bytes=VMEM_LIMIT),
+    )(wave)
+
+
+def total_kernel(received, rows_out, probe_out):
+    chunks, rows, _ = received.shape
+    whole = rows - 16
+    for at in range(0, rows, 16):
+        value = received[0, at : at + 16, :].astype(F32)
+        for chunk in range(1, chunks):
+            value = value + received[chunk, at : at + 16, :].astype(F32)
+        if at < whole:
+            rows_out[at : at + 16, :] = value
+        else:
+            probe_out[...] = value[:8, :HALF]
+
+
+def totals(received):
+    _, rows, _ = received.shape
+    return pl.pallas_call(
+        total_kernel,
+        name="totals",
+        out_shape=[
+            jax.ShapeDtypeStruct((rows - 16, PATCH), F32),
+            jax.ShapeDtypeStruct((8, HALF), F32),
+        ],
+        compiler_params=pltpu.CompilerParams(vmem_limit_bytes=VMEM_LIMIT),
+    )(received)
 
 
 def turned(array, distance):
@@ -431,21 +523,20 @@
     chunks = lax.axis_size("probe")
     where = jnp.stack([depth_at % RING, depth_at // RING]).astype(jnp.int32)
     own = transmission_windows(where, offsets, object_phase, object_amp)
-    ordered = split_order(prop_phase)
-    tables = (*transform_tables(N), jnp.cos(ordered), jnp.sin(ordered))
+    tables = (*transform_tables(N), *filters(prop_phase))
     start, waves = row_parity_first(where, residual, saved_waves)
     foreign = exchanged(own)
     *deep, leaving = run_chain(True, where, start, foreign, (), tables)
     arrived = lax.ppermute(leaving, "depth", [(RING + i, i) for i in range(RING)])
-    entries = run_chain(False, where, arrived, foreign, deep, tables)
-    payload = slice_terms(chunks, where, offsets, waves, own, exchanged(entries), tables)
+    *entries, ending = run_chain(False, where, arrived, foreign, deep, tables)
+    entries = exchanged(entries)
+    probe = lax.all_to_all(column_pieces(ending), "depth", 0, 0, tiled=True)
+    payload = slice_terms(chunks, where, offsets, waves, own, entries, tables, probe)
     received = lax.all_to_all(payload, "probe", 0, 0, tiled=True)
-    total = jnp.sum(received.astype(F32), axis=0)
-    rows_each = PATCH // chunks
-    object_grad = total[: 4 * rows_each].reshape(2, 2, rows_each, PATCH)
-    probe_rows = total[4 * rows_each :, :N].reshape(2, N // chunks, 8, N // 8)
-    spread = lax.all_to_all(jnp.moveaxis(probe_rows, 2, 0), "depth", 0, 0, tiled=True)
-    return (object_grad, spread[0])
+    rows, probe_rows = totals(received)
+    object_grad = rows.reshape(2, 2, PATCH // chunks, PATCH)
+    probe_grad = probe_rows.reshape(8, 2, 2, N // DEPTH).transpose(2, 0, 1, 3)
+    return (object_grad, probe_grad.reshape(2, 16, N // DEPTH))
 
 
 def solution(mesh):

time: 177 us -> 122 us (0.69)
  local copies, waits for them, and re-layouts: 65.2 us -> 6.69 us
  blocking collectives: 30.1 us -> 41.4 us
  waiting for transfers between devices: 31.4 us -> 26 us
  starting transfers between devices: 15.7 us -> 12.7 us
    sin x4 -> x0, local copies, waits for them, and re-layouts: 28.6 us -> none  [shards(): tables = (*transform_tables(N), jnp.cos(ordered), jnp.sin(ordered))]
    cos x2 -> x0, local copies, waits for them, and re-layouts: 28 us -> none  [shards(): tables = (*transform_tables(N), jnp.cos(ordered), jnp.sin(ordered))]
    all_to_all x0 -> x1, blocking collectives: none -> 13.4 us  [shards(): probe = lax.all_to_all(column_pieces(ending), 'depth', 0, 0, tiled=True)]
    all_to_all x1 -> x0, waiting for transfers between devices: 5.59 us -> none  [shards(): lax.all_to_all(jnp.moveaxis(probe_rows, 2, 0), 'depth', 0, 0, tiled=True)]
    all_to_all x1 -> x0, starting transfers between devices: 3.91 us -> none  [shards(): lax.all_to_all(jnp.moveaxis(probe_rows, 2, 0), 'depth', 0, 0, tiled=True)]
    all_to_all x1, blocking collectives: 30.1 us -> 28 us  [shards(): received = lax.all_to_all(payload, 'probe', 0, 0, tiled=True)]
    pallas_call x1, Pallas kernels: 3.68 us -> 5.7 us  [transmission_windows(): pl.pallas_call(window_kernel, name='windows', out_shape=[shape] * RING, i...]
    unnamed x17 -> x13, local copies, waits for them, and re-layouts: 6.69 us -> 6 us
  transfers between devices with their start and end apart: 8 -> 7, of which waited for: 4 -> 2; matrix products, arithmetic and copies ran while one was open for 35% -> 4% of each run, Pallas kernels for 1% -> 3%
where the time goes in v2:
time: 122 us
  blocking collectives  41.4 us (34%)
  Pallas kernels  29.2 us (24%)
  waiting for transfers between devices  26 us (21%)
  starting transfers between devices  12.7 us (10%)
  local copies, waits for them, and re-layouts  6.69 us (5%)
  other arithmetic  4.98 us (4%)
    all_to_all x1, blocking collectives, shards(): received = lax.all_to_all(payload, 'probe', 0, 0, tiled=True)  28 us
    ppermute x1, waiting for transfers between devices, shards(): lax.ppermute(leaving, 'depth', [(RING + i, i) for i in range(RING)])  14.4 us
    all_to_all x1, blocking collectives, shards(): probe = lax.all_to_all(column_pieces(ending), 'depth', 0, 0, tiled=True)  13.4 us
    ppermute x6, waiting for transfers between devices, turned(): return lax.ppermute(array, 'depth', route)  11.6 us
    ppermute x6, starting transfers between devices, turned(): return lax.ppermute(array, 'depth', route)  11.4 us
    pallas_call x1, Pallas kernels, slice_terms(): pl.pallas_call(terms_kernel, name='terms', out_shape=jax.ShapeDtypeStruct...  10.9 us
    pallas_call x2, Pallas kernels, run_chain(): pl.pallas_call(functools.partial(chain_kernel, first), name='chain_deep'...  8.8 us
    unnamed x13, local copies, waits for them, and re-layouts  6 us
  transfers between devices with their start and end apart: 7, of which 2 were waited for; matrix products, arithmetic and copies ran while one was open for 4% of the time, Pallas kernels for 3%

profile of v2, /device:TPU:0, one launch (start us, length us, event | category | flops | bytes accessed | tf_op | source)
XLA Modules:
  0.0 121.9 jit_solution(6818763332192022883)
XLA Ops:
  0.6 0.0 copy-start.1
  0.7 0.9 copy.9.offsets
  1.6 0.1 pad_add_fusion.where
  1.6 0.0 copy-start.2
  1.6 1.3 %copy-done.2 = f32[2,384,384]{2,1,0:T(8,128)S(1)} copy-done((f32[2,384,384]{2,1,0:T(8,128)S(1)}, f32[2,384,384]{2,1,0:T(8,128)}, u32[]{:S(2)}) %copy-start.2) | copy-done | bytes 1179672
  2.9 0.0 copy-start.3
  2.9 1.3 %copy-done.3 = f32[2,384,384]{2,1,0:T(8,128)S(1)} copy-done((f32[2,384,384]{2,1,0:T(8,128)S(1)}, f32[2,384,384]{2,1,0:T(8,128)}, u32[]{:S(2)}) %copy-start.3) | copy-done | bytes 1179672
  4.2 0.0 copy-start.5
  4.2 5.7 %windows.1 = (bf16[2,2,256,256]{3,2,1,0:T(8,128)(2,1)S(1)}, bf16[2,2,256,256]{3,2,1,0:T(8,128)(2,1)S(1)}, bf16[2,2,256,256]{3,2,1,0:T(8,128)(2,1)S(1)}, bf16[2,2,256,256]{3,2,1,0:T(8,128)(2,1)S(1)}) custom-call(s32[2]{0:T(128)S(1)} %pad_add_fusion.where, s32[4,2]{1,0:T(4,128)S(1)} %copy.9.offsets, f32[2,384,384]{2,1,0:T(8,128)S(1)} %copy-done.2, ...), custom_call_target="tpu_custom_call" | custom-call | tf_op jit(solution)/shard_map/windows/pallas_call | solution.py:193
  9.9 2.1 %collective-permute-start = (bf16[2,2,256,256]{3,2,1,0:T(8,128)(2,1)S(1)}, bf16[2,2,256,256]{3,2,1,0:T(8,128)(2,1)S(1)}, u32[]{:S(2)}, u32[]{:S(2)}) collective-permute-start(bf16[2,2,256,256]{3,2,1,0:T(8,128)(2,1)S(1)} %get-tuple-element.24.rest_1_), channel_id=1, source_target_pairs={{0,16},{16,32},{32,48},{48,0},{64,80},{80,96},{96,112},{112,64},{1... | collective-permute-start | bytes 1572872 | tf_op jit(solution)/shard_map/ppermute | solution.py:514
  12.0 3.6 %collective-permute-start.1 = (bf16[2,2,256,256]{3,2,1,0:T(8,128)(2,1)S(1)}, bf16[2,2,256,256]{3,2,1,0:T(8,128)(2,1)S(1)}, u32[]{:S(2)}, u32[]{:S(2)}) collective-permute-start(bf16[2,2,256,256]{3,2,1,0:T(8,128)(2,1)S(1)} %get-tuple-element.25.rest_2_), channel_id=1, source_target_pairs={{0,32},{16,48},{32,0},{48,16},{64,96},{80,112},{96,64},{112,80},{1... | collective-permute-start | bytes 1572872 | tf_op jit(solution)/shard_map/ppermute | solution.py:514
  15.6 1.0 collective-permute-start.2
  16.6 0.0 copy-done.5
  16.6 0.6 filters.1
  17.2 0.0 copy-done.1
  17.2 0.0 copy-start.4
  17.2 1.2 copy-done.4
  18.5 2.2 %reorder.1 = (bf16[2,256,256]{2,1,0:T(8,128)(2,1)S(1)}, bf16[4,2,2,256,256]{4,3,2,1,0:T(8,128)(2,1)S(1)}) custom-call(s32[2]{0:T(128)S(1)} %pad_add_fusion.where, bf16[4,2,256,256]{3,2,1,0:T(8,128)(2,1)S(1)} %copy-done.4, bf16[2,4,2,256,256]{4,3,2,1,0:T(8,128)(2,1)S(1)} %copy-done.1), custom_call_target="tpu_custom_call" | custom-call | tf_op jit(solution)/shard_map/reorder/pallas_call | solution.py:436
  20.6 0.0 copy-start
  20.6 1.3 %copy-done = bf16[4,2,2,256,256]{4,3,2,1,0:T(8,128)(2,1)} copy-done((bf16[4,2,2,256,256]{4,3,2,1,0:T(8,128)(2,1)}, bf16[4,2,2,256,256]{4,3,2,1,0:T(8,128)(2,1)S(1)}, u32[]{:S(2)}) %copy-start) | copy-done | bytes 2097176
  22.0 4.9 %fusion.11 = (bf16[2,256,256]{2,1,0:T(8,128)(2,1)S(1)}, bf16[2,256,256]{2,1,0:T(8,128)(2,1)S(1)}, bf16[2,256,256]{2,1,0:T(8,128)(2,1)S(1)}) fusion(f32[256]{0:T(256)S(1)} %get-tuple-element.50, s32[256]{0:T(256)S(1)} %get-tuple-element.47, s32[256]{0:T(256)S(1)} %get-tuple-element.48, pred[256]{0:T(512)(128)(4,1)S(1)} %get-tuple-element.45, ...), kind=kLoop, calls=%fused_computation.24 | loop fusion | flops 6160384 | bytes 791040 | tf_op jit(solution)/shard_map/convert_element_type | solution.py:46
  26.9 0.0 collective-permute-done.rest_1_
  26.9 11.6 %collective-permute-done.1.rest_2_ = bf16[2,2,256,256]{3,2,1,0:T(8,128)(2,1)S(1)} collective-permute-done((bf16[2,2,256,256]{3,2,1,0:T(8,128)(2,1)S(1)}, bf16[2,2,256,256]{3,2,1,0:T(8,128)(2,1)S(1)}, u32[]{:S(2)}, u32[]{:S(2)}) %collective-permute-start.1) | collective-permute-done | bytes 524320 | tf_op jit(solution)/shard_map/ppermute | solution.py:514
  38.5 0.0 collective-permute-done.2.rest_3_
  38.5 0.6 chain_deep.1
  39.1 1.3 %collective-permute-start.3 = (bf16[2,256,256]{2,1,0:T(8,128)(2,1)S(1)}, bf16[2,256,256]{2,1,0:T(8,128)(2,1)S(1)}, u32[]{:S(2)}, u32[]{:S(2)}) collective-permute-start(bf16[2,256,256]{2,1,0:T(8,128)(2,1)S(1)} %get-tuple-element.30), channel_id=1, source_target_pairs={{64,0},{80,16},{96,32},{112,48},{65,1},{81,17},{97,33},{113,49},{6... | collective-permute-start | bytes 786440 | tf_op jit(solution)/shard_map/ppermute | solution.py:530
  40.4 14.4 %collective-permute-done.3.start = bf16[2,256,256]{2,1,0:T(8,128)(2,1)S(1)} collective-permute-done((bf16[2,256,256]{2,1,0:T(8,128)(2,1)S(1)}, bf16[2,256,256]{2,1,0:T(8,128)(2,1)S(1)}, u32[]{:S(2)}, u32[]{:S(2)}) %collective-permute-start.3) | collective-permute-done | bytes 262176 | tf_op jit(solution)/shard_map/ppermute | solution.py:530
  54.8 8.2 %chain_top.1 = (bf16[2,256,256]{2,1,0:T(8,128)(2,1)S(1)}, bf16[2,256,256]{2,1,0:T(8,128)(2,1)S(1)}, bf16[2,256,256]{2,1,0:T(8,128)(2,1)S(1)}, bf16[2,256,256]{2,1,0:T(8,128)(2,1)S(1)}, bf16[2,256,256]{2,1,0:T(8,128)(2,1)S(1)}) custom-call(s32[2]{0:T(128)S(1)} %pad_add_fusion.where, bf16[2,256,256]{2,1,0:T(8,128)(2,1)S(1)} %collective-permute-done.3.start, ...), custom_call_target="tpu_custom_call" | custom-call | tf_op jit(solution)/shard_map/chain_top/pallas_call | solution.py:287
  63.0 2.0 %collective-permute-start.4 = (bf16[2,256,256]{2,1,0:T(8,128)(2,1)S(1)}, bf16[2,256,256]{2,1,0:T(8,128)(2,1)S(1)}, u32[]{:S(2)}, u32[]{:S(2)}) collective-permute-start(bf16[2,256,256]{2,1,0:T(8,128)(2,1)S(1)} %get-tuple-element.36), channel_id=1, source_target_pairs={{0,16},{16,32},{32,48},{48,0},{64,80},{80,96},{96,112},{112,64},{1... | collective-permute-start | bytes 786440 | tf_op jit(solution)/shard_map/ppermute | solution.py:514
  65.0 2.8 %collective-permute-start.5 = (bf16[2,256,256]{2,1,0:T(8,128)(2,1)S(1)}, bf16[2,256,256]{2,1,0:T(8,128)(2,1)S(1)}, u32[]{:S(2)}, u32[]{:S(2)}) collective-permute-start(bf16[2,256,256]{2,1,0:T(8,128)(2,1)S(1)} %get-tuple-element.37), channel_id=1, source_target_pairs={{0,32},{16,48},{32,0},{48,16},{64,96},{80,112},{96,64},{112,80},{1... | collective-permute-start | bytes 786440 | tf_op jit(solution)/shard_map/ppermute | solution.py:514
  67.7 0.0 collective-permute-start.6
  67.7 0.3 pieces.1
  68.0 13.4 %all_to_all.10.rest_13_ = bf16[8,128,128]{2,1,0:T(8,128)(2,1)S(1)} all-to-all(bf16[8,128,128]{2,1,0:T(8,128)(2,1)S(1)} %pieces.1), channel_id=1, replica_groups=mesh['depth'=8,'probe'=16] {'depth'}, dimensions={0} | all-to-all | bytes 524288 | tf_op jit(solution)/shard_map/all_to_all | solution.py:533
  81.5 0.0 collective-permute-done.4.rest_5_
  81.5 0.0 collective-permute-done.5.rest_6_
  81.5 0.0 collective-permute-done.6.rest_7_
  81.5 10.9 %terms.1 = bf16[16,112,384]{2,1,0:T(8,128)(2,1)S(1)} custom-call(s32[2]{0:T(128)S(1)} %pad_add_fusion.where, s32[4,2]{1,0:T(4,128)S(1)} %copy.9.offsets, bf16[4,2,2,256,256]{4,3,2,1,0:T(8,128)(2,1)} %copy-done, bf16[2,2,256,256]{3,2,1,0:T(8,128)(2,1)S(1)} %get-tuple-element.23.rest_0_, bf16[2,2,256,256]{3,2,1,0:T(8,128)(2,1)S(1)} %get-tuple-element.24.rest_1_, ...), custom_call_target="tpu_custom_call" | custom-call | tf_op jit(solution)/shard_map/terms/pallas_call | solution.py:395
  92.4 28.0 %all_to_all.11.received = bf16[16,112,384]{2,1,0:T(8,128)(2,1)S(1)} all-to-all(bf16[16,112,384]{2,1,0:T(8,128)(2,1)S(1)} %terms.1), channel_id=1, replica_groups=mesh['depth'=8,'probe'=16] {'probe'}, dimensions={0} | all-to-all | bytes 2752512 | tf_op jit(solution)/shard_map/all_to_all | solution.py:535
  120.3 0.8 totals.1
  121.2 0.1 reshape.14
  121.2 0.6 copy.10
  (3 shorter events, 0.0 us)
Async XLA Ops:
  0.6 16.6 %copy-start.1 = (bf16[2,4,2,256,256]{4,3,2,1,0:T(8,128)(2,1)S(1)}, bf16[2,4,2,256,256]{4,3,2,1,0:T(8,128)(2,1)}, u32[]{:S(2)}) copy-start(bf16[2,4,2,256,256]{4,3,2,1,0:T(8,128)(2,1)} %saved.1) | copy-start | bytes 6291460
  1.6 1.3 %copy-start.2 = (f32[2,384,384]{2,1,0:T(8,128)S(1)}, f32[2,384,384]{2,1,0:T(8,128)}, u32[]{:S(2)}) copy-start(f32[2,384,384]{2,1,0:T(8,128)} %phase_all.1) | copy-start | bytes 3538948
  2.9 1.3 %copy-start.3 = (f32[2,384,384]{2,1,0:T(8,128)S(1)}, f32[2,384,384]{2,1,0:T(8,128)}, u32[]{:S(2)}) copy-start(f32[2,384,384]{2,1,0:T(8,128)} %amp_all.1) | copy-start | bytes 3538948
  4.2 12.4 %copy-start.5 = (f32[256,256]{1,0:T(8,128)S(1)}, f32[256,256]{1,0:T(8,128)}, u32[]{:S(2)}) copy-start(f32[256,256]{1,0:T(8,128)} %phase.1) | copy-start | bytes 786436
  9.9 17.0 %collective-permute-start = (bf16[2,2,256,256]{3,2,1,0:T(8,128)(2,1)S(1)}, bf16[2,2,256,256]{3,2,1,0:T(8,128)(2,1)S(1)}, u32[]{:S(2)}, u32[]{:S(2)}) collective-permute-start(bf16[2,2,256,256]{3,2,1,0:T(8,128)(2,1)S(1)} %get-tuple-element.24.rest_1_), channel_id=1, source_target_pairs={{0,16},{16,32},{32,48},{48,0},{64,80},{80,96},{96,112},{112,64},{1... | collective-permute-start | bytes 1572872 | tf_op jit(solution)/shard_map/ppermute | solution.py:514
  12.0 26.5 %collective-permute-start.1 = (bf16[2,2,256,256]{3,2,1,0:T(8,128)(2,1)S(1)}, bf16[2,2,256,256]{3,2,1,0:T(8,128)(2,1)S(1)}, u32[]{:S(2)}, u32[]{:S(2)}) collective-permute-start(bf16[2,2,256,256]{3,2,1,0:T(8,128)(2,1)S(1)} %get-tuple-element.25.rest_2_), channel_id=1, source_target_pairs={{0,32},{16,48},{32,0},{48,16},{64,96},{80,112},{96,64},{112,80},{1... | collective-permute-start | bytes 1572872 | tf_op jit(solution)/shard_map/ppermute | solution.py:514
  15.6 22.9 %collective-permute-start.2 = (bf16[2,2,256,256]{3,2,1,0:T(8,128)(2,1)S(1)}, bf16[2,2,256,256]{3,2,1,0:T(8,128)(2,1)S(1)}, u32[]{:S(2)}, u32[]{:S(2)}) collective-permute-start(bf16[2,2,256,256]{3,2,1,0:T(8,128)(2,1)S(1)} %get-tuple-element.26.rest_3_), channel_id=1, source_target_pairs={{0,48},{16,0},{32,16},{48,32},{64,112},{80,64},{96,80},{112,96},{1... | collective-permute-start | bytes 1572872 | tf_op jit(solution)/shard_map/ppermute | solution.py:514
  17.2 1.2 %copy-start.4 = (bf16[4,2,256,256]{3,2,1,0:T(8,128)(2,1)S(1)}, bf16[4,2,256,256]{3,2,1,0:T(8,128)(2,1)}, u32[]{:S(2)}) copy-start(bf16[4,2,256,256]{3,2,1,0:T(8,128)(2,1)} %residual.1) | copy-start | bytes 3145732
  20.6 1.3 %copy-start = (bf16[4,2,2,256,256]{4,3,2,1,0:T(8,128)(2,1)}, bf16[4,2,2,256,256]{4,3,2,1,0:T(8,128)(2,1)S(1)}, u32[]{:S(2)}) copy-start(bf16[4,2,2,256,256]{4,3,2,1,0:T(8,128)(2,1)S(1)} %get-tuple-element.22.saved) | copy-start | bytes 6291460
  39.1 15.7 %collective-permute-start.3 = (bf16[2,256,256]{2,1,0:T(8,128)(2,1)S(1)}, bf16[2,256,256]{2,1,0:T(8,128)(2,1)S(1)}, u32[]{:S(2)}, u32[]{:S(2)}) collective-permute-start(bf16[2,256,256]{2,1,0:T(8,128)(2,1)S(1)} %get-tuple-element.30), channel_id=1, source_target_pairs={{64,0},{80,16},{96,32},{112,48},{65,1},{81,17},{97,33},{113,49},{6... | collective-permute-start | bytes 786440 | tf_op jit(solution)/shard_map/ppermute | solution.py:530
  63.0 18.5 %collective-permute-start.4 = (bf16[2,256,256]{2,1,0:T(8,128)(2,1)S(1)}, bf16[2,256,256]{2,1,0:T(8,128)(2,1)S(1)}, u32[]{:S(2)}, u32[]{:S(2)}) collective-permute-start(bf16[2,256,256]{2,1,0:T(8,128)(2,1)S(1)} %get-tuple-element.36), channel_id=1, source_target_pairs={{0,16},{16,32},{32,48},{48,0},{64,80},{80,96},{96,112},{112,64},{1... | collective-permute-start | bytes 786440 | tf_op jit(solution)/shard_map/ppermute | solution.py:514
  65.0 16.5 %collective-permute-start.5 = (bf16[2,256,256]{2,1,0:T(8,128)(2,1)S(1)}, bf16[2,256,256]{2,1,0:T(8,128)(2,1)S(1)}, u32[]{:S(2)}, u32[]{:S(2)}) collective-permute-start(bf16[2,256,256]{2,1,0:T(8,128)(2,1)S(1)} %get-tuple-element.37), channel_id=1, source_target_pairs={{0,32},{16,48},{32,0},{48,16},{64,96},{80,112},{96,64},{112,80},{1... | collective-permute-start | bytes 786440 | tf_op jit(solution)/shard_map/ppermute | solution.py:514
  67.7 13.8 %collective-permute-start.6 = (bf16[2,256,256]{2,1,0:T(8,128)(2,1)S(1)}, bf16[2,256,256]{2,1,0:T(8,128)(2,1)S(1)}, u32[]{:S(2)}, u32[]{:S(2)}) collective-permute-start(bf16[2,256,256]{2,1,0:T(8,128)(2,1)S(1)} %get-tuple-element.38), channel_id=1, source_target_pairs={{0,48},{16,0},{32,16},{48,32},{64,112},{80,64},{96,80},{112,96},{1... | collective-permute-start | bytes 786440 | tf_op jit(solution)/shard_map/ppermute | solution.py:514

commit v3 on v2

--- a/solution.py
+++ b/solution.py
@@ -18,10 +18,9 @@
 ANY = pl.BlockSpec(memory_space=pl.ANY)
 VM = pl.BlockSpec(memory_space=pltpu.VMEM)
 SM = pl.BlockSpec(memory_space=pltpu.SMEM)
-HB = pl.BlockSpec(memory_space=pltpu.HBM)
 SINE = (0.999999995716, -0.166666579699, 0.00833305061733, -0.000198090463574, 2.60516627618e-06)
 COSINE = (0.99999999978, -0.49999999357, 0.0416666362089, -0.00138883608423, 2.47601355058e-05, -2.60510761786e-07)
-VMEM_LIMIT = 48 * 1024 * 1024
+VMEM_LIMIT = 20 * 1024 * 1024
 
 
 def half(index):
@@ -52,7 +51,7 @@
     return jnp.dot(a, b, preferred_element_type=F32)
 
 
-def back_step(source, tables, mixed, filtered, second, finish):
+def back_step(source, tables, mixed, filtered, second, finish, ready=None):
     inward, table, flipped, kernel_cos, kernel_sin = tables
     for part in (0, 1):
         even = dot(inward[0, half(part), :], source[0])
@@ -79,6 +78,8 @@
         for col in (0, 1):
             second[col, half(0), half(part)] = total[:, half(col)]
             second[col, half(1), half(part)] = diff[:, half(col)]
+    if ready is not None:
+        ready()
     totals, diffs = [], []
     for row in (0, 1):
         even = dot(second[0, half(row), :], table[0])
@@ -194,7 +195,7 @@
         window_kernel,
         name="windows",
         out_shape=[shape] * RING,
-        in_specs=[SM, SM, HB, HB],
+        in_specs=[SM, SM, ANY, ANY],
         out_specs=[VM] * RING,
         scratch_shapes=[
             pltpu.VMEM((2, 2, 3, PATCH, HALF), F32),
@@ -217,37 +218,43 @@
     rank = where[0]
     active = where[1] == 1 if first else where[1] == 0
 
-    def loads():
-        copies = []
-        for distance in range(RING):
-            slot = (rank + RING - distance) % RING
-            copies.append(
-                pltpu.make_async_copy(windows[distance], trans.at[slot], in_sems.at[distance])
-            )
-        copies.append(
-            pltpu.make_async_copy(start, waves.at[(2 * RING - 1 - rank) % RING], in_sems.at[RING])
-        )
-        return copies
-
-    def stores():
-        return [
-            pltpu.make_async_copy(waves.at[k], outs[k], out_sems.at[k]) for k in range(count)
-        ]
+    def window_load(distance):
+        slot = (rank + RING - distance) % RING
+        return pltpu.make_async_copy(windows[distance], trans.at[slot], in_sems.at[slot])
+
+    def store(k):
+        return pltpu.make_async_copy(waves.at[k], outs[k], out_sems.at[k])
 
     @pl.when(active)
     def _():
-        for copy in loads():
-            copy.start()
-        for copy in loads():
-            copy.wait()
+        begin_load = pltpu.make_async_copy(
+            start, waves.at[(2 * RING - 1 - rank) % RING], in_sems.at[RING]
+        )
+        begin_load.start()
+        for distance in range(RING):
+            window_load(distance).start()
+        begin_load.wait()
 
         def pair(step, carry):
             pair_at = RING - 1 - step
-            source = waves.at[(pair_at + RING - rank) % RING]
+            slot = (pair_at + RING - rank) % RING
+            for k in range(RING):
+
+                @pl.when(slot == k)
+                def _(k=k):
+                    store(k).start()
+
+            source = waves.at[slot]
             target = waves.at[
                 jnp.where(pair_at == 0, RING, (pair_at + 2 * RING - 1 - rank) % RING)
             ]
             for layer, begin, end in ((1, source, middle), (0, middle, target)):
+
+                def ready(layer=layer):
+                    if layer == 1:
+                        pltpu.make_async_copy(
+                            windows[0], trans.at[pair_at], in_sems.at[pair_at]
+                        ).wait()
 
                 def finish(parity, reals, imags, layer=layer, end=end):
                     for col in (0, 1):
@@ -257,14 +264,13 @@
                         end[parity, half(0), half(col)] = (tr * qr + ti * qi).astype(BF)
                         end[parity, half(1), half(col)] = (tr * qi - ti * qr).astype(BF)
 
-                back_step(begin, tables, mixed, filtered, second, finish)
+                back_step(begin, tables, mixed, filtered, second, finish, ready)
             return carry
 
         lax.fori_loop(0, RING, pair, 0)
-        for copy in stores():
-            copy.start()
-        for copy in stores():
-            copy.wait()
+        store(RING).start()
+        for k in range(RING + 1):
+            store(k).wait()
 
     if not first:
 
@@ -302,117 +308,102 @@
     )(where, start, *windows, *earlier, *tables)
 
 
-def terms_kernel(where, offsets, saved, *rest):
-    windows = rest[:RING]
-    entries = rest[RING : 2 * RING]
-    tables = rest[2 * RING : 2 * RING + 5]
-    probe, payload = rest[2 * RING + 5 : 2 * RING + 7]
-    trans, waves, psi, grads, middle_sum, middle, mixed, filtered, second, sems = rest[
-        2 * RING + 7 :
-    ]
-    rank = where[0]
-
-    def loads(index):
-        position = (rank + RING - index) % RING
-        return [
-            pltpu.make_async_copy(entries[index], waves.at[index], sems.at[0, index]),
-            pltpu.make_async_copy(
-                windows[(RING - index) % RING], trans.at[index], sems.at[1, index]
-            ),
-            pltpu.make_async_copy(saved.at[position], psi.at[index], sems.at[2, index]),
-        ]
-
-    for index in range(RING):
-        for copy in loads(index):
-            copy.start()
-    grads[...] = jnp.zeros_like(grads)
-    for index in range(RING):
-        for copy in loads(index):
-            copy.wait()
+def visit_kernel(index, where, offsets, entry, window, psi, *rest):
+    tables = rest[:5]
+    grads, middle, mixed, filtered, second = rest[-5:]
+    if index == 0:
+        grads[...] = jnp.zeros_like(grads)
     lane = lax.broadcasted_iota(jnp.int32, (HALF, HALF), 1)
-
-    def visit(index, carry):
-        position = (rank + RING - index) % RING
-        col_at = offsets[position, 1]
-        turn = col_at % HALF
-        inside = lane >= col_at
-
-        for layer in (1, 0):
-
-            def finish(parity, reals, imags, layer=layer):
-                terms = ([], [])
-                for col in (0, 1):
-                    wr = psi[index, layer, parity, half(0), half(col)].astype(F32)
-                    wi = psi[index, layer, parity, half(1), half(col)].astype(F32)
-                    tr = trans[index, layer, parity, half(0), half(col)].astype(F32)
-                    ti = trans[index, layer, parity, half(1), half(col)].astype(F32)
-                    qr, qi = reals[col], imags[col]
-                    terms[0].append(pltpu.roll(wr * qr + wi * qi, turn, 1))
-                    terms[1].append(pltpu.roll(wr * qi - wi * qr, turn, 1))
-                    if layer == 1:
-                        middle[parity, half(0), half(col)] = (tr * qr + ti * qi).astype(BF)
-                        middle[parity, half(1), half(col)] = (tr * qi - ti * qr).astype(BF)
-                rows = pl.ds(offsets[position, 0] + parity, HALF, stride=2)
-                zero = jnp.zeros((HALF, HALF), F32)
-                for part in (0, 1):
-                    left, right = terms[part]
-                    placed = (
-                        jnp.where(inside, left, zero),
-                        jnp.where(inside, right, left),
-                        jnp.where(inside, zero, right),
-                    )
-                    for col in range(3):
-                        grads[layer, part, col, rows, :] += placed[col]
-
-            begin = waves.at[index] if layer == 1 else middle
-            back_step(begin, tables, mixed, filtered, second, finish)
-        return carry
-
-    lax.fori_loop(0, RING, visit, 0)
+    position = (where[0] + RING - index) % RING
+    col_at = offsets[position, 1]
+    turn = col_at % HALF
+    inside = lane >= col_at
+
+    for layer in (1, 0):
+
+        def finish(parity, reals, imags, layer=layer):
+            terms = ([], [])
+            for col in (0, 1):
+                wr = psi[layer, parity, half(0), half(col)].astype(F32)
+                wi = psi[layer, parity, half(1), half(col)].astype(F32)
+                qr, qi = reals[col], imags[col]
+                terms[0].append(pltpu.roll(wr * qr + wi * qi, turn, 1))
+                terms[1].append(pltpu.roll(wr * qi - wi * qr, turn, 1))
+                if layer == 1:
+                    tr = window[layer, parity, half(0), half(col)].astype(F32)
+                    ti = window[layer, parity, half(1), half(col)].astype(F32)
+                    middle[parity, half(0), half(col)] = (tr * qr + ti * qi).astype(BF)
+                    middle[parity, half(1), half(col)] = (tr * qi - ti * qr).astype(BF)
+            rows = pl.ds(offsets[position, 0] + parity, HALF, stride=2)
+            zero = jnp.zeros((HALF, HALF), F32)
+            for part in (0, 1):
+                left, right = terms[part]
+                placed = (
+                    jnp.where(inside, left, zero),
+                    jnp.where(inside, right, left),
+                    jnp.where(inside, zero, right),
+                )
+                for col in range(3):
+                    grads[layer, part, col, rows, :] += placed[col]
+
+        back_step(entry if layer == 1 else middle, tables, mixed, filtered, second, finish)
+
+
+def visit(index, where, offsets, entry, window, psi, tables, grads):
+    earlier = () if index == 0 else (grads,)
+    return pl.pallas_call(
+        functools.partial(visit_kernel, index),
+        name=f"visit_{index}",
+        out_shape=jax.ShapeDtypeStruct((2, 2, 3, PATCH, HALF), F32),
+        in_specs=[SM, SM] + [VM] * (8 + len(earlier)),
+        out_specs=VM,
+        scratch_shapes=[pltpu.VMEM((2, N, N), BF), *step_scratch()],
+        input_output_aliases={10: 0} if earlier else {},
+        compiler_params=pltpu.CompilerParams(vmem_limit_bytes=VMEM_LIMIT),
+    )(where, offsets, entry, window, psi, *tables, *earlier)
+
+
+def pack_kernel(grads, probe, payload, summed):
     chunks = payload.shape[0]
     rows_each = PATCH // chunks
-    whole = 4 * rows_each
     total = jnp.zeros((HALF, HALF), F32)
     for source in range(DEPTH):
         total = total + probe[source].astype(F32)
-    middle_sum[...] = total
-
-    def pack(chunk, carry):
-        rows = pl.ds(pl.multiple_of(chunk * rows_each, 8), rows_each)
-        own = pl.ds(pl.multiple_of(chunk * 8, 8), 8)
+    summed[...] = total
+    for chunk in range(chunks):
+        rows = slice(chunk * rows_each, (chunk + 1) * rows_each)
         for col in range(3):
             pieces = [grads[layer, part, col, rows, :] for layer in (0, 1) for part in (0, 1)]
-            pieces.append(middle_sum[own, :] if col == 0 else jnp.zeros((8, HALF), F32))
+            own = slice(8 * chunk, 8 * chunk + 8)
+            pieces.append(summed[own, :] if col == 0 else jnp.zeros((8, HALF), F32))
             pieces.append(jnp.zeros((8, HALF), F32))
             payload[chunk, :, half(col)] = jnp.concatenate(pieces, 0).astype(BF)
-        return carry
-
-    lax.fori_loop(0, chunks, pack, 0)
-
-
-def slice_terms(chunks, where, offsets, saved, windows, entries, tables, probe):
+
+
+def packed(chunks, grads, probe):
     rows = 4 * (PATCH // chunks) + 16
     return pl.pallas_call(
-        terms_kernel,
-        name="terms",
+        pack_kernel,
+        name="pack",
         out_shape=jax.ShapeDtypeStruct((chunks, rows, PATCH), BF),
-        in_specs=[SM, SM, ANY] + [ANY] * (2 * RING) + [VM] * 6,
+        in_specs=[VM, VM],
         out_specs=VM,
-        scratch_shapes=[
-            pltpu.VMEM((RING, 2, 2, N, N), BF),
-            pltpu.VMEM((RING, 2, N, N), BF),
-            pltpu.VMEM((RING, 2, 2, N, N), BF),
-            pltpu.VMEM((2, 2, 3, PATCH, HALF), F32),
-            pltpu.VMEM((HALF, HALF), F32),
-            pltpu.VMEM((2, N, N), BF),
-            *step_scratch(),
-            pltpu.SemaphoreType.DMA((3, RING)),
-        ],
-        compiler_params=pltpu.CompilerParams(vmem_limit_bytes=VMEM_LIMIT),
-    )(where, offsets, saved, *windows, *entries, *tables, probe)
-
-
-def order_kernel(where, residual, saved, start, waves):
+        scratch_shapes=[pltpu.VMEM((HALF, HALF), F32)],
+        compiler_params=pltpu.CompilerParams(vmem_limit_bytes=VMEM_LIMIT),
+    )(grads, probe)
+
+
+def order_kernel(where, residual, saved, start, *rest):
+    outs, (first, waves, sems) = rest[:RING], rest[RING:]
+    rank = where[0]
+    loads = [pltpu.make_async_copy(residual.at[rank], first, sems.at[RING])]
+    for index in range(RING):
+        position = (rank + RING - index) % RING
+        loads.append(
+            pltpu.make_async_copy(saved.at[:, position], waves.at[index], sems.at[index])
+        )
+    for copy in loads:
+        copy.start()
     rows = lax.broadcasted_iota(jnp.int32, (N, N), 0)
     cols = lax.broadcasted_iota(jnp.int32, (N, N), 1)
     take = (cols == 2 * (rows % HALF) + rows // HALF).astype(F32).astype(BF)
@@ -423,12 +414,12 @@
             for parity in (0, 1):
                 target[parity, half(part), :] = ordered[half(parity), :]
 
-    for layer in (0, 1):
-        reorder(saved.at[layer, 0], waves.at[0, layer])
-
-    @pl.when(pl.program_id(0) == where[0])
-    def _():
-        reorder(residual.at[0], start)
+    loads[0].wait()
+    reorder(first, start)
+    for index in range(RING):
+        loads[1 + index].wait()
+        for layer in (0, 1):
+            reorder(waves.at[index, layer], outs[index].at[layer])
 
 
 def row_parity_first(where, residual, saved):
@@ -436,19 +427,14 @@
     return pl.pallas_call(
         order_kernel,
         name="reorder",
-        out_shape=[
-            jax.ShapeDtypeStruct(wave, BF),
-            jax.ShapeDtypeStruct((RING, 2, *wave), BF),
-        ],
-        grid=(RING,),
-        in_specs=[
-            SM,
-            pl.BlockSpec((1, *wave), lambda i: (i, 0, 0, 0)),
-            pl.BlockSpec((2, 1, *wave), lambda i: (0, i, 0, 0, 0)),
-        ],
-        out_specs=[
-            pl.BlockSpec(wave, lambda i: (0, 0, 0)),
-            pl.BlockSpec((1, 2, *wave), lambda i: (i, 0, 0, 0, 0)),
+        out_shape=[jax.ShapeDtypeStruct(wave, BF)]
+        + [jax.ShapeDtypeStruct((2, *wave), BF)] * RING,
+        in_specs=[SM, ANY, ANY],
+        out_specs=[VM] * (RING + 1),
+        scratch_shapes=[
+            pltpu.VMEM(wave, BF),
+            pltpu.VMEM((RING, 2, *wave), BF),
+            pltpu.SemaphoreType.DMA((RING + 1,)),
         ],
         compiler_params=pltpu.CompilerParams(vmem_limit_bytes=VMEM_LIMIT),
     )(where, residual, saved)
@@ -524,14 +510,20 @@
     where = jnp.stack([depth_at % RING, depth_at // RING]).astype(jnp.int32)
     own = transmission_windows(where, offsets, object_phase, object_amp)
     tables = (*transform_tables(N), *filters(prop_phase))
-    start, waves = row_parity_first(where, residual, saved_waves)
+    start, *waves = row_parity_first(where, residual, saved_waves)
     foreign = exchanged(own)
     *deep, leaving = run_chain(True, where, start, foreign, (), tables)
     arrived = lax.ppermute(leaving, "depth", [(RING + i, i) for i in range(RING)])
     *entries, ending = run_chain(False, where, arrived, foreign, deep, tables)
     entries = exchanged(entries)
     probe = lax.all_to_all(column_pieces(ending), "depth", 0, 0, tiled=True)
-    payload = slice_terms(chunks, where, offsets, waves, own, entries, tables, probe)
+    grads = None
+    for index in (0, 3, 1, 2):
+        window = own[(RING - index) % RING]
+        grads = visit(
+            index, where, offsets, entries[index], window, waves[index], tables, grads
+        )
+    payload = packed(chunks, grads, probe)
     received = lax.all_to_all(payload, "probe", 0, 0, tiled=True)
     rows, probe_rows = totals(received)
     object_grad = rows.reshape(2, 2, PATCH // chunks, PATCH)

time: 122 us -> 122 us (level)
  blocking collectives: 41.4 us -> 28 us
  local copies, waits for them, and re-layouts: 6.69 us -> 11.7 us
  starting transfers between devices: 12.7 us -> 16.9 us
  Pallas kernels: 29.2 us -> 32.6 us
    all_to_all x1 -> x0, blocking collectives: 13.4 us -> none  [shards(): probe = lax.all_to_all(column_pieces(ending), 'depth', 0, 0, tiled=True)]
    unnamed x13 -> x51, local copies, waits for them, and re-layouts: 6 us -> 11 us
    all_to_all x0 -> x1, starting transfers between devices: none -> 4.22 us  [shards(): probe = lax.all_to_all(column_pieces(ending), 'depth', 0, 0, tiled=True)]
    pallas_call x1 -> x5, Pallas kernels: 10.9 us -> 13.3 us  [the longest x4 12.2 us: visit(): pl.pallas_call(functools.partial(visit_kernel, index), name=f'visit_{inde...]
  transfers between devices with their start and end apart: 7 -> 8, of which waited for: 2 -> 4; matrix products, arithmetic and copies ran while one was open for 4% -> 4% of each run, Pallas kernels for 3% -> 13%
where the time goes in v3:
time: 122 us; the launch traced here: 121 us
  Pallas kernels  32.6 us (27%)
  blocking collectives  28 us (23%)
  waiting for transfers between devices  26.2 us (21%)
  starting transfers between devices  16.9 us (14%)
  local copies, waits for them, and re-layouts  11.7 us (10%)
  other arithmetic  5.01 us (4%)
    all_to_all x1, blocking collectives, shards(): received = lax.all_to_all(payload, 'probe', 0, 0, tiled=True)  28 us
    ppermute x1, waiting for transfers between devices, shards(): lax.ppermute(leaving, 'depth', [(RING + i, i) for i in range(RING)])  14.7 us
    pallas_call x4, Pallas kernels, visit(): pl.pallas_call(functools.partial(visit_kernel, index), name=f'visit_{inde...  12.2 us
    ppermute x6, waiting for transfers between devices, turned(): return lax.ppermute(array, 'depth', route)  11.5 us
    ppermute x6, starting transfers between devices, turned(): return lax.ppermute(array, 'depth', route)  11.3 us
    unnamed x51, local copies, waits for them, and re-layouts  11 us
    pallas_call x2, Pallas kernels, run_chain(): pl.pallas_call(functools.partial(chain_kernel, first), name='chain_deep'...  8.94 us
    pallas_call x1, Pallas kernels, transmission_windows(): pl.pallas_call(window_kernel, name='windows', out_shape=[shape] * RING, i...  5.7 us
  transfers between devices with their start and end apart: 8, of which 4 were waited for; matrix products, arithmetic and copies ran while one was open for 4% of the time, Pallas kernels for 13%

profile of v3, /device:TPU:0, one launch (start us, length us, event | category | flops | bytes accessed | tf_op | source)
XLA Modules:
  0.0 121.2 jit_solution(1132383116893138229)
XLA Ops:
  0.7 0.9 copy.15.offsets
  1.6 0.1 pad_add_fusion.where
  1.6 1.3 %copy-done.5 = f32[2,384,384]{2,1,0:T(8,128)S(1)} copy-done((f32[2,384,384]{2,1,0:T(8,128)S(1)}, f32[2,384,384]{2,1,0:T(8,128)}, u32[]{:S(2)}) %copy-start.5) | copy-done | bytes 1179672
  2.9 1.3 %copy-done.6 = f32[2,384,384]{2,1,0:T(8,128)S(1)} copy-done((f32[2,384,384]{2,1,0:T(8,128)S(1)}, f32[2,384,384]{2,1,0:T(8,128)}, u32[]{:S(2)}) %copy-start.6) | copy-done | bytes 1179672
  4.2 5.7 %windows.1 = (bf16[2,2,256,256]{3,2,1,0:T(8,128)(2,1)S(1)}, bf16[2,2,256,256]{3,2,1,0:T(8,128)(2,1)S(1)}, bf16[2,2,256,256]{3,2,1,0:T(8,128)(2,1)S(1)}, bf16[2,2,256,256]{3,2,1,0:T(8,128)(2,1)S(1)}) custom-call(s32[2]{0:T(128)S(1)} %pad_add_fusion.where, s32[4,2]{1,0:T(4,128)S(1)} %copy.15.offsets, f32[2,384,384]{2,1,0:T(8,128)S(1)} %copy-done.5, ...), custom_call_target="tpu_custom_call" | custom-call | tf_op jit(solution)/shard_map/windows/pallas_call | solution.py:194
  9.9 0.0 copy-start.10
  9.9 0.0 copy-start.12
  9.9 0.0 copy-start.14
  9.9 2.1 %collective-permute-start = (bf16[2,2,256,256]{3,2,1,0:T(8,128)(2,1)S(1)}, bf16[2,2,256,256]{3,2,1,0:T(8,128)(2,1)S(1)}, u32[]{:S(2)}, u32[]{:S(2)}) collective-permute-start(bf16[2,2,256,256]{3,2,1,0:T(8,128)(2,1)S(1)} %get-tuple-element.27.window), channel_id=1, source_target_pairs={{0,16},{16,32},{32,48},{48,0},{64,80},{80,96},{96,112},{112,64},{1... | collective-permute-start | bytes 1572872 | tf_op jit(solution)/shard_map/ppermute | solution.py:500
  12.0 3.6 %collective-permute-start.1 = (bf16[2,2,256,256]{3,2,1,0:T(8,128)(2,1)S(1)}, bf16[2,2,256,256]{3,2,1,0:T(8,128)(2,1)S(1)}, u32[]{:S(2)}, u32[]{:S(2)}) collective-permute-start(bf16[2,2,256,256]{3,2,1,0:T(8,128)(2,1)S(1)} %get-tuple-element.28.window), channel_id=1, source_target_pairs={{0,32},{16,48},{32,0},{48,16},{64,96},{80,112},{96,64},{112,80},{1... | collective-permute-start | bytes 1572872 | tf_op jit(solution)/shard_map/ppermute | solution.py:500
  15.6 1.0 collective-permute-start.2
  16.6 0.6 filters.1
  17.3 0.0 copy-start.7
  17.3 1.2 %copy-done.7 = bf16[4,2,256,256]{3,2,1,0:T(8,128)(2,1)S(1)} copy-done((bf16[4,2,256,256]{3,2,1,0:T(8,128)(2,1)S(1)}, bf16[4,2,256,256]{3,2,1,0:T(8,128)(2,1)}, u32[]{:S(2)}) %copy-start.7) | copy-done | bytes 1048600
  18.5 2.3 %reorder.1 = (bf16[2,256,256]{2,1,0:T(8,128)(2,1)S(1)}, bf16[2,2,256,256]{3,2,1,0:T(8,128)(2,1)S(1)}, bf16[2,2,256,256]{3,2,1,0:T(8,128)(2,1)S(1)}, bf16[2,2,256...) custom-call(s32[2]{0:T(128)S(1)} %pad_add_fusion.where, bf16[4,2,256,256]{3,2,1,0:T(8,128)(2,1)S(1)} %copy-done.7, ...), custom_call_target="tpu_custom_call" | custom-call | tf_op jit(solution)/shard_map/reorder/pallas_call | solution.py:427
  20.8 0.8 copy-done.16
  21.6 0.8 copy-done.18
  22.4 4.9 %fusion.11 = (bf16[2,256,256]{2,1,0:T(8,128)(2,1)S(1)}, bf16[2,256,256]{2,1,0:T(8,128)(2,1)S(1)}, bf16[2,256,256]{2,1,0:T(8,128)(2,1)S(1)}) fusion(f32[256]{0:T(256)S(1)} %get-tuple-element.56, s32[256]{0:T(256)S(1)} %get-tuple-element.53, s32[256]{0:T(256)S(1)} %get-tuple-element.54, pred[256]{0:T(512)(128)(4,1)S(1)} %get-tuple-element.51, ...), kind=kLoop, calls=%fused_computation.24 | loop fusion | flops 6160384 | bytes 791040 | tf_op jit(solution)/shard_map/convert_element_type | solution.py:45
  27.4 0.0 collective-permute-done.rest_1_
  27.4 11.1 %collective-permute-done.1.rest_2_ = bf16[2,2,256,256]{3,2,1,0:T(8,128)(2,1)S(1)} collective-permute-done((bf16[2,2,256,256]{3,2,1,0:T(8,128)(2,1)S(1)}, bf16[2,2,256,256]{3,2,1,0:T(8,128)(2,1)S(1)}, u32[]{:S(2)}, u32[]{:S(2)}) %collective-permute-start.1) | collective-permute-done | bytes 524320 | tf_op jit(solution)/shard_map/ppermute | solution.py:500
  38.5 0.0 collective-permute-done.2.rest_3_
  38.5 0.6 chain_deep.1
  39.2 1.3 %collective-permute-start.3 = (bf16[2,256,256]{2,1,0:T(8,128)(2,1)S(1)}, bf16[2,256,256]{2,1,0:T(8,128)(2,1)S(1)}, u32[]{:S(2)}, u32[]{:S(2)}) collective-permute-start(bf16[2,256,256]{2,1,0:T(8,128)(2,1)S(1)} %get-tuple-element.32), channel_id=1, source_target_pairs={{64,0},{80,16},{96,32},{112,48},{65,1},{81,17},{97,33},{113,49},{6... | collective-permute-start | bytes 786440 | tf_op jit(solution)/shard_map/ppermute | solution.py:516
  40.5 14.7 %collective-permute-done.3.start = bf16[2,256,256]{2,1,0:T(8,128)(2,1)S(1)} collective-permute-done((bf16[2,256,256]{2,1,0:T(8,128)(2,1)S(1)}, bf16[2,256,256]{2,1,0:T(8,128)(2,1)S(1)}, u32[]{:S(2)}, u32[]{:S(2)}) %collective-permute-start.3) | collective-permute-done | bytes 262176 | tf_op jit(solution)/shard_map/ppermute | solution.py:516
  55.1 8.3 %chain_top.1 = (bf16[2,256,256]{2,1,0:T(8,128)(2,1)S(1)}, bf16[2,256,256]{2,1,0:T(8,128)(2,1)}, bf16[2,256,256]{2,1,0:T(8,128)(2,1)}, bf16[2,256,256]{2,1,0:T(8,128)(2,1)}, bf16[2,256,256]{2,1,0:T(8,128)(2,1)S(1)}) custom-call(s32[2]{0:T(128)S(1)} %pad_add_fusion.where, bf16[2,256,256]{2,1,0:T(8,128)(2,1)S(1)} %collective-permute-done.3.start, ...), custom_call_target="tpu_custom_call" | custom-call | tf_op jit(solution)/shard_map/chain_top/pallas_call | solution.py:293
  63.5 0.7 copy-done.22
  64.2 3.2 %collective-permute-start.6 = (bf16[2,256,256]{2,1,0:T(8,128)(2,1)}, bf16[2,256,256]{2,1,0:T(8,128)(2,1)}, u32[]{:S(2)}, u32[]{:S(2)}) collective-permute-start(bf16[2,256,256]{2,1,0:T(8,128)(2,1)} %get-tuple-element.41), channel_id=1, source_target_pairs={{0,48},{16,0},{32,16},{48,32},{64,112},{80,64},{96,80},{112,96},{1... | collective-permute-start | bytes 786440 | tf_op jit(solution)/shard_map/ppermute | solution.py:500
  67.4 0.0 collective-permute-start.5
  67.4 1.5 %collective-permute-start.4 = (bf16[2,256,256]{2,1,0:T(8,128)(2,1)}, bf16[2,256,256]{2,1,0:T(8,128)(2,1)}, u32[]{:S(2)}, u32[]{:S(2)}) collective-permute-start(bf16[2,256,256]{2,1,0:T(8,128)(2,1)} %get-tuple-element.37), channel_id=1, source_target_pairs={{0,32},{16,48},{32,0},{48,16},{64,96},{80,112},{96,64},{112,80},{1... | collective-permute-start | bytes 786440 | tf_op jit(solution)/shard_map/ppermute | solution.py:500
  68.8 1.0 pieces.1
  69.8 4.2 %all-to-all-start = ((bf16[8,128,128]{2,1,0:T(8,128)(2,1)}), bf16[8,128,128]{2,1,0:T(8,128)(2,1)}, u32[]{:S(2)}, u32[]{:S(2)}) async-start(bf16[8,128,128]{2,1,0:T(8,128)(2,1)} %pieces.1), calls=%async_computation | async-start | bytes 524288 | tf_op jit(solution)/shard_map/all_to_all | solution.py:519
  74.0 0.9 copy-done.1
  75.0 1.0 copy-done.3
  76.0 1.0 copy-done.9
  77.1 0.9 copy-done.23
  78.0 2.8 %visit_0.1.rest_5_ = f32[2,2,3,384,128]{4,3,2,1,0:T(8,128)S(1)} custom-call(s32[2]{0:T(128)S(1)} %pad_add_fusion.where, s32[4,2]{1,0:T(4,128)S(1)} %copy.15.offsets, bf16[2,256,256]{2,1,0:T(8,128)(2,1)S(1)} %copy-done.23, bf16[2,2,256,256]{3,2,1,0:T(8,128)(2,1)S(1)} %copy-done.3, bf16[2,2,256,256]{3,2,1,0:T(8,128)(2,1)S(1)} %copy-done.9, ...), custom_call_target="tpu_custom_call" | custom-call | tf_op jit(solution)/shard_map/visit_0/pallas_call | solution.py:354
  80.8 0.1 collective-permute-done.6.entry
  80.9 3.1 %visit_3.1.rest_5_ = f32[2,2,3,384,128]{4,3,2,1,0:T(8,128)S(1)} custom-call(s32[2]{0:T(128)S(1)} %pad_add_fusion.where, s32[4,2]{1,0:T(4,128)S(1)} %copy.15.offsets, bf16[2,256,256]{2,1,0:T(8,128)(2,1)} %collective-permute-done.6.entry, bf16[2,2,256,256]{3,2,1,0:T(8,128)(2,1)S(1)} %copy-done.15, ...), custom_call_target="tpu_custom_call", output_to_operand_aliasing={{}: (10, {})} | custom-call | tf_op jit(solution)/shard_map/visit_3/pallas_call | solution.py:354
  84.1 0.3 collective-permute-done.5.entry
  84.4 3.2 %visit_1.1.rest_5_ = f32[2,2,3,384,128]{4,3,2,1,0:T(8,128)S(1)} custom-call(s32[2]{0:T(128)S(1)} %pad_add_fusion.where, s32[4,2]{1,0:T(4,128)S(1)} %copy.15.offsets, bf16[2,256,256]{2,1,0:T(8,128)(2,1)} %collective-permute-done.5.entry, bf16[2,2,256,256]{3,2,1,0:T(8,128)(2,1)S(1)} %copy-done.13, ...), custom_call_target="tpu_custom_call", output_to_operand_aliasing={{}: (10, {})} | custom-call | tf_op jit(solution)/shard_map/visit_1/pallas_call | solution.py:354
  87.5 0.0 collective-permute-done.4.entry
  87.6 3.1 %visit_2.1.grads = f32[2,2,3,384,128]{4,3,2,1,0:T(8,128)S(1)} custom-call(s32[2]{0:T(128)S(1)} %pad_add_fusion.where, s32[4,2]{1,0:T(4,128)S(1)} %copy.15.offsets, bf16[2,256,256]{2,1,0:T(8,128)(2,1)} %collective-permute-done.4.entry, bf16[2,2,256,256]{3,2,1,0:T(8,128)(2,1)S(1)} %copy-done.11, ...), custom_call_target="tpu_custom_call", output_to_operand_aliasing={{}: (10, {})} | custom-call | tf_op jit(solution)/shard_map/visit_2/pallas_call | solution.py:354
  90.6 0.0 all-to-all-done.probe
  90.6 1.1 pack.1
  91.8 28.0 %all_to_all.10.received = bf16[16,112,384]{2,1,0:T(8,128)(2,1)S(1)} all-to-all(bf16[16,112,384]{2,1,0:T(8,128)(2,1)S(1)} %pack.1), channel_id=1, replica_groups=mesh['depth'=8,'probe'=16] {'probe'}, dimensions={0} | all-to-all | bytes 2752512 | tf_op jit(solution)/shard_map/all_to_all | solution.py:527
  119.7 0.8 totals.1
  120.5 0.1 reshape.14
  120.6 0.6 copy.16
  (39 shorter events, 0.1 us)
Async XLA Ops:
  0.6 16.6 %copy-start.4 = (bf16[2,4,2,256,256]{4,3,2,1,0:T(8,128)(2,1)S(1)}, bf16[2,4,2,256,256]{4,3,2,1,0:T(8,128)(2,1)}, u32[]{:S(2)}) copy-start(bf16[2,4,2,256,256]{4,3,2,1,0:T(8,128)(2,1)} %saved.1) | copy-start | bytes 6291460
  1.6 1.3 %copy-start.5 = (f32[2,384,384]{2,1,0:T(8,128)S(1)}, f32[2,384,384]{2,1,0:T(8,128)}, u32[]{:S(2)}) copy-start(f32[2,384,384]{2,1,0:T(8,128)} %phase_all.1) | copy-start | bytes 3538948
  2.9 1.3 %copy-start.6 = (f32[2,384,384]{2,1,0:T(8,128)S(1)}, f32[2,384,384]{2,1,0:T(8,128)}, u32[]{:S(2)}) copy-start(f32[2,384,384]{2,1,0:T(8,128)} %amp_all.1) | copy-start | bytes 3538948
  4.2 12.5 %copy-start.24 = (f32[256,256]{1,0:T(8,128)S(1)}, f32[256,256]{1,0:T(8,128)}, u32[]{:S(2)}) copy-start(f32[256,256]{1,0:T(8,128)} %phase.1) | copy-start | bytes 786436
  9.9 17.4 %copy-start.10 = (bf16[2,2,256,256]{3,2,1,0:T(8,128)(2,1)}, bf16[2,2,256,256]{3,2,1,0:T(8,128)(2,1)S(1)}, u32[]{:S(2)}) copy-start(bf16[2,2,256,256]{3,2,1,0:T(8,128)(2,1)S(1)} %get-tuple-element.28.window) | copy-start | bytes 1572868
  9.9 17.4 %copy-start.12 = (bf16[2,2,256,256]{3,2,1,0:T(8,128)(2,1)}, bf16[2,2,256,256]{3,2,1,0:T(8,128)(2,1)S(1)}, u32[]{:S(2)}) copy-start(bf16[2,2,256,256]{3,2,1,0:T(8,128)(2,1)S(1)} %get-tuple-element.29.window) | copy-start | bytes 1572868
  9.9 17.4 %copy-start.14 = (bf16[2,2,256,256]{3,2,1,0:T(8,128)(2,1)}, bf16[2,2,256,256]{3,2,1,0:T(8,128)(2,1)S(1)}, u32[]{:S(2)}) copy-start(bf16[2,2,256,256]{3,2,1,0:T(8,128)(2,1)S(1)} %get-tuple-element.27.window) | copy-start | bytes 1572868
  9.9 45.2 %copy-start.2 = (bf16[2,2,256,256]{3,2,1,0:T(8,128)(2,1)}, bf16[2,2,256,256]{3,2,1,0:T(8,128)(2,1)S(1)}, u32[]{:S(2)}) copy-start(bf16[2,2,256,256]{3,2,1,0:T(8,128)(2,1)S(1)} %get-tuple-element.26.rest_0_.window) | copy-start | bytes 1572868
  9.9 17.4 %collective-permute-start = (bf16[2,2,256,256]{3,2,1,0:T(8,128)(2,1)S(1)}, bf16[2,2,256,256]{3,2,1,0:T(8,128)(2,1)S(1)}, u32[]{:S(2)}, u32[]{:S(2)}) collective-permute-start(bf16[2,2,256,256]{3,2,1,0:T(8,128)(2,1)S(1)} %get-tuple-element.27.window), channel_id=1, source_target_pairs={{0,16},{16,32},{32,48},{48,0},{64,80},{80,96},{96,112},{112,64},{1... | collective-permute-start | bytes 1572872 | tf_op jit(solution)/shard_map/ppermute | solution.py:500
  12.0 26.5 %collective-permute-start.1 = (bf16[2,2,256,256]{3,2,1,0:T(8,128)(2,1)S(1)}, bf16[2,2,256,256]{3,2,1,0:T(8,128)(2,1)S(1)}, u32[]{:S(2)}, u32[]{:S(2)}) collective-permute-start(bf16[2,2,256,256]{3,2,1,0:T(8,128)(2,1)S(1)} %get-tuple-element.28.window), channel_id=1, source_target_pairs={{0,32},{16,48},{32,0},{48,16},{64,96},{80,112},{96,64},{112,80},{1... | collective-permute-start | bytes 1572872 | tf_op jit(solution)/shard_map/ppermute | solution.py:500
  15.6 22.9 %collective-permute-start.2 = (bf16[2,2,256,256]{3,2,1,0:T(8,128)(2,1)S(1)}, bf16[2,2,256,256]{3,2,1,0:T(8,128)(2,1)S(1)}, u32[]{:S(2)}, u32[]{:S(2)}) collective-permute-start(bf16[2,2,256,256]{3,2,1,0:T(8,128)(2,1)S(1)} %get-tuple-element.29.window), channel_id=1, source_target_pairs={{0,48},{16,0},{32,16},{48,32},{64,112},{80,64},{96,80},{112,96},{1... | collective-permute-start | bytes 1572872 | tf_op jit(solution)/shard_map/ppermute | solution.py:500
  17.3 1.2 %copy-start.7 = (bf16[4,2,256,256]{3,2,1,0:T(8,128)(2,1)S(1)}, bf16[4,2,256,256]{3,2,1,0:T(8,128)(2,1)}, u32[]{:S(2)}) copy-start(bf16[4,2,256,256]{3,2,1,0:T(8,128)(2,1)} %residual.1) | copy-start | bytes 3145732
  20.8 0.8 copy-start.16
  21.6 0.8 copy-start.18
  22.4 16.1 %copy-start.8 = (bf16[2,2,256,256]{3,2,1,0:T(8,128)(2,1)}, bf16[2,2,256,256]{3,2,1,0:T(8,128)(2,1)S(1)}, u32[]{:S(2)}) copy-start(bf16[2,2,256,256]{3,2,1,0:T(8,128)(2,1)S(1)} %get-tuple-element.44.psi) | copy-start | bytes 1572868
  22.4 16.8 %copy-start.20 = (bf16[2,2,256,256]{3,2,1,0:T(8,128)(2,1)}, bf16[2,2,256,256]{3,2,1,0:T(8,128)(2,1)S(1)}, u32[]{:S(2)}) copy-start(bf16[2,2,256,256]{3,2,1,0:T(8,128)(2,1)S(1)} %get-tuple-element.42.psi) | copy-start | bytes 1572868
  27.3 36.1 %copy-start = (bf16[2,256,256]{2,1,0:T(8,128)(2,1)}, bf16[2,256,256]{2,1,0:T(8,128)(2,1)S(1)}, u32[]{:S(2)}) copy-start(bf16[2,256,256]{2,1,0:T(8,128)(2,1)S(1)} %get-tuple-element.50.rest_6_.rest_10_.rest_2_) | copy-start | bytes 786436
  39.2 16.0 %collective-permute-start.3 = (bf16[2,256,256]{2,1,0:T(8,128)(2,1)S(1)}, bf16[2,256,256]{2,1,0:T(8,128)(2,1)S(1)}, u32[]{:S(2)}, u32[]{:S(2)}) collective-permute-start(bf16[2,256,256]{2,1,0:T(8,128)(2,1)S(1)} %get-tuple-element.32), channel_id=1, source_target_pairs={{64,0},{80,16},{96,32},{112,48},{65,1},{81,17},{97,33},{113,49},{6... | collective-permute-start | bytes 786440 | tf_op jit(solution)/shard_map/ppermute | solution.py:516
  63.5 0.7 copy-start.22
  64.2 16.8 %collective-permute-start.6 = (bf16[2,256,256]{2,1,0:T(8,128)(2,1)}, bf16[2,256,256]{2,1,0:T(8,128)(2,1)}, u32[]{:S(2)}, u32[]{:S(2)}) collective-permute-start(bf16[2,256,256]{2,1,0:T(8,128)(2,1)} %get-tuple-element.41), channel_id=1, source_target_pairs={{0,48},{16,0},{32,16},{48,32},{64,112},{80,64},{96,80},{112,96},{1... | collective-permute-start | bytes 786440 | tf_op jit(solution)/shard_map/ppermute | solution.py:500
  67.4 17.0 %collective-permute-start.5 = (bf16[2,256,256]{2,1,0:T(8,128)(2,1)}, bf16[2,256,256]{2,1,0:T(8,128)(2,1)}, u32[]{:S(2)}, u32[]{:S(2)}) collective-permute-start(bf16[2,256,256]{2,1,0:T(8,128)(2,1)} %get-tuple-element.39), channel_id=1, source_target_pairs={{0,16},{16,32},{32,48},{48,0},{64,80},{80,96},{96,112},{112,64},{1... | collective-permute-start | bytes 786440 | tf_op jit(solution)/shard_map/ppermute | solution.py:500
  67.4 20.2 %collective-permute-start.4 = (bf16[2,256,256]{2,1,0:T(8,128)(2,1)}, bf16[2,256,256]{2,1,0:T(8,128)(2,1)}, u32[]{:S(2)}, u32[]{:S(2)}) collective-permute-start(bf16[2,256,256]{2,1,0:T(8,128)(2,1)} %get-tuple-element.37), channel_id=1, source_target_pairs={{0,32},{16,48},{32,0},{48,16},{64,96},{80,112},{96,64},{112,80},{1... | collective-permute-start | bytes 786440 | tf_op jit(solution)/shard_map/ppermute | solution.py:500
  69.8 20.8 %all-to-all-start = ((bf16[8,128,128]{2,1,0:T(8,128)(2,1)}), bf16[8,128,128]{2,1,0:T(8,128)(2,1)}, u32[]{:S(2)}, u32[]{:S(2)}) async-start(bf16[8,128,128]{2,1,0:T(8,128)(2,1)} %pieces.1), calls=%async_computation | async-start | bytes 524288 | tf_op jit(solution)/shard_map/all_to_all | solution.py:519
  74.0 1.0 copy-start.1
  75.0 1.0 copy-start.3
  76.0 1.0 copy-start.9
  77.1 0.9 copy-start.23
  78.0 2.9 %copy-start.15 = (bf16[2,2,256,256]{3,2,1,0:T(8,128)(2,1)S(1)}, bf16[2,2,256,256]{3,2,1,0:T(8,128)(2,1)}, u32[]{:S(2)}) copy-start(bf16[2,2,256,256]{3,2,1,0:T(8,128)(2,1)} %copy-done.14) | copy-start | bytes 1572868
  78.0 2.9 %copy-start.21 = (bf16[2,2,256,256]{3,2,1,0:T(8,128)(2,1)S(1)}, bf16[2,2,256,256]{3,2,1,0:T(8,128)(2,1)}, u32[]{:S(2)}) copy-start(bf16[2,2,256,256]{3,2,1,0:T(8,128)(2,1)} %copy-done.20) | copy-start | bytes 1572868
  80.9 3.4 %copy-start.13 = (bf16[2,2,256,256]{3,2,1,0:T(8,128)(2,1)S(1)}, bf16[2,2,256,256]{3,2,1,0:T(8,128)(2,1)}, u32[]{:S(2)}) copy-start(bf16[2,2,256,256]{3,2,1,0:T(8,128)(2,1)} %copy-done.12) | copy-start | bytes 1572868
  80.9 3.4 %copy-start.19 = (bf16[2,2,256,256]{3,2,1,0:T(8,128)(2,1)S(1)}, bf16[2,2,256,256]{3,2,1,0:T(8,128)(2,1)}, u32[]{:S(2)}) copy-start(bf16[2,2,256,256]{3,2,1,0:T(8,128)(2,1)} %copy-done.18) | copy-start | bytes 1572868
  84.3 3.2 %copy-start.11 = (bf16[2,2,256,256]{3,2,1,0:T(8,128)(2,1)S(1)}, bf16[2,2,256,256]{3,2,1,0:T(8,128)(2,1)}, u32[]{:S(2)}) copy-start(bf16[2,2,256,256]{3,2,1,0:T(8,128)(2,1)} %copy-done.10) | copy-start | bytes 1572868
  84.3 3.2 %copy-start.17 = (bf16[2,2,256,256]{3,2,1,0:T(8,128)(2,1)S(1)}, bf16[2,2,256,256]{3,2,1,0:T(8,128)(2,1)}, u32[]{:S(2)}) copy-start(bf16[2,2,256,256]{3,2,1,0:T(8,128)(2,1)} %copy-done.16) | copy-start | bytes 1572868

commit v4 on v3

--- a/solution.py
+++ b/solution.py
@@ -11,6 +11,7 @@
 BF = jnp.bfloat16
 F32 = jnp.float32
 RING = 4
+FAR = 2
 DEPTH = 8
 N = 256
 HALF = 128
@@ -21,6 +22,10 @@
 SINE = (0.999999995716, -0.166666579699, 0.00833305061733, -0.000198090463574, 2.60516627618e-06)
 COSINE = (0.99999999978, -0.49999999357, 0.0416666362089, -0.00138883608423, 2.47601355058e-05, -2.60510761786e-07)
 VMEM_LIMIT = 20 * 1024 * 1024
+
+
+def in_hbm(array):
+    return pltpu.with_memory_space_constraint(array, pltpu.HBM)
 
 
 def half(index):
@@ -145,7 +150,7 @@
 
 
 def window_kernel(where, offsets, phase_all, amp_all, *rest):
-    outs, (field, phase, amp, sems) = rest[:RING], rest[RING:]
+    outs, (field, phase, amp, sems) = rest[: RING + 1], rest[RING + 1 :]
     rank = where[0]
 
     def loads(layer, block):
@@ -183,20 +188,25 @@
                     turned = [
                         pltpu.roll(field[layer, part, col, rows, :], turn, 1) for col in range(3)
                     ]
+                    if distance == FAR:
+                        target = outs[distance if layer else RING]
+                    else:
+                        target = outs[distance].at[layer]
                     for col in (0, 1):
-                        outs[distance][layer, parity, half(part), half(col)] = jnp.where(
+                        target[parity, half(part), half(col)] = jnp.where(
                             inside, turned[col], turned[col + 1]
                         ).astype(BF)
 
 
 def transmission_windows(where, offsets, phase, amp):
-    shape = jax.ShapeDtypeStruct((2, 2, N, N), BF)
+    both = jax.ShapeDtypeStruct((2, 2, N, N), BF)
+    single = jax.ShapeDtypeStruct((2, N, N), BF)
     return pl.pallas_call(
         window_kernel,
         name="windows",
-        out_shape=[shape] * RING,
+        out_shape=[both, both, single, both, single],
         in_specs=[SM, SM, ANY, ANY],
-        out_specs=[VM] * RING,
+        out_specs=[VM] * (RING + 1),
         scratch_shapes=[
             pltpu.VMEM((2, 2, 3, PATCH, HALF), F32),
             pltpu.VMEM((2, PATCH, PATCH), F32),
@@ -204,13 +214,13 @@
             pltpu.SemaphoreType.DMA((2, 2, 3)),
         ],
         compiler_params=pltpu.CompilerParams(vmem_limit_bytes=VMEM_LIMIT),
-    )(where, offsets, phase, amp)
+    )(where, offsets, in_hbm(phase), in_hbm(amp))
 
 
 def chain_kernel(first, where, start, *rest):
-    windows = rest[:RING]
-    earlier = () if first else rest[RING : 2 * RING]
-    rest = rest[RING + len(earlier) :]
+    windows = rest[: RING + 1]
+    earlier = () if first else rest[RING + 1 : 2 * RING + 1]
+    rest = rest[RING + 1 + len(earlier) :]
     tables = rest[:5]
     count = RING + 1
     outs = rest[5 : 5 + count]
@@ -218,9 +228,13 @@
     rank = where[0]
     active = where[1] == 1 if first else where[1] == 0
 
-    def window_load(distance):
+    def window_load(distance, layer):
         slot = (rank + RING - distance) % RING
-        return pltpu.make_async_copy(windows[distance], trans.at[slot], in_sems.at[slot])
+        if distance == FAR:
+            source = windows[distance if layer else RING]
+        else:
+            source = windows[distance].at[layer]
+        return pltpu.make_async_copy(source, trans.at[slot, layer], in_sems.at[slot, layer])
 
     def store(k):
         return pltpu.make_async_copy(waves.at[k], outs[k], out_sems.at[k])
@@ -228,11 +242,12 @@
     @pl.when(active)
     def _():
         begin_load = pltpu.make_async_copy(
-            start, waves.at[(2 * RING - 1 - rank) % RING], in_sems.at[RING]
+            start, waves.at[(2 * RING - 1 - rank) % RING], in_sems.at[RING, 0]
         )
         begin_load.start()
         for distance in range(RING):
-            window_load(distance).start()
+            for layer in (1, 0):
+                window_load(distance, layer).start()
         begin_load.wait()
 
         def pair(step, carry):
@@ -251,10 +266,9 @@
             for layer, begin, end in ((1, source, middle), (0, middle, target)):
 
                 def ready(layer=layer):
-                    if layer == 1:
-                        pltpu.make_async_copy(
-                            windows[0], trans.at[pair_at], in_sems.at[pair_at]
-                        ).wait()
+                    pltpu.make_async_copy(
+                        windows[0].at[layer], trans.at[pair_at, layer], in_sems.at[pair_at, layer]
+                    ).wait()
 
                 def finish(parity, reals, imags, layer=layer, end=end):
                     for col in (0, 1):
@@ -294,23 +308,30 @@
         functools.partial(chain_kernel, first),
         name="chain_deep" if first else "chain_top",
         out_shape=[wave] * count,
-        in_specs=[SM, ANY] + [ANY] * RING + [ANY] * len(earlier) + [VM] * 5,
+        in_specs=[SM, ANY] + [ANY] * (RING + 1) + [ANY] * len(earlier) + [VM] * 5,
         out_specs=[ANY] * count,
         scratch_shapes=[
             pltpu.VMEM((RING, 2, 2, N, N), BF),
             pltpu.VMEM((RING + 1, 2, N, N), BF),
             pltpu.VMEM((2, N, N), BF),
             *step_scratch(),
-            pltpu.SemaphoreType.DMA((RING + 1,)),
+            pltpu.SemaphoreType.DMA((RING + 1, 2)),
             pltpu.SemaphoreType.DMA((RING + 1,)),
         ],
         compiler_params=pltpu.CompilerParams(vmem_limit_bytes=VMEM_LIMIT),
     )(where, start, *windows, *earlier, *tables)
 
 
-def visit_kernel(index, where, offsets, entry, window, psi, *rest):
+def visit_kernel(index, where, offsets, entry_at, window_at, psi_at, *rest):
     tables = rest[:5]
-    grads, middle, mixed, filtered, second = rest[-5:]
+    grads, entry, window, psi, middle, mixed, filtered, second, sems = rest[-9:]
+    loads = [
+        pltpu.make_async_copy(entry_at, entry, sems.at[0]),
+        pltpu.make_async_copy(window_at if index == FAR else window_at.at[1], window, sems.at[1]),
+        pltpu.make_async_copy(psi_at, psi, sems.at[2]),
+    ]
+    for copy in loads:
+        copy.start()
     if index == 0:
         grads[...] = jnp.zeros_like(grads)
     lane = lax.broadcasted_iota(jnp.int32, (HALF, HALF), 1)
@@ -318,6 +339,11 @@
     col_at = offsets[position, 1]
     turn = col_at % HALF
     inside = lane >= col_at
+    loads[0].wait()
+
+    def ready():
+        loads[1].wait()
+        loads[2].wait()
 
     for layer in (1, 0):
 
@@ -330,8 +356,8 @@
                 terms[0].append(pltpu.roll(wr * qr + wi * qi, turn, 1))
                 terms[1].append(pltpu.roll(wr * qi - wi * qr, turn, 1))
                 if layer == 1:
-                    tr = window[layer, parity, half(0), half(col)].astype(F32)
-                    ti = window[layer, parity, half(1), half(col)].astype(F32)
+                    tr = window[parity, half(0), half(col)].astype(F32)
+                    ti = window[parity, half(1), half(col)].astype(F32)
                     middle[parity, half(0), half(col)] = (tr * qr + ti * qi).astype(BF)
                     middle[parity, half(1), half(col)] = (tr * qi - ti * qr).astype(BF)
             rows = pl.ds(offsets[position, 0] + parity, HALF, stride=2)
@@ -346,7 +372,10 @@
                 for col in range(3):
                     grads[layer, part, col, rows, :] += placed[col]
 
-        back_step(entry if layer == 1 else middle, tables, mixed, filtered, second, finish)
+        if layer == 1:
+            back_step(entry, tables, mixed, filtered, second, finish, ready)
+        else:
+            back_step(middle, tables, mixed, filtered, second, finish)
 
 
 def visit(index, where, offsets, entry, window, psi, tables, grads):
@@ -355,12 +384,19 @@
         functools.partial(visit_kernel, index),
         name=f"visit_{index}",
         out_shape=jax.ShapeDtypeStruct((2, 2, 3, PATCH, HALF), F32),
-        in_specs=[SM, SM] + [VM] * (8 + len(earlier)),
+        in_specs=[SM, SM] + [ANY] * 3 + [VM] * (5 + len(earlier)),
         out_specs=VM,
-        scratch_shapes=[pltpu.VMEM((2, N, N), BF), *step_scratch()],
+        scratch_shapes=[
+            pltpu.VMEM((2, N, N), BF),
+            pltpu.VMEM((2, N, N), BF),
+            pltpu.VMEM((2, 2, N, N), BF),
+            pltpu.VMEM((2, N, N), BF),
+            *step_scratch(),
+            pltpu.SemaphoreType.DMA((3,)),
+        ],
         input_output_aliases={10: 0} if earlier else {},
         compiler_params=pltpu.CompilerParams(vmem_limit_bytes=VMEM_LIMIT),
-    )(where, offsets, entry, window, psi, *tables, *earlier)
+    )(where, offsets, *(in_hbm(array) for array in (entry, window, psi)), *tables, *earlier)
 
 
 def pack_kernel(grads, probe, payload, summed):
@@ -394,7 +430,7 @@
 
 
 def order_kernel(where, residual, saved, start, *rest):
-    outs, (first, waves, sems) = rest[:RING], rest[RING:]
+    outs, (first, waves, done, sems, out_sems) = rest[:RING], rest[RING:]
     rank = where[0]
     loads = [pltpu.make_async_copy(residual.at[rank], first, sems.at[RING])]
     for index in range(RING):
@@ -414,12 +450,17 @@
             for parity in (0, 1):
                 target[parity, half(part), :] = ordered[half(parity), :]
 
+    stores = []
     loads[0].wait()
     reorder(first, start)
     for index in range(RING):
         loads[1 + index].wait()
         for layer in (0, 1):
-            reorder(waves.at[index, layer], outs[index].at[layer])
+            reorder(waves.at[index, layer], done.at[index, layer])
+        stores.append(pltpu.make_async_copy(done.at[index], outs[index], out_sems.at[index]))
+        stores[-1].start()
+    for copy in stores:
+        copy.wait()
 
 
 def row_parity_first(where, residual, saved):
@@ -430,14 +471,16 @@
         out_shape=[jax.ShapeDtypeStruct(wave, BF)]
         + [jax.ShapeDtypeStruct((2, *wave), BF)] * RING,
         in_specs=[SM, ANY, ANY],
-        out_specs=[VM] * (RING + 1),
+        out_specs=[VM] + [pl.BlockSpec(memory_space=pltpu.HBM)] * RING,
         scratch_shapes=[
             pltpu.VMEM(wave, BF),
             pltpu.VMEM((RING, 2, *wave), BF),
+            pltpu.VMEM((RING, 2, *wave), BF),
             pltpu.SemaphoreType.DMA((RING + 1,)),
+            pltpu.SemaphoreType.DMA((RING,)),
         ],
         compiler_params=pltpu.CompilerParams(vmem_limit_bytes=VMEM_LIMIT),
-    )(where, residual, saved)
+    )(where, in_hbm(residual), in_hbm(saved))
 
 
 def pieces_kernel(wave, pieces):
@@ -504,6 +547,14 @@
     return [arrays[0]] + [turned(arrays[k], k) for k in range(1, RING)]
 
 
+def exchanged_windows(own):
+    relay = turned(own[RING], RING - 1)
+    back = turned(own[3], 3)
+    far = turned(own[FAR], FAR)
+    ahead = turned(own[1], 1)
+    return [own[0], ahead, far, back, turned(relay, RING - 1)]
+
+
 def shards(residual, saved_waves, object_phase, object_amp, prop_phase, offsets):
     depth_at = lax.axis_index("depth")
     chunks = lax.axis_size("probe")
@@ -511,18 +562,20 @@
     own = transmission_windows(where, offsets, object_phase, object_amp)
     tables = (*transform_tables(N), *filters(prop_phase))
     start, *waves = row_parity_first(where, residual, saved_waves)
-    foreign = exchanged(own)
+    foreign = exchanged_windows(own)
     *deep, leaving = run_chain(True, where, start, foreign, (), tables)
     arrived = lax.ppermute(leaving, "depth", [(RING + i, i) for i in range(RING)])
     *entries, ending = run_chain(False, where, arrived, foreign, deep, tables)
     entries = exchanged(entries)
-    probe = lax.all_to_all(column_pieces(ending), "depth", 0, 0, tiled=True)
     grads = None
     for index in (0, 3, 1, 2):
         window = own[(RING - index) % RING]
         grads = visit(
             index, where, offsets, entries[index], window, waves[index], tables, grads
         )
+        if index == 0:
+            ending, grads = lax.optimization_barrier((ending, grads))
+            probe = lax.all_to_all(column_pieces(ending), "depth", 0, 0, tiled=True)
     payload = packed(chunks, grads, probe)
     received = lax.all_to_all(payload, "probe", 0, 0, tiled=True)
     rows, probe_rows = totals(received)

time: 122 us -> 122 us (level)
  local copies, waits for them, and re-layouts: 11.7 us -> 5.48 us
  starting transfers between devices: 16.9 us -> 21.6 us
    unnamed x51 -> x27, local copies, waits for them, and re-layouts: 11 us -> 4.78 us
    ppermute x6 -> x8, starting transfers between devices: 11.3 us -> 16.3 us  [turned(): return lax.ppermute(array, 'depth', route)]
    pallas_call x4, Pallas kernels: 12.2 us -> 14.6 us  [visit(): pl.pallas_call(functools.partial(visit_kernel, index), name=f'visit_{inde...]
    pallas_call x1, Pallas kernels: 5.7 us -> 3.7 us  [transmission_windows(): pl.pallas_call(window_kernel, name='windows', out_shape=[both, both, sing...]
    ppermute x6 -> x8, waiting for transfers between devices: 11.5 us -> 11.4 us  [turned(): return lax.ppermute(array, 'depth', route)]
  transfers between devices with their start and end apart: 8 -> 10, of which waited for: 4 -> 4; matrix products, arithmetic and copies ran while one was open for 4% -> 4% of each run, Pallas kernels for 13% -> 15%
where the time goes in v4:
time: 122 us; the launch traced here: 121 us
  Pallas kernels  33.6 us (28%)
  blocking collectives  28 us (23%)
  waiting for transfers between devices  26.3 us (22%)
  starting transfers between devices  21.6 us (18%)
  local copies, waits for them, and re-layouts  5.48 us (4%)
  other arithmetic  4.98 us (4%)
    all_to_all x1, blocking collectives, shards(): received = lax.all_to_all(payload, 'probe', 0, 0, tiled=True)  28 us
    ppermute x8, starting transfers between devices, turned(): return lax.ppermute(array, 'depth', route)  16.3 us
    ppermute x1, waiting for transfers between devices, shards(): lax.ppermute(leaving, 'depth', [(RING + i, i) for i in range(RING)])  14.9 us
    pallas_call x4, Pallas kernels, visit(): pl.pallas_call(functools.partial(visit_kernel, index), name=f'visit_{inde...  14.6 us
    ppermute x8, waiting for transfers between devices, turned(): return lax.ppermute(array, 'depth', route)  11.4 us
    pallas_call x2, Pallas kernels, run_chain(): pl.pallas_call(functools.partial(chain_kernel, first), name='chain_deep'...  9.26 us
    convert_element_type x1, other arithmetic, build(): return (value * factor).astype(BF)  4.89 us
    unnamed x27, local copies, waits for them, and re-layouts  4.78 us
  transfers between devices with their start and end apart: 10, of which 4 were waited for; matrix products, arithmetic and copies ran while one was open for 4% of the time, Pallas kernels for 15%

profile of v4, /device:TPU:0, one launch (start us, length us, event | category | flops | bytes accessed | tf_op | source)
XLA Modules:
  0.0 120.9 jit_solution(16968976599121368554)
XLA Ops:
  0.6 0.0 copy-start.11
  0.7 0.8 copy.15.offsets
  1.5 0.1 pad_add_fusion.where
  1.5 3.7 %windows.1 = (bf16[2,2,256,256]{3,2,1,0:T(8,128)(2,1)S(1)}, bf16[2,2,256,256]{3,2,1,0:T(8,128)(2,1)S(1)}, bf16[2,256,256]{2,1,0:T(8,128)(2,1)S(1)}, bf16[2,2,256...) custom-call(s32[2]{0:T(128)S(1)} %pad_add_fusion.where, s32[4,2]{1,0:T(4,128)S(1)} %copy.15.offsets, ...), custom_call_target="tpu_custom_call" | custom-call | tf_op jit(solution)/shard_map/windows/pallas_call | solution.py:204
  5.2 0.0 copy-start.5
  5.3 0.0 copy-start.6
  5.3 0.0 copy-start.12
  5.3 0.0 copy-start.2
  5.3 4.2 %collective-permute-start.3 = (bf16[2,256,256]{2,1,0:T(8,128)(2,1)S(1)}, bf16[2,256,256]{2,1,0:T(8,128)(2,1)S(1)}, u32[]{:S(2)}, u32[]{:S(2)}) collective-permute-start(bf16[2,256,256]{2,1,0:T(8,128)(2,1)S(1)} %get-tuple-element.33), channel_id=1, source_target_pairs={{0,48},{16,0},{32,16},{48,32},{64,112},{80,64},{96,80},{112,96},{1... | collective-permute-start | bytes 786440 | tf_op jit(solution)/shard_map/ppermute | solution.py:543
  9.5 0.0 collective-permute-start.1
  9.5 1.3 %collective-permute-start = (bf16[2,2,256,256]{3,2,1,0:T(8,128)(2,1)S(1)}, bf16[2,2,256,256]{3,2,1,0:T(8,128)(2,1)S(1)}, u32[]{:S(2)}, u32[]{:S(2)}) collective-permute-start(bf16[2,2,256,256]{3,2,1,0:T(8,128)(2,1)S(1)} %get-tuple-element.30.window_at), channel_id=1, source_target_pairs={{0,16},{16,32},{32,48},{48,0},{64,80},{80,96},{96,112},{112,64},{1... | collective-permute-start | bytes 1572872 | tf_op jit(solution)/shard_map/ppermute | solution.py:543
  10.8 2.0 %collective-permute-start.2 = (bf16[2,2,256,256]{3,2,1,0:T(8,128)(2,1)S(1)}, bf16[2,2,256,256]{3,2,1,0:T(8,128)(2,1)S(1)}, u32[]{:S(2)}, u32[]{:S(2)}) collective-permute-start(bf16[2,2,256,256]{3,2,1,0:T(8,128)(2,1)S(1)} %get-tuple-element.32.window_at), channel_id=1, source_target_pairs={{0,48},{16,0},{32,16},{48,32},{64,112},{80,64},{96,80},{112,96},{1... | collective-permute-start | bytes 1572872 | tf_op jit(solution)/shard_map/ppermute | solution.py:543
  12.8 0.6 filters.1
  13.4 3.2 %reorder.1 = (bf16[2,256,256]{2,1,0:T(8,128)(2,1)S(1)}, bf16[2,2,256,256]{3,2,1,0:T(8,128)(2,1)S(1)}, bf16[2,2,256,256]{3,2,1,0:T(8,128)(2,1)S(1)}, bf16[2,2,256...) custom-call(s32[2]{0:T(128)S(1)} %pad_add_fusion.where, bf16[4,2,256,256]{3,2,1,0:T(8,128)(2,1)} %residual.1, ...), custom_call_target="tpu_custom_call" | custom-call | tf_op jit(solution)/shard_map/reorder/pallas_call | solution.py:468
  16.6 0.8 copy-done.4
  17.4 0.8 copy-done.9
  18.2 3.6 %collective-permute-done.3 = bf16[2,256,256]{2,1,0:T(8,128)(2,1)S(1)} collective-permute-done((bf16[2,256,256]{2,1,0:T(8,128)(2,1)S(1)}, bf16[2,256,256]{2,1,0:T(8,128)(2,1)S(1)}, u32[]{:S(2)}, u32[]{:S(2)}) %collective-permute-start.3) | collective-permute-done | bytes 262176 | tf_op jit(solution)/shard_map/ppermute | solution.py:543
  21.8 3.7 %collective-permute-start.4 = (bf16[2,256,256]{2,1,0:T(8,128)(2,1)S(1)}, bf16[2,256,256]{2,1,0:T(8,128)(2,1)S(1)}, u32[]{:S(2)}, u32[]{:S(2)}) collective-permute-start(bf16[2,256,256]{2,1,0:T(8,128)(2,1)S(1)} %collective-permute-done.3), channel_id=1, source_target_pairs={{0,48},{16,0},{32,16},{48,32},{64,112},{80,64},{96,80},{112,96},{1... | collective-permute-start | bytes 786440 | tf_op jit(solution)/shard_map/ppermute | solution.py:543
  25.5 4.9 %fusion.11 = (bf16[2,256,256]{2,1,0:T(8,128)(2,1)S(1)}, bf16[2,256,256]{2,1,0:T(8,128)(2,1)S(1)}, bf16[2,256,256]{2,1,0:T(8,128)(2,1)S(1)}) fusion(f32[256]{0:T(256)S(1)} %get-tuple-element.62, s32[256]{0:T(256)S(1)} %get-tuple-element.59, s32[256]{0:T(256)S(1)} %get-tuple-element.60, pred[256]{0:T(512)(128)(4,1)S(1)} %get-tuple-element.57, ...), kind=kLoop, calls=%fused_computation.24 | loop fusion | flops 6160384 | bytes 791040 | tf_op jit(solution)/shard_map/convert_element_type | solution.py:50
  30.4 0.0 collective-permute-done.1.rest_2_
  30.5 7.1 %collective-permute-done.4.rest_4_ = bf16[2,256,256]{2,1,0:T(8,128)(2,1)S(1)} collective-permute-done((bf16[2,256,256]{2,1,0:T(8,128)(2,1)S(1)}, bf16[2,256,256]{2,1,0:T(8,128)(2,1)S(1)}, u32[]{:S(2)}, u32[]{:S(2)}) %collective-permute-start.4) | collective-permute-done | bytes 262176 | tf_op jit(solution)/shard_map/ppermute | solution.py:543
  37.5 0.0 collective-permute-done.rest_1_
  37.5 0.0 collective-permute-done.2.rest_3_
  37.5 0.7 chain_deep.1
  38.3 1.3 %collective-permute-start.5 = (bf16[2,256,256]{2,1,0:T(8,128)(2,1)S(1)}, bf16[2,256,256]{2,1,0:T(8,128)(2,1)S(1)}, u32[]{:S(2)}, u32[]{:S(2)}) collective-permute-start(bf16[2,256,256]{2,1,0:T(8,128)(2,1)S(1)} %get-tuple-element.36), channel_id=1, source_target_pairs={{64,0},{80,16},{96,32},{112,48},{65,1},{81,17},{97,33},{113,49},{6... | collective-permute-start | bytes 786440 | tf_op jit(solution)/shard_map/ppermute | solution.py:567
  39.6 14.9 %collective-permute-done.5.start = bf16[2,256,256]{2,1,0:T(8,128)(2,1)S(1)} collective-permute-done((bf16[2,256,256]{2,1,0:T(8,128)(2,1)S(1)}, bf16[2,256,256]{2,1,0:T(8,128)(2,1)S(1)}, u32[]{:S(2)}, u32[]{:S(2)}) %collective-permute-start.5) | collective-permute-done | bytes 262176 | tf_op jit(solution)/shard_map/ppermute | solution.py:567
  54.5 8.6 %chain_top.1 = (bf16[2,256,256]{2,1,0:T(8,128)(2,1)S(1)}, bf16[2,256,256]{2,1,0:T(8,128)(2,1)}, bf16[2,256,256]{2,1,0:T(8,128)(2,1)}, bf16[2,256,256]{2,1,0:T(8,128)(2,1)}, bf16[2,256,256]{2,1,0:T(8,128)(2,1)S(1)}) custom-call(s32[2]{0:T(128)S(1)} %pad_add_fusion.where, bf16[2,256,256]{2,1,0:T(8,128)(2,1)S(1)} %collective-permute-done.5.start, ...), custom_call_target="tpu_custom_call" | custom-call | tf_op jit(solution)/shard_map/chain_top/pallas_call | solution.py:307
  63.1 0.7 copy-done.10
  63.8 3.7 %collective-permute-start.8 = (bf16[2,256,256]{2,1,0:T(8,128)(2,1)}, bf16[2,256,256]{2,1,0:T(8,128)(2,1)}, u32[]{:S(2)}, u32[]{:S(2)}) collective-permute-start(bf16[2,256,256]{2,1,0:T(8,128)(2,1)} %get-tuple-element.45), channel_id=1, source_target_pairs={{0,48},{16,0},{32,16},{48,32},{64,112},{80,64},{96,80},{112,96},{1... | collective-permute-start | bytes 786440 | tf_op jit(solution)/shard_map/ppermute | solution.py:543
  67.5 0.0 collective-permute-start.7
  67.5 1.5 %collective-permute-start.6 = (bf16[2,256,256]{2,1,0:T(8,128)(2,1)}, bf16[2,256,256]{2,1,0:T(8,128)(2,1)}, u32[]{:S(2)}, u32[]{:S(2)}) collective-permute-start(bf16[2,256,256]{2,1,0:T(8,128)(2,1)} %get-tuple-element.41), channel_id=1, source_target_pairs={{0,32},{16,48},{32,0},{48,16},{64,96},{80,112},{96,64},{112,80},{1... | collective-permute-start | bytes 786440 | tf_op jit(solution)/shard_map/ppermute | solution.py:543
  68.9 3.7 %visit_0.1.rest_5_ = f32[2,2,3,384,128]{4,3,2,1,0:T(8,128)S(1)} custom-call(s32[2]{0:T(128)S(1)} %pad_add_fusion.where, s32[4,2]{1,0:T(4,128)S(1)} %copy.15.offsets, bf16[2,256,256]{2,1,0:T(8,128)(2,1)} %copy-done.10, bf16[2,2,256,256]{3,2,1,0:T(8,128)(2,1)} %copy-done.2, bf16[2,2,256,256]{3,2,1,0:T(8,128)(2,1)} %copy-done.4, ...), custom_call_target="tpu_custom_call" | custom-call | tf_op jit(solution)/shard_map/visit_0/pallas_call | solution.py:383
  72.6 0.3 pieces.1
  72.9 0.7 copy-done.3
  73.6 4.0 %all-to-all-start = ((bf16[8,128,128]{2,1,0:T(8,128)(2,1)}), bf16[8,128,128]{2,1,0:T(8,128)(2,1)}, u32[]{:S(2)}, u32[]{:S(2)}) async-start(bf16[8,128,128]{2,1,0:T(8,128)(2,1)} %copy-done.3), calls=%async_computation | async-start | bytes 524288 | tf_op jit(solution)/shard_map/all_to_all | solution.py:578
  77.6 0.6 collective-permute-done.8.entry_at
  78.3 0.9 copy-done.1
  79.2 3.7 %visit_3.1.rest_5_ = f32[2,2,3,384,128]{4,3,2,1,0:T(8,128)S(1)} custom-call(s32[2]{0:T(128)S(1)} %pad_add_fusion.where, s32[4,2]{1,0:T(4,128)S(1)} %copy.15.offsets, bf16[2,256,256]{2,1,0:T(8,128)(2,1)} %collective-permute-done.8.entry_at, bf16[2,2,256,256]{3,2,1,0:T(8,128)(2,1)} %copy-done.6, ...), custom_call_target="tpu_custom_call", output_to_operand_aliasing={{}: (10, {})} | custom-call | tf_op jit(solution)/shard_map/visit_3/pallas_call | solution.py:383
  82.9 0.0 collective-permute-done.7.entry_at
  82.9 3.6 %visit_1.1.rest_5_ = f32[2,2,3,384,128]{4,3,2,1,0:T(8,128)S(1)} custom-call(s32[2]{0:T(128)S(1)} %pad_add_fusion.where, s32[4,2]{1,0:T(4,128)S(1)} %copy.15.offsets, bf16[2,256,256]{2,1,0:T(8,128)(2,1)} %collective-permute-done.7.entry_at, bf16[2,2,256,256]{3,2,1,0:T(8,128)(2,1)} %copy-done.5, ...), custom_call_target="tpu_custom_call", output_to_operand_aliasing={{}: (10, {})} | custom-call | tf_op jit(solution)/shard_map/visit_1/pallas_call | solution.py:383
  86.5 0.0 collective-permute-done.6.entry_at
  86.6 3.6 %visit_2.1.grads = f32[2,2,3,384,128]{4,3,2,1,0:T(8,128)S(1)} custom-call(s32[2]{0:T(128)S(1)} %pad_add_fusion.where, s32[4,2]{1,0:T(4,128)S(1)} %copy.15.offsets, bf16[2,256,256]{2,1,0:T(8,128)(2,1)} %collective-permute-done.6.entry_at, bf16[2,256,256]{2,1,0:T(8,128)(2,1)} %copy-done.12, ...), custom_call_target="tpu_custom_call", output_to_operand_aliasing={{}: (10, {})} | custom-call | tf_op jit(solution)/shard_map/visit_2/pallas_call | solution.py:383
  90.2 0.0 all-to-all-done.probe
  90.2 1.1 pack.1
  91.4 28.0 %all_to_all.10.received = bf16[16,112,384]{2,1,0:T(8,128)(2,1)S(1)} all-to-all(bf16[16,112,384]{2,1,0:T(8,128)(2,1)S(1)} %pack.1), channel_id=1, replica_groups=mesh['depth'=8,'probe'=16] {'probe'}, dimensions={0} | all-to-all | bytes 2752512 | tf_op jit(solution)/shard_map/all_to_all | solution.py:580
  119.4 0.8 totals.1
  120.2 0.1 reshape.14
  120.3 0.6 copy.16
  (19 shorter events, 0.0 us)
Async XLA Ops:
  0.6 12.1 %copy-start.11 = (f32[256,256]{1,0:T(8,128)S(1)}, f32[256,256]{1,0:T(8,128)}, u32[]{:S(2)}) copy-start(f32[256,256]{1,0:T(8,128)} %phase.1) | copy-start | bytes 786436
  5.2 25.2 %copy-start.5 = (bf16[2,2,256,256]{3,2,1,0:T(8,128)(2,1)}, bf16[2,2,256,256]{3,2,1,0:T(8,128)(2,1)S(1)}, u32[]{:S(2)}) copy-start(bf16[2,2,256,256]{3,2,1,0:T(8,128)(2,1)S(1)} %get-tuple-element.32.window_at) | copy-start | bytes 1572868
  5.3 25.2 %copy-start.6 = (bf16[2,2,256,256]{3,2,1,0:T(8,128)(2,1)}, bf16[2,2,256,256]{3,2,1,0:T(8,128)(2,1)S(1)}, u32[]{:S(2)}) copy-start(bf16[2,2,256,256]{3,2,1,0:T(8,128)(2,1)S(1)} %get-tuple-element.30.window_at) | copy-start | bytes 1572868
  5.3 25.2 %copy-start.12 = (bf16[2,256,256]{2,1,0:T(8,128)(2,1)}, bf16[2,256,256]{2,1,0:T(8,128)(2,1)S(1)}, u32[]{:S(2)}) copy-start(bf16[2,256,256]{2,1,0:T(8,128)(2,1)S(1)} %get-tuple-element.31.window_at) | copy-start | bytes 786436
  5.3 49.2 %copy-start.2 = (bf16[2,2,256,256]{3,2,1,0:T(8,128)(2,1)}, bf16[2,2,256,256]{3,2,1,0:T(8,128)(2,1)S(1)}, u32[]{:S(2)}) copy-start(bf16[2,2,256,256]{3,2,1,0:T(8,128)(2,1)S(1)} %get-tuple-element.29.rest_0_.window_at) | copy-start | bytes 1572868
  5.3 16.5 %collective-permute-start.3 = (bf16[2,256,256]{2,1,0:T(8,128)(2,1)S(1)}, bf16[2,256,256]{2,1,0:T(8,128)(2,1)S(1)}, u32[]{:S(2)}, u32[]{:S(2)}) collective-permute-start(bf16[2,256,256]{2,1,0:T(8,128)(2,1)S(1)} %get-tuple-element.33), channel_id=1, source_target_pairs={{0,48},{16,0},{32,16},{48,32},{64,112},{80,64},{96,80},{112,96},{1... | collective-permute-start | bytes 786440 | tf_op jit(solution)/shard_map/ppermute | solution.py:543
  9.5 20.9 %collective-permute-start.1 = (bf16[2,256,256]{2,1,0:T(8,128)(2,1)S(1)}, bf16[2,256,256]{2,1,0:T(8,128)(2,1)S(1)}, u32[]{:S(2)}, u32[]{:S(2)}) collective-permute-start(bf16[2,256,256]{2,1,0:T(8,128)(2,1)S(1)} %get-tuple-element.31.window_at), channel_id=1, source_target_pairs={{0,32},{16,48},{32,0},{48,16},{64,96},{80,112},{96,64},{112,80},{1... | collective-permute-start | bytes 786440 | tf_op jit(solution)/shard_map/ppermute | solution.py:543
  9.5 28.0 %collective-permute-start = (bf16[2,2,256,256]{3,2,1,0:T(8,128)(2,1)S(1)}, bf16[2,2,256,256]{3,2,1,0:T(8,128)(2,1)S(1)}, u32[]{:S(2)}, u32[]{:S(2)}) collective-permute-start(bf16[2,2,256,256]{3,2,1,0:T(8,128)(2,1)S(1)} %get-tuple-element.30.window_at), channel_id=1, source_target_pairs={{0,16},{16,32},{32,48},{48,0},{64,80},{80,96},{96,112},{112,64},{1... | collective-permute-start | bytes 1572872 | tf_op jit(solution)/shard_map/ppermute | solution.py:543
  10.8 26.8 %collective-permute-start.2 = (bf16[2,2,256,256]{3,2,1,0:T(8,128)(2,1)S(1)}, bf16[2,2,256,256]{3,2,1,0:T(8,128)(2,1)S(1)}, u32[]{:S(2)}, u32[]{:S(2)}) collective-permute-start(bf16[2,2,256,256]{3,2,1,0:T(8,128)(2,1)S(1)} %get-tuple-element.32.window_at), channel_id=1, source_target_pairs={{0,48},{16,0},{32,16},{48,32},{64,112},{80,64},{96,80},{112,96},{1... | collective-permute-start | bytes 1572872 | tf_op jit(solution)/shard_map/ppermute | solution.py:543
  16.6 0.8 copy-start.4
  17.4 0.8 copy-start.9
  18.2 19.4 %copy-start.7 = (bf16[2,2,256,256]{3,2,1,0:T(8,128)(2,1)}, bf16[2,2,256,256]{3,2,1,0:T(8,128)(2,1)S(1)}, u32[]{:S(2)}) copy-start(bf16[2,2,256,256]{3,2,1,0:T(8,128)(2,1)S(1)} %get-tuple-element.42.psi_at) | copy-start | bytes 1572868
  18.2 20.1 %copy-start.8 = (bf16[2,2,256,256]{3,2,1,0:T(8,128)(2,1)}, bf16[2,2,256,256]{3,2,1,0:T(8,128)(2,1)S(1)}, u32[]{:S(2)}) copy-start(bf16[2,2,256,256]{3,2,1,0:T(8,128)(2,1)S(1)} %get-tuple-element.44.psi_at) | copy-start | bytes 1572868
  21.8 15.7 %collective-permute-start.4 = (bf16[2,256,256]{2,1,0:T(8,128)(2,1)S(1)}, bf16[2,256,256]{2,1,0:T(8,128)(2,1)S(1)}, u32[]{:S(2)}, u32[]{:S(2)}) collective-permute-start(bf16[2,256,256]{2,1,0:T(8,128)(2,1)S(1)} %collective-permute-done.3), channel_id=1, source_target_pairs={{0,48},{16,0},{32,16},{48,32},{64,112},{80,64},{96,80},{112,96},{1... | collective-permute-start | bytes 786440 | tf_op jit(solution)/shard_map/ppermute | solution.py:543
  30.4 38.5 %copy-start = (bf16[2,256,256]{2,1,0:T(8,128)(2,1)}, bf16[2,256,256]{2,1,0:T(8,128)(2,1)S(1)}, u32[]{:S(2)}) copy-start(bf16[2,256,256]{2,1,0:T(8,128)(2,1)S(1)} %get-tuple-element.56.rest_7_.rest_11_.rest_2_) | copy-start | bytes 786436
  38.3 16.2 %collective-permute-start.5 = (bf16[2,256,256]{2,1,0:T(8,128)(2,1)S(1)}, bf16[2,256,256]{2,1,0:T(8,128)(2,1)S(1)}, u32[]{:S(2)}, u32[]{:S(2)}) collective-permute-start(bf16[2,256,256]{2,1,0:T(8,128)(2,1)S(1)} %get-tuple-element.36), channel_id=1, source_target_pairs={{64,0},{80,16},{96,32},{112,48},{65,1},{81,17},{97,33},{113,49},{6... | collective-permute-start | bytes 786440 | tf_op jit(solution)/shard_map/ppermute | solution.py:567
  63.1 0.7 copy-start.10
  63.8 14.5 %collective-permute-start.8 = (bf16[2,256,256]{2,1,0:T(8,128)(2,1)}, bf16[2,256,256]{2,1,0:T(8,128)(2,1)}, u32[]{:S(2)}, u32[]{:S(2)}) collective-permute-start(bf16[2,256,256]{2,1,0:T(8,128)(2,1)} %get-tuple-element.45), channel_id=1, source_target_pairs={{0,48},{16,0},{32,16},{48,32},{64,112},{80,64},{96,80},{112,96},{1... | collective-permute-start | bytes 786440 | tf_op jit(solution)/shard_map/ppermute | solution.py:543
  67.5 15.4 %collective-permute-start.7 = (bf16[2,256,256]{2,1,0:T(8,128)(2,1)}, bf16[2,256,256]{2,1,0:T(8,128)(2,1)}, u32[]{:S(2)}, u32[]{:S(2)}) collective-permute-start(bf16[2,256,256]{2,1,0:T(8,128)(2,1)} %get-tuple-element.43), channel_id=1, source_target_pairs={{0,16},{16,32},{32,48},{48,0},{64,80},{80,96},{96,112},{112,64},{1... | collective-permute-start | bytes 786440 | tf_op jit(solution)/shard_map/ppermute | solution.py:543
  67.5 19.1 %collective-permute-start.6 = (bf16[2,256,256]{2,1,0:T(8,128)(2,1)}, bf16[2,256,256]{2,1,0:T(8,128)(2,1)}, u32[]{:S(2)}, u32[]{:S(2)}) collective-permute-start(bf16[2,256,256]{2,1,0:T(8,128)(2,1)} %get-tuple-element.41), channel_id=1, source_target_pairs={{0,32},{16,48},{32,0},{48,16},{64,96},{80,112},{96,64},{112,80},{1... | collective-permute-start | bytes 786440 | tf_op jit(solution)/shard_map/ppermute | solution.py:543
  72.9 0.7 copy-start.3
  73.6 16.6 %all-to-all-start = ((bf16[8,128,128]{2,1,0:T(8,128)(2,1)}), bf16[8,128,128]{2,1,0:T(8,128)(2,1)}, u32[]{:S(2)}, u32[]{:S(2)}) async-start(bf16[8,128,128]{2,1,0:T(8,128)(2,1)} %copy-done.3), calls=%async_computation | async-start | bytes 524288 | tf_op jit(solution)/shard_map/all_to_all | solution.py:578
  78.3 0.9 copy-start.1

commit v5 on v4

--- a/solution.py
+++ b/solution.py
@@ -11,11 +11,12 @@
 BF = jnp.bfloat16
 F32 = jnp.float32
 RING = 4
-FAR = 2
 DEPTH = 8
 N = 256
 HALF = 128
 PATCH = 384
+EACH = PATCH // 16
+CHUNK = 4 * EACH + 16
 ANY = pl.BlockSpec(memory_space=pl.ANY)
 VM = pl.BlockSpec(memory_space=pltpu.VMEM)
 SM = pl.BlockSpec(memory_space=pltpu.SMEM)
@@ -150,7 +151,7 @@
 
 
 def window_kernel(where, offsets, phase_all, amp_all, *rest):
-    outs, (field, phase, amp, sems) = rest[: RING + 1], rest[RING + 1 :]
+    outs, (field, phase, amp, sems) = rest[:RING], rest[RING:]
     rank = where[0]
 
     def loads(layer, block):
@@ -188,10 +189,7 @@
                     turned = [
                         pltpu.roll(field[layer, part, col, rows, :], turn, 1) for col in range(3)
                     ]
-                    if distance == FAR:
-                        target = outs[distance if layer else RING]
-                    else:
-                        target = outs[distance].at[layer]
+                    target = outs[distance].at[layer]
                     for col in (0, 1):
                         target[parity, half(part), half(col)] = jnp.where(
                             inside, turned[col], turned[col + 1]
@@ -199,14 +197,13 @@
 
 
 def transmission_windows(where, offsets, phase, amp):
-    both = jax.ShapeDtypeStruct((2, 2, N, N), BF)
-    single = jax.ShapeDtypeStruct((2, N, N), BF)
+    shape = jax.ShapeDtypeStruct((2, 2, N, N), BF)
     return pl.pallas_call(
         window_kernel,
         name="windows",
-        out_shape=[both, both, single, both, single],
+        out_shape=[shape] * RING,
         in_specs=[SM, SM, ANY, ANY],
-        out_specs=[VM] * (RING + 1),
+        out_specs=[VM] * RING,
         scratch_shapes=[
             pltpu.VMEM((2, 2, 3, PATCH, HALF), F32),
             pltpu.VMEM((2, PATCH, PATCH), F32),
@@ -218,9 +215,9 @@
 
 
 def chain_kernel(first, where, start, *rest):
-    windows = rest[: RING + 1]
-    earlier = () if first else rest[RING + 1 : 2 * RING + 1]
-    rest = rest[RING + 1 + len(earlier) :]
+    windows = rest[:RING]
+    earlier = () if first else rest[RING : 2 * RING]
+    rest = rest[RING + len(earlier) :]
     tables = rest[:5]
     count = RING + 1
     outs = rest[5 : 5 + count]
@@ -230,10 +227,7 @@
 
     def window_load(distance, layer):
         slot = (rank + RING - distance) % RING
-        if distance == FAR:
-            source = windows[distance if layer else RING]
-        else:
-            source = windows[distance].at[layer]
+        source = windows[distance].at[layer]
         return pltpu.make_async_copy(source, trans.at[slot, layer], in_sems.at[slot, layer])
 
     def store(k):
@@ -308,7 +302,7 @@
         functools.partial(chain_kernel, first),
         name="chain_deep" if first else "chain_top",
         out_shape=[wave] * count,
-        in_specs=[SM, ANY] + [ANY] * (RING + 1) + [ANY] * len(earlier) + [VM] * 5,
+        in_specs=[SM, ANY] + [ANY] * RING + [ANY] * len(earlier) + [VM] * 5,
         out_specs=[ANY] * count,
         scratch_shapes=[
             pltpu.VMEM((RING, 2, 2, N, N), BF),
@@ -327,7 +321,7 @@
     grads, entry, window, psi, middle, mixed, filtered, second, sems = rest[-9:]
     loads = [
         pltpu.make_async_copy(entry_at, entry, sems.at[0]),
-        pltpu.make_async_copy(window_at if index == FAR else window_at.at[1], window, sems.at[1]),
+        pltpu.make_async_copy(window_at.at[1], window, sems.at[1]),
         pltpu.make_async_copy(psi_at, psi, sems.at[2]),
     ]
     for copy in loads:
@@ -396,37 +390,111 @@
         ],
         input_output_aliases={10: 0} if earlier else {},
         compiler_params=pltpu.CompilerParams(vmem_limit_bytes=VMEM_LIMIT),
-    )(where, offsets, *(in_hbm(array) for array in (entry, window, psi)), *tables, *earlier)
-
-
-def pack_kernel(grads, probe, payload, summed):
-    chunks = payload.shape[0]
-    rows_each = PATCH // chunks
+    )(where, offsets, entry, in_hbm(window), in_hbm(psi), *tables, *earlier)
+
+
+def pack_kernel(where, grads, probe, keep, send, summed):
+    core, y_at = where[2], where[3]
     total = jnp.zeros((HALF, HALF), F32)
     for source in range(DEPTH):
         total = total + probe[source].astype(F32)
     summed[...] = total
-    for chunk in range(chunks):
-        rows = slice(chunk * rows_each, (chunk + 1) * rows_each)
-        for col in range(3):
-            pieces = [grads[layer, part, col, rows, :] for layer in (0, 1) for part in (0, 1)]
-            own = slice(8 * chunk, 8 * chunk + 8)
-            pieces.append(summed[own, :] if col == 0 else jnp.zeros((8, HALF), F32))
-            pieces.append(jnp.zeros((8, HALF), F32))
-            payload[chunk, :, half(col)] = jnp.concatenate(pieces, 0).astype(BF)
-
-
-def packed(chunks, grads, probe):
-    rows = 4 * (PATCH // chunks) + 16
+    for distance in range(RING):
+        for x_at in (0, 1):
+            for out, core_at in ((keep, core), (send, 1 - core)):
+                chunk = (x_at * RING + (y_at + distance) % RING) * 2 + core_at
+                rows = pl.ds(pl.multiple_of(chunk * EACH, 8), EACH)
+                own = pl.ds(pl.multiple_of(chunk * 8, 8), 8)
+                for col in range(3):
+                    pieces = [
+                        grads[layer, part, col, rows, :] for layer in (0, 1) for part in (0, 1)
+                    ]
+                    pieces.append(summed[own, :] if col == 0 else jnp.zeros((8, HALF), F32))
+                    pieces.append(jnp.zeros((8, HALF), F32))
+                    out[distance, x_at, :, half(col)] = jnp.concatenate(pieces, 0).astype(BF)
+
+
+def packed(where, grads, probe):
+    shape = jax.ShapeDtypeStruct((RING, 2, CHUNK, PATCH), BF)
     return pl.pallas_call(
         pack_kernel,
         name="pack",
-        out_shape=jax.ShapeDtypeStruct((chunks, rows, PATCH), BF),
+        out_shape=[shape, shape],
+        in_specs=[SM, VM, VM],
+        out_specs=[VM, VM],
+        scratch_shapes=[pltpu.VMEM((HALF, HALF), F32)],
+        compiler_params=pltpu.CompilerParams(vmem_limit_bytes=VMEM_LIMIT),
+    )(where, grads, probe)
+
+
+def core_sum_kernel(keep, arrived, *outs):
+    for distance in range(RING):
+        for x_at in (0, 1):
+            total = keep[distance, x_at].astype(F32) + arrived[distance, x_at].astype(F32)
+            outs[distance][x_at] = total.astype(BF)
+
+
+def core_sum(keep, arrived):
+    return pl.pallas_call(
+        core_sum_kernel,
+        name="core_sum",
+        out_shape=[jax.ShapeDtypeStruct((2, CHUNK, PATCH), BF)] * RING,
         in_specs=[VM, VM],
-        out_specs=VM,
-        scratch_shapes=[pltpu.VMEM((HALF, HALF), F32)],
-        compiler_params=pltpu.CompilerParams(vmem_limit_bytes=VMEM_LIMIT),
-    )(grads, probe)
+        out_specs=[VM] * RING,
+        compiler_params=pltpu.CompilerParams(vmem_limit_bytes=VMEM_LIMIT),
+    )(keep, arrived)
+
+
+def ring_sum_kernel(where, *rest):
+    parts, (keep, send) = rest[:RING], rest[RING:]
+    x_at = where[4]
+    for out, which in ((keep, x_at), (send, 1 - x_at)):
+        total = parts[0][which].astype(F32)
+        for part in parts[1:]:
+            total = total + part[which].astype(F32)
+        out[...] = total.astype(out.dtype)
+
+
+def ring_sum(where, parts):
+    return pl.pallas_call(
+        ring_sum_kernel,
+        name="ring_sum",
+        out_shape=[
+            jax.ShapeDtypeStruct((CHUNK, PATCH), F32),
+            jax.ShapeDtypeStruct((CHUNK, PATCH), BF),
+        ],
+        in_specs=[SM] + [VM] * RING,
+        out_specs=[VM, VM],
+        compiler_params=pltpu.CompilerParams(vmem_limit_bytes=VMEM_LIMIT),
+    )(where, *parts)
+
+
+def last_sum_kernel(keep, arrived, rows_out, probe_out):
+    total = keep[...] + arrived[...].astype(F32)
+    rows_out[...] = total[: 4 * EACH]
+    probe_out[...] = total[4 * EACH : 4 * EACH + 8, :HALF]
+
+
+def last_sum(keep, arrived):
+    return pl.pallas_call(
+        last_sum_kernel,
+        name="last_sum",
+        out_shape=[
+            jax.ShapeDtypeStruct((4 * EACH, PATCH), F32),
+            jax.ShapeDtypeStruct((8, HALF), F32),
+        ],
+        compiler_params=pltpu.CompilerParams(vmem_limit_bytes=VMEM_LIMIT),
+    )(keep, arrived)
+
+
+def moved(array, dx, dy, dc):
+    route = [
+        (8 * x + 2 * y + c, 8 * (x ^ dx) + 2 * ((y + dy) % RING) + (c ^ dc))
+        for x in range(2)
+        for y in range(RING)
+        for c in range(2)
+    ]
+    return lax.ppermute(array, "probe", route)
 
 
 def order_kernel(where, residual, saved, start, *rest):
@@ -508,32 +576,6 @@
     )(wave)
 
 
-def total_kernel(received, rows_out, probe_out):
-    chunks, rows, _ = received.shape
-    whole = rows - 16
-    for at in range(0, rows, 16):
-        value = received[0, at : at + 16, :].astype(F32)
-        for chunk in range(1, chunks):
-            value = value + received[chunk, at : at + 16, :].astype(F32)
-        if at < whole:
-            rows_out[at : at + 16, :] = value
-        else:
-            probe_out[...] = value[:8, :HALF]
-
-
-def totals(received):
-    _, rows, _ = received.shape
-    return pl.pallas_call(
-        total_kernel,
-        name="totals",
-        out_shape=[
-            jax.ShapeDtypeStruct((rows - 16, PATCH), F32),
-            jax.ShapeDtypeStruct((8, HALF), F32),
-        ],
-        compiler_params=pltpu.CompilerParams(vmem_limit_bytes=VMEM_LIMIT),
-    )(received)
-
-
 def turned(array, distance):
     route = [
         (RING * ring + i, RING * ring + (i + distance) % RING)
@@ -547,22 +589,16 @@
     return [arrays[0]] + [turned(arrays[k], k) for k in range(1, RING)]
 
 
-def exchanged_windows(own):
-    relay = turned(own[RING], RING - 1)
-    back = turned(own[3], 3)
-    far = turned(own[FAR], FAR)
-    ahead = turned(own[1], 1)
-    return [own[0], ahead, far, back, turned(relay, RING - 1)]
-
-
 def shards(residual, saved_waves, object_phase, object_amp, prop_phase, offsets):
     depth_at = lax.axis_index("depth")
-    chunks = lax.axis_size("probe")
-    where = jnp.stack([depth_at % RING, depth_at // RING]).astype(jnp.int32)
+    probe_at = lax.axis_index("probe")
+    where = jnp.stack(
+        [depth_at % RING, depth_at // RING, probe_at % 2, probe_at // 2 % RING, probe_at // 8]
+    ).astype(jnp.int32)
     own = transmission_windows(where, offsets, object_phase, object_amp)
     tables = (*transform_tables(N), *filters(prop_phase))
     start, *waves = row_parity_first(where, residual, saved_waves)
-    foreign = exchanged_windows(own)
+    foreign = exchanged(own)
     *deep, leaving = run_chain(True, where, start, foreign, (), tables)
     arrived = lax.ppermute(leaving, "depth", [(RING + i, i) for i in range(RING)])
     *entries, ending = run_chain(False, where, arrived, foreign, deep, tables)
@@ -576,10 +612,12 @@
         if index == 0:
             ending, grads = lax.optimization_barrier((ending, grads))
             probe = lax.all_to_all(column_pieces(ending), "depth", 0, 0, tiled=True)
-    payload = packed(chunks, grads, probe)
-    received = lax.all_to_all(payload, "probe", 0, 0, tiled=True)
-    rows, probe_rows = totals(received)
-    object_grad = rows.reshape(2, 2, PATCH // chunks, PATCH)
+    keep, send = packed(where, grads, probe)
+    parts = list(core_sum(keep, moved(send, 0, 0, 1)))
+    parts = parts[:1] + [moved(parts[k], 0, k, 0) for k in range(1, RING)]
+    keep, send = ring_sum(where, parts)
+    rows, probe_rows = last_sum(keep, moved(send, 1, 0, 0))
+    object_grad = rows.reshape(2, 2, EACH, PATCH)
     probe_grad = probe_rows.reshape(8, 2, 2, N // DEPTH).transpose(2, 0, 1, 3)
     return (object_grad, probe_grad.reshape(2, 16, N // DEPTH))
 

time: 122 us -> 112 us (0.918)
  blocking collectives: 28 us -> 0 us
  waiting for transfers between devices: 26.3 us -> 38.9 us
  starting transfers between devices: 21.6 us -> 26.7 us
    all_to_all x1 -> x0, blocking collectives: 28 us -> none  [shards(): received = lax.all_to_all(payload, 'probe', 0, 0, tiled=True)]
    ppermute x0 -> x5, waiting for transfers between devices: none -> 11.1 us  [moved(): return lax.ppermute(array, 'probe', route)]
    ppermute x0 -> x5, starting transfers between devices: none -> 9.87 us  [moved(): return lax.ppermute(array, 'probe', route)]
    ppermute x8 -> x6, starting transfers between devices: 16.3 us -> 11.5 us  [turned(): return lax.ppermute(array, 'depth', route)]
    ppermute x8 -> x6, waiting for transfers between devices: 11.4 us -> 12.9 us  [turned(): return lax.ppermute(array, 'depth', route)]
    pallas_call x3 -> x5, Pallas kernels: 5.65 us -> 6.36 us  [the longest x1 3.69 us: transmission_windows(): pl.pallas_call(window_kernel, name='windows', out_shape=[shape] * RING, i...]
    unnamed x27 -> x25, local copies, waits for them, and re-layouts: 4.78 us -> 4.85 us
  transfers between devices with their start and end apart: 10 -> 13, of which waited for: 4 -> 7; matrix products, arithmetic and copies ran while one was open for 4% -> 4% of each run, Pallas kernels for 15% -> 16%
where the time goes in v5:
time: 112 us; the launch traced here: 111 us
  waiting for transfers between devices  38.9 us (35%)
  Pallas kernels  33.8 us (30%)
  starting transfers between devices  26.7 us (24%)
  local copies, waits for them, and re-layouts  5.62 us (5%)
  other arithmetic  4.93 us (4%)
    ppermute x1, waiting for transfers between devices, shards(): lax.ppermute(leaving, 'depth', [(RING + i, i) for i in range(RING)])  14.9 us
    pallas_call x4, Pallas kernels, visit(): pl.pallas_call(functools.partial(visit_kernel, index), name=f'visit_{inde...  14.1 us
    ppermute x6, waiting for transfers between devices, turned(): return lax.ppermute(array, 'depth', route)  12.9 us
    ppermute x6, starting transfers between devices, turned(): return lax.ppermute(array, 'depth', route)  11.5 us
    ppermute x5, waiting for transfers between devices, moved(): return lax.ppermute(array, 'probe', route)  11.1 us
    ppermute x5, starting transfers between devices, moved(): return lax.ppermute(array, 'probe', route)  9.87 us
    pallas_call x2, Pallas kernels, run_chain(): pl.pallas_call(functools.partial(chain_kernel, first), name='chain_deep'...  9.26 us
    convert_element_type x1, other arithmetic, build(): return (value * factor).astype(BF)  4.92 us
  transfers between devices with their start and end apart: 13, of which 7 were waited for; matrix products, arithmetic and copies ran while one was open for 4% of the time, Pallas kernels for 16%

profile of v5, /device:TPU:0, one launch (start us, length us, event | category | flops | bytes accessed | tf_op | source)
XLA Modules:
  0.0 110.9 jit_solution(12255137347718412611)
XLA Ops:
  0.7 0.8 copy.15.offsets
  1.5 0.1 stack.23.where
  1.6 3.7 %windows.1 = (bf16[2,2,256,256]{3,2,1,0:T(8,128)(2,1)S(1)}, bf16[2,2,256,256]{3,2,1,0:T(8,128)(2,1)S(1)}, bf16[2,2,256,256]{3,2,1,0:T(8,128)(2,1)S(1)}, bf16[2,2,256,256]{3,2,1,0:T(8,128)(2,1)S(1)}) custom-call(s32[5]{0:T(128)S(1)} %stack.23.where, s32[4,2]{1,0:T(4,128)S(1)} %copy.15.offsets, f32[2,384,384]{2,1,0:T(8,128)} %phase_all.1, f32[2,384,384]{2,1,0:T(8,128)} %amp_all.1), custom_call_target="tpu_custom_call" | custom-call | tf_op jit(solution)/shard_map/windows/pallas_call | solution.py:201
  5.3 2.1 %collective-permute-start = (bf16[2,2,256,256]{3,2,1,0:T(8,128)(2,1)S(1)}, bf16[2,2,256,256]{3,2,1,0:T(8,128)(2,1)S(1)}, u32[]{:S(2)}, u32[]{:S(2)}) collective-permute-start(bf16[2,2,256,256]{3,2,1,0:T(8,128)(2,1)S(1)} %get-tuple-element.37.window_at), channel_id=1, source_target_pairs={{0,16},{16,32},{32,48},{48,0},{64,80},{80,96},{96,112},{112,64},{1... | collective-permute-start | bytes 1572872 | tf_op jit(solution)/shard_map/ppermute | solution.py:585
  7.4 3.6 %collective-permute-start.1 = (bf16[2,2,256,256]{3,2,1,0:T(8,128)(2,1)S(1)}, bf16[2,2,256,256]{3,2,1,0:T(8,128)(2,1)S(1)}, u32[]{:S(2)}, u32[]{:S(2)}) collective-permute-start(bf16[2,2,256,256]{3,2,1,0:T(8,128)(2,1)S(1)} %get-tuple-element.38.window_at), channel_id=1, source_target_pairs={{0,32},{16,48},{32,0},{48,16},{64,96},{80,112},{96,64},{112,80},{1... | collective-permute-start | bytes 1572872 | tf_op jit(solution)/shard_map/ppermute | solution.py:585
  11.0 1.0 collective-permute-start.2
  12.0 0.6 filters.1
  12.6 3.2 %reorder.1 = (bf16[2,256,256]{2,1,0:T(8,128)(2,1)S(1)}, bf16[2,2,256,256]{3,2,1,0:T(8,128)(2,1)S(1)}, bf16[2,2,256,256]{3,2,1,0:T(8,128)(2,1)S(1)}, bf16[2,2,256...) custom-call(s32[5]{0:T(128)S(1)} %stack.23.where, bf16[4,2,256,256]{3,2,1,0:T(8,128)(2,1)} %residual.1, ...), custom_call_target="tpu_custom_call" | custom-call | tf_op jit(solution)/shard_map/reorder/pallas_call | solution.py:536
  15.8 0.8 copy-done.4
  16.6 0.8 copy-done.9
  17.4 0.8 copy-done.10
  18.2 4.9 %fusion.11 = (bf16[2,256,256]{2,1,0:T(8,128)(2,1)S(1)}, bf16[2,256,256]{2,1,0:T(8,128)(2,1)S(1)}, bf16[2,256,256]{2,1,0:T(8,128)(2,1)S(1)}) fusion(f32[256]{0:T(256)S(1)} %get-tuple-element.76, s32[256]{0:T(256)S(1)} %get-tuple-element.73, s32[256]{0:T(256)S(1)} %get-tuple-element.74, pred[256]{0:T(512)(128)(4,1)S(1)} %get-tuple-element.71, ...), kind=kLoop, calls=%fused_computation.24 | loop fusion | flops 6160384 | bytes 791040 | tf_op jit(solution)/shard_map/convert_element_type | solution.py:51
  23.2 0.0 collective-permute-done.rest_1_
  23.2 10.7 %collective-permute-done.1.rest_2_ = bf16[2,2,256,256]{3,2,1,0:T(8,128)(2,1)S(1)} collective-permute-done((bf16[2,2,256,256]{3,2,1,0:T(8,128)(2,1)S(1)}, bf16[2,2,256,256]{3,2,1,0:T(8,128)(2,1)S(1)}, u32[]{:S(2)}, u32[]{:S(2)}) %collective-permute-start.1) | collective-permute-done | bytes 524320 | tf_op jit(solution)/shard_map/ppermute | solution.py:585
  33.9 0.0 collective-permute-done.2.rest_3_
  33.9 0.7 chain_deep.1
  34.6 1.3 %collective-permute-start.3 = (bf16[2,256,256]{2,1,0:T(8,128)(2,1)S(1)}, bf16[2,256,256]{2,1,0:T(8,128)(2,1)S(1)}, u32[]{:S(2)}, u32[]{:S(2)}) collective-permute-start(bf16[2,256,256]{2,1,0:T(8,128)(2,1)S(1)} %get-tuple-element.42), channel_id=1, source_target_pairs={{64,0},{80,16},{96,32},{112,48},{65,1},{81,17},{97,33},{113,49},{6... | collective-permute-start | bytes 786440 | tf_op jit(solution)/shard_map/ppermute | solution.py:603
  35.9 14.9 %collective-permute-done.3.start = bf16[2,256,256]{2,1,0:T(8,128)(2,1)S(1)} collective-permute-done((bf16[2,256,256]{2,1,0:T(8,128)(2,1)S(1)}, bf16[2,256,256]{2,1,0:T(8,128)(2,1)S(1)}, u32[]{:S(2)}, u32[]{:S(2)}) %collective-permute-start.3) | collective-permute-done | bytes 262176 | tf_op jit(solution)/shard_map/ppermute | solution.py:603
  50.8 8.6 %chain_top.1 = (bf16[2,256,256]{2,1,0:T(8,128)(2,1)S(1)}, bf16[2,256,256]{2,1,0:T(8,128)(2,1)}, bf16[2,256,256]{2,1,0:T(8,128)(2,1)}, bf16[2,256,256]{2,1,0:T(8,128)(2,1)}, bf16[2,256,256]{2,1,0:T(8,128)(2,1)S(1)}) custom-call(s32[5]{0:T(128)S(1)} %stack.23.where, bf16[2,256,256]{2,1,0:T(8,128)(2,1)S(1)} %collective-permute-done.3.start, ...), custom_call_target="tpu_custom_call" | custom-call | tf_op jit(solution)/shard_map/chain_top/pallas_call | solution.py:301
  59.4 3.3 %collective-permute-start.6 = (bf16[2,256,256]{2,1,0:T(8,128)(2,1)}, bf16[2,256,256]{2,1,0:T(8,128)(2,1)}, u32[]{:S(2)}, u32[]{:S(2)}) collective-permute-start(bf16[2,256,256]{2,1,0:T(8,128)(2,1)} %get-tuple-element.51), channel_id=1, source_target_pairs={{0,48},{16,0},{32,16},{48,32},{64,112},{80,64},{96,80},{112,96},{1... | collective-permute-start | bytes 786440 | tf_op jit(solution)/shard_map/ppermute | solution.py:585
  62.6 0.0 collective-permute-start.5
  62.6 1.5 %collective-permute-start.4 = (bf16[2,256,256]{2,1,0:T(8,128)(2,1)}, bf16[2,256,256]{2,1,0:T(8,128)(2,1)}, u32[]{:S(2)}, u32[]{:S(2)}) collective-permute-start(bf16[2,256,256]{2,1,0:T(8,128)(2,1)} %get-tuple-element.47), channel_id=1, source_target_pairs={{0,32},{16,48},{32,0},{48,16},{64,96},{80,112},{96,64},{112,80},{1... | collective-permute-start | bytes 786440 | tf_op jit(solution)/shard_map/ppermute | solution.py:585
  64.2 3.2 %visit_0.1.rest_5_ = f32[2,2,3,384,128]{4,3,2,1,0:T(8,128)S(1)} custom-call(s32[5]{0:T(128)S(1)} %stack.23.where, s32[4,2]{1,0:T(4,128)S(1)} %copy.15.offsets, bf16[2,256,256]{2,1,0:T(8,128)(2,1)S(1)} %get-tuple-element.54.entry_at, bf16[2,2,256,256]{3,2,1,0:T(8,128)(2,1)} %copy-done.2, bf16[2,2,256,256]{3,2,1,0:T(8,128)(2,1)} %copy-done.4, ...), custom_call_target="tpu_custom_call" | custom-call | tf_op jit(solution)/shard_map/visit_0/pallas_call | solution.py:377
  67.4 0.3 pieces.1
  67.7 0.7 copy-done.3
  68.3 4.1 %all-to-all-start = ((bf16[8,128,128]{2,1,0:T(8,128)(2,1)}), bf16[8,128,128]{2,1,0:T(8,128)(2,1)}, u32[]{:S(2)}, u32[]{:S(2)}) async-start(bf16[8,128,128]{2,1,0:T(8,128)(2,1)} %copy-done.3), calls=%async_computation | async-start | bytes 524288 | tf_op jit(solution)/shard_map/all_to_all | solution.py:614
  72.4 2.2 %collective-permute-done.6.entry_at = bf16[2,256,256]{2,1,0:T(8,128)(2,1)} collective-permute-done((bf16[2,256,256]{2,1,0:T(8,128)(2,1)}, bf16[2,256,256]{2,1,0:T(8,128)(2,1)}, u32[]{:S(2)}, u32[]{:S(2)}) %collective-permute-start.6) | collective-permute-done | bytes 262176 | tf_op jit(solution)/shard_map/ppermute | solution.py:585
  74.6 0.9 copy-done.1
  75.6 3.7 %visit_3.1.rest_5_ = f32[2,2,3,384,128]{4,3,2,1,0:T(8,128)S(1)} custom-call(s32[5]{0:T(128)S(1)} %stack.23.where, s32[4,2]{1,0:T(4,128)S(1)} %copy.15.offsets, bf16[2,256,256]{2,1,0:T(8,128)(2,1)} %collective-permute-done.6.entry_at, bf16[2,2,256,256]{3,2,1,0:T(8,128)(2,1)} %copy-done.7, ...), custom_call_target="tpu_custom_call", output_to_operand_aliasing={{}: (10, {})} | custom-call | tf_op jit(solution)/shard_map/visit_3/pallas_call | solution.py:377
  79.2 0.0 collective-permute-done.5.entry_at
  79.2 3.7 %visit_1.1.rest_5_ = f32[2,2,3,384,128]{4,3,2,1,0:T(8,128)S(1)} custom-call(s32[5]{0:T(128)S(1)} %stack.23.where, s32[4,2]{1,0:T(4,128)S(1)} %copy.15.offsets, bf16[2,256,256]{2,1,0:T(8,128)(2,1)} %collective-permute-done.5.entry_at, bf16[2,2,256,256]{3,2,1,0:T(8,128)(2,1)} %copy-done.6, ...), custom_call_target="tpu_custom_call", output_to_operand_aliasing={{}: (10, {})} | custom-call | tf_op jit(solution)/shard_map/visit_1/pallas_call | solution.py:377
  82.9 3.6 %visit_2.1.grads = f32[2,2,3,384,128]{4,3,2,1,0:T(8,128)S(1)} custom-call(s32[5]{0:T(128)S(1)} %stack.23.where, s32[4,2]{1,0:T(4,128)S(1)} %copy.15.offsets, bf16[2,256,256]{2,1,0:T(8,128)(2,1)} %collective-permute-done.4.entry_at, bf16[2,2,256,256]{3,2,1,0:T(8,128)(2,1)} %copy-done.5, ...), custom_call_target="tpu_custom_call", output_to_operand_aliasing={{}: (10, {})} | custom-call | tf_op jit(solution)/shard_map/visit_2/pallas_call | solution.py:377
  86.6 1.2 %pack.1 = (bf16[4,2,112,384]{3,2,1,0:T(8,128)(2,1)S(1)}, bf16[4,2,112,384]{3,2,1,0:T(8,128)(2,1)S(1)}) custom-call(s32[5]{0:T(128)S(1)} %stack.23.where, f32[2,2,3,384,128]{4,3,2,1,0:T(8,128)S(1)} %visit_2.1.grads, bf16[8,128,128]{2,1,0:T(8,128)(2,1)} %all-to-all-done.probe), custom_call_target="tpu_custom_call" | custom-call | tf_op jit(solution)/shard_map/pack/pallas_call | solution.py:419
  87.8 0.1 collective-permute-start.7
  87.9 2.1 %collective-permute-done.7.arrived = bf16[4,2,112,384]{3,2,1,0:T(8,128)(2,1)S(1)} collective-permute-done((bf16[4,2,112,384]{3,2,1,0:T(8,128)(2,1)S(1)}, bf16[4,2,112,384]{3,2,1,0:T(8,128)(2,1)S(1)}, u32[]{:S(2)}, u32[]{:S(2)}) %collective-permute-start.7) | collective-permute-done | bytes 688160 | tf_op jit(solution)/shard_map/ppermute | solution.py:497
  90.0 0.2 core_sum.1
  90.2 1.6 %collective-permute-start.8 = (bf16[2,112,384]{2,1,0:T(8,128)(2,1)S(1)}, bf16[2,112,384]{2,1,0:T(8,128)(2,1)S(1)}, u32[]{:S(2)}, u32[]{:S(2)}) collective-permute-start(bf16[2,112,384]{2,1,0:T(8,128)(2,1)S(1)} %get-tuple-element.61), channel_id=1, source_target_pairs={{0,2},{1,3},{2,4},{3,5},{4,6},{5,7},{6,0},{7,1},{8,10},{9,11},{10,... | collective-permute-start | bytes 516104 | tf_op jit(solution)/shard_map/ppermute | solution.py:497
  91.8 2.9 %collective-permute-start.9 = (bf16[2,112,384]{2,1,0:T(8,128)(2,1)S(1)}, bf16[2,112,384]{2,1,0:T(8,128)(2,1)S(1)}, u32[]{:S(2)}, u32[]{:S(2)}) collective-permute-start(bf16[2,112,384]{2,1,0:T(8,128)(2,1)S(1)} %get-tuple-element.62), channel_id=1, source_target_pairs={{0,4},{1,5},{2,6},{3,7},{4,0},{5,1},{6,2},{7,3},{8,12},{9,13},{10,... | collective-permute-start | bytes 516104 | tf_op jit(solution)/shard_map/ppermute | solution.py:497
  94.7 1.9 %collective-permute-start.10 = (bf16[2,112,384]{2,1,0:T(8,128)(2,1)S(1)}, bf16[2,112,384]{2,1,0:T(8,128)(2,1)S(1)}, u32[]{:S(2)}, u32[]{:S(2)}) collective-permute-start(bf16[2,112,384]{2,1,0:T(8,128)(2,1)S(1)} %get-tuple-element.63), channel_id=1, source_target_pairs={{0,6},{1,7},{2,0},{3,1},{4,2},{5,3},{6,4},{7,5},{8,14},{9,15},{10,... | collective-permute-start | bytes 516104 | tf_op jit(solution)/shard_map/ppermute | solution.py:497
  96.6 1.3 %collective-permute-done.8.rest_1_ = bf16[2,112,384]{2,1,0:T(8,128)(2,1)S(1)} collective-permute-done((bf16[2,112,384]{2,1,0:T(8,128)(2,1)S(1)}, bf16[2,112,384]{2,1,0:T(8,128)(2,1)S(1)}, u32[]{:S(2)}, u32[]{:S(2)}) %collective-permute-start.8) | collective-permute-done | bytes 172064 | tf_op jit(solution)/shard_map/ppermute | solution.py:497
  97.9 4.9 %collective-permute-done.9.rest_2_ = bf16[2,112,384]{2,1,0:T(8,128)(2,1)S(1)} collective-permute-done((bf16[2,112,384]{2,1,0:T(8,128)(2,1)S(1)}, bf16[2,112,384]{2,1,0:T(8,128)(2,1)S(1)}, u32[]{:S(2)}, u32[]{:S(2)}) %collective-permute-start.9) | collective-permute-done | bytes 172064 | tf_op jit(solution)/shard_map/ppermute | solution.py:497
  102.8 0.0 collective-permute-done.10.rest_3_
  102.8 0.6 ring_sum.1
  103.4 3.3 %collective-permute-start.11 = (bf16[112,384]{1,0:T(8,128)(2,1)S(1)}, bf16[112,384]{1,0:T(8,128)(2,1)S(1)}, u32[]{:S(2)}, u32[]{:S(2)}) collective-permute-start(bf16[112,384]{1,0:T(8,128)(2,1)S(1)} %get-tuple-element.65), channel_id=1, source_target_pairs={{0,8},{1,9},{2,10},{3,11},{4,12},{5,13},{6,14},{7,15},{8,0},{9,1},... | collective-permute-start | bytes 258056 | tf_op jit(solution)/shard_map/ppermute | solution.py:497
  106.8 2.7 %collective-permute-done.11.arrived = bf16[112,384]{1,0:T(8,128)(2,1)S(1)} collective-permute-done((bf16[112,384]{1,0:T(8,128)(2,1)S(1)}, bf16[112,384]{1,0:T(8,128)(2,1)S(1)}, u32[]{:S(2)}, u32[]{:S(2)}) %collective-permute-start.11) | collective-permute-done | bytes 86048 | tf_op jit(solution)/shard_map/ppermute | solution.py:497
  109.5 0.7 last_sum.1
  110.2 0.1 reshape.14
  110.3 0.6 copy.16
  (24 shorter events, 0.1 us)
Async XLA Ops:
  0.6 11.4 %copy-start.11 = (f32[256,256]{1,0:T(8,128)S(1)}, f32[256,256]{1,0:T(8,128)}, u32[]{:S(2)}) copy-start(f32[256,256]{1,0:T(8,128)} %phase.1) | copy-start | bytes 786436
  5.3 29.3 %copy-start.5 = (bf16[2,2,256,256]{3,2,1,0:T(8,128)(2,1)}, bf16[2,2,256,256]{3,2,1,0:T(8,128)(2,1)S(1)}, u32[]{:S(2)}) copy-start(bf16[2,2,256,256]{3,2,1,0:T(8,128)(2,1)S(1)} %get-tuple-element.38.window_at) | copy-start | bytes 1572868
  5.3 29.3 %copy-start.6 = (bf16[2,2,256,256]{3,2,1,0:T(8,128)(2,1)}, bf16[2,2,256,256]{3,2,1,0:T(8,128)(2,1)S(1)}, u32[]{:S(2)}) copy-start(bf16[2,2,256,256]{3,2,1,0:T(8,128)(2,1)S(1)} %get-tuple-element.39.window_at) | copy-start | bytes 1572868
  5.3 29.3 %copy-start.7 = (bf16[2,2,256,256]{3,2,1,0:T(8,128)(2,1)}, bf16[2,2,256,256]{3,2,1,0:T(8,128)(2,1)S(1)}, u32[]{:S(2)}) copy-start(bf16[2,2,256,256]{3,2,1,0:T(8,128)(2,1)S(1)} %get-tuple-element.37.window_at) | copy-start | bytes 1572868
  5.3 45.5 %copy-start.2 = (bf16[2,2,256,256]{3,2,1,0:T(8,128)(2,1)}, bf16[2,2,256,256]{3,2,1,0:T(8,128)(2,1)S(1)}, u32[]{:S(2)}) copy-start(bf16[2,2,256,256]{3,2,1,0:T(8,128)(2,1)S(1)} %get-tuple-element.36.rest_0_.window_at) | copy-start | bytes 1572868
  5.3 17.9 %collective-permute-start = (bf16[2,2,256,256]{3,2,1,0:T(8,128)(2,1)S(1)}, bf16[2,2,256,256]{3,2,1,0:T(8,128)(2,1)S(1)}, u32[]{:S(2)}, u32[]{:S(2)}) collective-permute-start(bf16[2,2,256,256]{3,2,1,0:T(8,128)(2,1)S(1)} %get-tuple-element.37.window_at), channel_id=1, source_target_pairs={{0,16},{16,32},{32,48},{48,0},{64,80},{80,96},{96,112},{112,64},{1... | collective-permute-start | bytes 1572872 | tf_op jit(solution)/shard_map/ppermute | solution.py:585
  7.4 26.5 %collective-permute-start.1 = (bf16[2,2,256,256]{3,2,1,0:T(8,128)(2,1)S(1)}, bf16[2,2,256,256]{3,2,1,0:T(8,128)(2,1)S(1)}, u32[]{:S(2)}, u32[]{:S(2)}) collective-permute-start(bf16[2,2,256,256]{3,2,1,0:T(8,128)(2,1)S(1)} %get-tuple-element.38.window_at), channel_id=1, source_target_pairs={{0,32},{16,48},{32,0},{48,16},{64,96},{80,112},{96,64},{112,80},{1... | collective-permute-start | bytes 1572872 | tf_op jit(solution)/shard_map/ppermute | solution.py:585
  11.0 22.9 %collective-permute-start.2 = (bf16[2,2,256,256]{3,2,1,0:T(8,128)(2,1)S(1)}, bf16[2,2,256,256]{3,2,1,0:T(8,128)(2,1)S(1)}, u32[]{:S(2)}, u32[]{:S(2)}) collective-permute-start(bf16[2,2,256,256]{3,2,1,0:T(8,128)(2,1)S(1)} %get-tuple-element.39.window_at), channel_id=1, source_target_pairs={{0,48},{16,0},{32,16},{48,32},{64,112},{80,64},{96,80},{112,96},{1... | collective-permute-start | bytes 1572872 | tf_op jit(solution)/shard_map/ppermute | solution.py:585
  15.8 0.8 copy-start.4
  16.6 0.8 copy-start.9
  17.4 0.8 copy-start.10
  18.2 15.7 %copy-start.8 = (bf16[2,2,256,256]{3,2,1,0:T(8,128)(2,1)}, bf16[2,2,256,256]{3,2,1,0:T(8,128)(2,1)S(1)}, u32[]{:S(2)}) copy-start(bf16[2,2,256,256]{3,2,1,0:T(8,128)(2,1)S(1)} %get-tuple-element.48.psi_at) | copy-start | bytes 1572868
  23.2 41.0 %copy-start = (bf16[2,256,256]{2,1,0:T(8,128)(2,1)}, bf16[2,256,256]{2,1,0:T(8,128)(2,1)S(1)}, u32[]{:S(2)}) copy-start(bf16[2,256,256]{2,1,0:T(8,128)(2,1)S(1)} %get-tuple-element.70.rest_6_.rest_10_.rest_2_) | copy-start | bytes 786436
  34.6 16.2 %collective-permute-start.3 = (bf16[2,256,256]{2,1,0:T(8,128)(2,1)S(1)}, bf16[2,256,256]{2,1,0:T(8,128)(2,1)S(1)}, u32[]{:S(2)}, u32[]{:S(2)}) collective-permute-start(bf16[2,256,256]{2,1,0:T(8,128)(2,1)S(1)} %get-tuple-element.42), channel_id=1, source_target_pairs={{64,0},{80,16},{96,32},{112,48},{65,1},{81,17},{97,33},{113,49},{6... | collective-permute-start | bytes 786440 | tf_op jit(solution)/shard_map/ppermute | solution.py:603
  59.4 15.2 %collective-permute-start.6 = (bf16[2,256,256]{2,1,0:T(8,128)(2,1)}, bf16[2,256,256]{2,1,0:T(8,128)(2,1)}, u32[]{:S(2)}, u32[]{:S(2)}) collective-permute-start(bf16[2,256,256]{2,1,0:T(8,128)(2,1)} %get-tuple-element.51), channel_id=1, source_target_pairs={{0,48},{16,0},{32,16},{48,32},{64,112},{80,64},{96,80},{112,96},{1... | collective-permute-start | bytes 786440 | tf_op jit(solution)/shard_map/ppermute | solution.py:585
  62.6 16.6 %collective-permute-start.5 = (bf16[2,256,256]{2,1,0:T(8,128)(2,1)}, bf16[2,256,256]{2,1,0:T(8,128)(2,1)}, u32[]{:S(2)}, u32[]{:S(2)}) collective-permute-start(bf16[2,256,256]{2,1,0:T(8,128)(2,1)} %get-tuple-element.49), channel_id=1, source_target_pairs={{0,16},{16,32},{32,48},{48,0},{64,80},{80,96},{96,112},{112,64},{1... | collective-permute-start | bytes 786440 | tf_op jit(solution)/shard_map/ppermute | solution.py:585
  62.6 20.3 %collective-permute-start.4 = (bf16[2,256,256]{2,1,0:T(8,128)(2,1)}, bf16[2,256,256]{2,1,0:T(8,128)(2,1)}, u32[]{:S(2)}, u32[]{:S(2)}) collective-permute-start(bf16[2,256,256]{2,1,0:T(8,128)(2,1)} %get-tuple-element.47), channel_id=1, source_target_pairs={{0,32},{16,48},{32,0},{48,16},{64,96},{80,112},{96,64},{112,80},{1... | collective-permute-start | bytes 786440 | tf_op jit(solution)/shard_map/ppermute | solution.py:585
  67.7 0.7 copy-start.3
  68.3 18.2 %all-to-all-start = ((bf16[8,128,128]{2,1,0:T(8,128)(2,1)}), bf16[8,128,128]{2,1,0:T(8,128)(2,1)}, u32[]{:S(2)}, u32[]{:S(2)}) async-start(bf16[8,128,128]{2,1,0:T(8,128)(2,1)} %copy-done.3), calls=%async_computation | async-start | bytes 524288 | tf_op jit(solution)/shard_map/all_to_all | solution.py:614
  74.6 0.9 copy-start.1
  87.8 2.2 %collective-permute-start.7 = (bf16[4,2,112,384]{3,2,1,0:T(8,128)(2,1)S(1)}, bf16[4,2,112,384]{3,2,1,0:T(8,128)(2,1)S(1)}, u32[]{:S(2)}, u32[]{:S(2)}) collective-permute-start(bf16[4,2,112,384]{3,2,1,0:T(8,128)(2,1)S(1)} %get-tuple-element.59), channel_id=1, source_target_pairs={{0,1},{1,0},{2,3},{3,2},{4,5},{5,4},{6,7},{7,6},{8,9},{9,8},{10,11... | collective-permute-start | bytes 2064392 | tf_op jit(solution)/shard_map/ppermute | solution.py:497
  90.2 7.8 %collective-permute-start.8 = (bf16[2,112,384]{2,1,0:T(8,128)(2,1)S(1)}, bf16[2,112,384]{2,1,0:T(8,128)(2,1)S(1)}, u32[]{:S(2)}, u32[]{:S(2)}) collective-permute-start(bf16[2,112,384]{2,1,0:T(8,128)(2,1)S(1)} %get-tuple-element.61), channel_id=1, source_target_pairs={{0,2},{1,3},{2,4},{3,5},{4,6},{5,7},{6,0},{7,1},{8,10},{9,11},{10,... | collective-permute-start | bytes 516104 | tf_op jit(solution)/shard_map/ppermute | solution.py:497
  91.8 11.0 %collective-permute-start.9 = (bf16[2,112,384]{2,1,0:T(8,128)(2,1)S(1)}, bf16[2,112,384]{2,1,0:T(8,128)(2,1)S(1)}, u32[]{:S(2)}, u32[]{:S(2)}) collective-permute-start(bf16[2,112,384]{2,1,0:T(8,128)(2,1)S(1)} %get-tuple-element.62), channel_id=1, source_target_pairs={{0,4},{1,5},{2,6},{3,7},{4,0},{5,1},{6,2},{7,3},{8,12},{9,13},{10,... | collective-permute-start | bytes 516104 | tf_op jit(solution)/shard_map/ppermute | solution.py:497
  94.7 8.1 %collective-permute-start.10 = (bf16[2,112,384]{2,1,0:T(8,128)(2,1)S(1)}, bf16[2,112,384]{2,1,0:T(8,128)(2,1)S(1)}, u32[]{:S(2)}, u32[]{:S(2)}) collective-permute-start(bf16[2,112,384]{2,1,0:T(8,128)(2,1)S(1)} %get-tuple-element.63), channel_id=1, source_target_pairs={{0,6},{1,7},{2,0},{3,1},{4,2},{5,3},{6,4},{7,5},{8,14},{9,15},{10,... | collective-permute-start | bytes 516104 | tf_op jit(solution)/shard_map/ppermute | solution.py:497
  103.4 6.1 %collective-permute-start.11 = (bf16[112,384]{1,0:T(8,128)(2,1)S(1)}, bf16[112,384]{1,0:T(8,128)(2,1)S(1)}, u32[]{:S(2)}, u32[]{:S(2)}) collective-permute-start(bf16[112,384]{1,0:T(8,128)(2,1)S(1)} %get-tuple-element.65), channel_id=1, source_target_pairs={{0,8},{1,9},{2,10},{3,11},{4,12},{5,13},{6,14},{7,15},{8,0},{9,1},... | collective-permute-start | bytes 258056 | tf_op jit(solution)/shard_map/ppermute | solution.py:497

commit v6 on v5

--- a/solution.py
+++ b/solution.py
@@ -31,26 +31,6 @@
 
 def half(index):
     return slice(index * HALF, (index + 1) * HALF)
-
-
-def transform_tables(width):
-    span = width // 2
-    shape = (2, width, width)
-    parity = lax.broadcasted_iota(jnp.int32, shape, 0)
-
-    def build(spread_dim, sign):
-        rows = lax.broadcasted_iota(jnp.int32, shape, 1)
-        cols = lax.broadcasted_iota(jnp.int32, shape, 2)
-        spread, other = (rows, cols) if spread_dim == 1 else (cols, rows)
-        order = (2 * (spread % span) + parity) * (other % span) % width
-        phase = 2.0 * math.pi / width * order.astype(F32)
-        factor = 1.0 / math.sqrt(width)
-        low = rows < span
-        left = cols < span
-        value = jnp.where(low == left, jnp.cos(phase), jnp.where(low, sign, -sign) * jnp.sin(phase))
-        return (value * factor).astype(BF)
-
-    return build(2, 1.0), build(1, 1.0), build(2, -1.0)
 
 
 def dot(a, b):
@@ -119,7 +99,27 @@
     return 2.0 * low_sine * low_cosine, 1.0 - 2.0 * low_sine * low_sine
 
 
-def filter_kernel(phase, kernel_cos, kernel_sin, plain):
+def write_tables(inward, table, flipped):
+    first = lax.broadcasted_iota(jnp.int32, (HALF, HALF), 0)
+    second = lax.broadcasted_iota(jnp.int32, (HALF, HALF), 1)
+    factor = 1.0 / math.sqrt(N)
+    for spread, other, targets in (
+        (second, first, ((inward, 1.0), (flipped, -1.0))),
+        (first, second, ((table, 1.0),)),
+    ):
+        for parity in (0, 1):
+            order = (2 * spread + parity) * other % N
+            order = jnp.where(order > HALF, order - N, order)
+            sine, cosine = sine_and_cosine(2.0 * math.pi / N * order.astype(F32))
+            for target, sign in targets:
+                for row in (0, 1):
+                    target[parity, half(row), half(row)] = (cosine * factor).astype(BF)
+                    turned_sine = sine * (factor * (sign if row == 0 else -sign))
+                    target[parity, half(row), half(1 - row)] = turned_sine.astype(BF)
+
+
+def filter_kernel(phase, inward, table, flipped, kernel_cos, kernel_sin, plain):
+    write_tables(inward, table, flipped)
     rows = lax.broadcasted_iota(jnp.int32, (N, N), 0)
     cols = lax.broadcasted_iota(jnp.int32, (N, N), 1)
     take = (rows == 2 * (cols % HALF) + cols // HALF).astype(F32).astype(BF)
@@ -141,10 +141,13 @@
 
 def filters(phase):
     shape = jax.ShapeDtypeStruct((N, N), F32)
+    pair = jax.ShapeDtypeStruct((2, N, N), BF)
     return pl.pallas_call(
         filter_kernel,
         name="filters",
-        out_shape=[shape, shape],
+        out_shape=[pair, pair, pair, shape, shape],
+        in_specs=[VM],
+        out_specs=[VM] * 5,
         scratch_shapes=[pltpu.VMEM((2, 2, N, HALF), F32)],
         compiler_params=pltpu.CompilerParams(vmem_limit_bytes=VMEM_LIMIT),
     )(phase)
@@ -214,35 +217,36 @@
     )(where, offsets, in_hbm(phase), in_hbm(amp))
 
 
+def column_pieces(wave, place_at, target):
+    width = N // DEPTH
+    lane = lax.broadcasted_iota(jnp.int32, (HALF, HALF), 1) // width
+    for far in (0, 1):
+        value = jnp.zeros((HALF, HALF), F32)
+        for parity in (0, 1):
+            for part in (0, 1):
+                place = 2 * parity + part
+                source = wave[parity, half(part), half(far)].astype(F32)
+                turn = (place + RING - place_at) % RING * width
+                value = jnp.where(lane == place, pltpu.roll(source, turn, 1), value)
+        target[:, half(far)] = value.astype(BF)
+
+
 def chain_kernel(first, where, start, *rest):
-    windows = rest[:RING]
-    earlier = () if first else rest[RING : 2 * RING]
-    rest = rest[RING + len(earlier) :]
+    count = RING + 1 if first else RING
+    windows = rest[: RING + 1]
+    earlier = () if first else rest[RING + 1 : 2 * RING + 1]
+    rest = rest[RING + 1 + len(earlier) :]
     tables = rest[:5]
-    count = RING + 1
     outs = rest[5 : 5 + count]
-    trans, waves, middle, mixed, filtered, second, in_sems, out_sems = rest[5 + count :]
+    trans, waves, middle, mixed, filtered, second = rest[5 + count :]
     rank = where[0]
     active = where[1] == 1 if first else where[1] == 0
-
-    def window_load(distance, layer):
-        slot = (rank + RING - distance) % RING
-        source = windows[distance].at[layer]
-        return pltpu.make_async_copy(source, trans.at[slot, layer], in_sems.at[slot, layer])
-
-    def store(k):
-        return pltpu.make_async_copy(waves.at[k], outs[k], out_sems.at[k])
+    inner = jnp.logical_or(rank == 1, rank == 2)
 
     @pl.when(active)
     def _():
-        begin_load = pltpu.make_async_copy(
-            start, waves.at[(2 * RING - 1 - rank) % RING], in_sems.at[RING, 0]
-        )
-        begin_load.start()
-        for distance in range(RING):
-            for layer in (1, 0):
-                window_load(distance, layer).start()
-        begin_load.wait()
+        for parity in (0, 1):
+            waves[(2 * RING - 1 - rank) % RING, parity] = start[parity * N : (parity + 1) * N, :]
 
         def pair(step, carry):
             pair_at = RING - 1 - step
@@ -251,7 +255,8 @@
 
                 @pl.when(slot == k)
                 def _(k=k):
-                    store(k).start()
+                    for parity in (0, 1):
+                        outs[k][parity * N : (parity + 1) * N, :] = waves[k, parity]
 
             source = waves.at[slot]
             target = waves.at[
@@ -260,14 +265,21 @@
             for layer, begin, end in ((1, source, middle), (0, middle, target)):
 
                 def ready(layer=layer):
-                    pltpu.make_async_copy(
-                        windows[0].at[layer], trans.at[pair_at, layer], in_sems.at[pair_at, layer]
-                    ).wait()
+                    distance = (rank + RING - pair_at) % RING
+                    index = jnp.where(
+                        jnp.logical_and(distance == 2, jnp.logical_not(inner)), RING, distance
+                    )
+                    for k in range(RING + 1):
+
+                        @pl.when(index == k)
+                        def _(k=k):
+                            for parity in (0, 1):
+                                trans[parity] = windows[k][layer, parity]
 
                 def finish(parity, reals, imags, layer=layer, end=end):
                     for col in (0, 1):
-                        tr = trans[pair_at, layer, parity, half(0), half(col)].astype(F32)
-                        ti = trans[pair_at, layer, parity, half(1), half(col)].astype(F32)
+                        tr = trans[parity, half(0), half(col)].astype(F32)
+                        ti = trans[parity, half(1), half(col)].astype(F32)
                         qr, qi = reals[col], imags[col]
                         end[parity, half(0), half(col)] = (tr * qr + ti * qi).astype(BF)
                         end[parity, half(1), half(col)] = (tr * qi - ti * qr).astype(BF)
@@ -276,56 +288,44 @@
             return carry
 
         lax.fori_loop(0, RING, pair, 0)
-        store(RING).start()
-        for k in range(RING + 1):
-            store(k).wait()
+        if first:
+            for parity in (0, 1):
+                outs[RING][parity * N : (parity + 1) * N, :] = waves[RING, parity]
+        else:
+            for k in range(RING):
+                column_pieces(waves.at[RING], (rank + k) % RING, outs[k].at[2 * N :])
 
     if not first:
 
         @pl.when(jnp.logical_not(active))
         def _():
-            copies = [
-                pltpu.make_async_copy(earlier[k], outs[k], out_sems.at[k]) for k in range(RING)
-            ]
-            middle[...] = jnp.zeros_like(middle)
-            copies.append(pltpu.make_async_copy(middle, outs[RING], out_sems.at[RING]))
-            for copy in copies:
-                copy.start()
-            for copy in copies:
-                copy.wait()
+            for k in range(RING):
+                outs[k][: 2 * N, :] = earlier[k][...]
+                outs[k][2 * N :, :] = jnp.zeros((HALF, N), BF)
 
 
 def run_chain(first, where, start, windows, earlier, tables):
-    count = RING + 1
-    wave = jax.ShapeDtypeStruct((2, N, N), BF)
+    count = RING + 1 if first else RING
+    wave = jax.ShapeDtypeStruct((2 * N if first else 2 * N + HALF, N), BF)
     return pl.pallas_call(
         functools.partial(chain_kernel, first),
         name="chain_deep" if first else "chain_top",
         out_shape=[wave] * count,
-        in_specs=[SM, ANY] + [ANY] * RING + [ANY] * len(earlier) + [VM] * 5,
-        out_specs=[ANY] * count,
+        in_specs=[SM] + [VM] * (RING + 7 + len(earlier)),
+        out_specs=[VM] * count,
         scratch_shapes=[
-            pltpu.VMEM((RING, 2, 2, N, N), BF),
+            pltpu.VMEM((2, N, N), BF),
             pltpu.VMEM((RING + 1, 2, N, N), BF),
             pltpu.VMEM((2, N, N), BF),
             *step_scratch(),
-            pltpu.SemaphoreType.DMA((RING + 1, 2)),
-            pltpu.SemaphoreType.DMA((RING + 1,)),
         ],
         compiler_params=pltpu.CompilerParams(vmem_limit_bytes=VMEM_LIMIT),
     )(where, start, *windows, *earlier, *tables)
 
 
-def visit_kernel(index, where, offsets, entry_at, window_at, psi_at, *rest):
+def visit_kernel(index, where, offsets, entry, window, psi, *rest):
     tables = rest[:5]
-    grads, entry, window, psi, middle, mixed, filtered, second, sems = rest[-9:]
-    loads = [
-        pltpu.make_async_copy(entry_at, entry, sems.at[0]),
-        pltpu.make_async_copy(window_at.at[1], window, sems.at[1]),
-        pltpu.make_async_copy(psi_at, psi, sems.at[2]),
-    ]
-    for copy in loads:
-        copy.start()
+    grads, middle, mixed, filtered, second = rest[-5:]
     if index == 0:
         grads[...] = jnp.zeros_like(grads)
     lane = lax.broadcasted_iota(jnp.int32, (HALF, HALF), 1)
@@ -333,11 +333,6 @@
     col_at = offsets[position, 1]
     turn = col_at % HALF
     inside = lane >= col_at
-    loads[0].wait()
-
-    def ready():
-        loads[1].wait()
-        loads[2].wait()
 
     for layer in (1, 0):
 
@@ -350,8 +345,8 @@
                 terms[0].append(pltpu.roll(wr * qr + wi * qi, turn, 1))
                 terms[1].append(pltpu.roll(wr * qi - wi * qr, turn, 1))
                 if layer == 1:
-                    tr = window[parity, half(0), half(col)].astype(F32)
-                    ti = window[parity, half(1), half(col)].astype(F32)
+                    tr = window[layer, parity, half(0), half(col)].astype(F32)
+                    ti = window[layer, parity, half(1), half(col)].astype(F32)
                     middle[parity, half(0), half(col)] = (tr * qr + ti * qi).astype(BF)
                     middle[parity, half(1), half(col)] = (tr * qi - ti * qr).astype(BF)
             rows = pl.ds(offsets[position, 0] + parity, HALF, stride=2)
@@ -367,7 +362,8 @@
                     grads[layer, part, col, rows, :] += placed[col]
 
         if layer == 1:
-            back_step(entry, tables, mixed, filtered, second, finish, ready)
+            waves = (entry[:N, :], entry[N : 2 * N, :])
+            back_step(waves, tables, mixed, filtered, second, finish)
         else:
             back_step(middle, tables, mixed, filtered, second, finish)
 
@@ -378,27 +374,49 @@
         functools.partial(visit_kernel, index),
         name=f"visit_{index}",
         out_shape=jax.ShapeDtypeStruct((2, 2, 3, PATCH, HALF), F32),
-        in_specs=[SM, SM] + [ANY] * 3 + [VM] * (5 + len(earlier)),
+        in_specs=[SM, SM] + [VM] * (8 + len(earlier)),
         out_specs=VM,
         scratch_shapes=[
             pltpu.VMEM((2, N, N), BF),
-            pltpu.VMEM((2, N, N), BF),
-            pltpu.VMEM((2, 2, N, N), BF),
-            pltpu.VMEM((2, N, N), BF),
             *step_scratch(),
-            pltpu.SemaphoreType.DMA((3,)),
         ],
         input_output_aliases={10: 0} if earlier else {},
         compiler_params=pltpu.CompilerParams(vmem_limit_bytes=VMEM_LIMIT),
-    )(where, offsets, entry, in_hbm(window), in_hbm(psi), *tables, *earlier)
-
-
-def pack_kernel(where, grads, probe, keep, send, summed):
+    )(where, offsets, entry, window, psi, *tables, *earlier)
+
+
+def probe_sum_kernel(*refs):
+    entries, (own, other) = refs[:RING], refs[RING:]
+    total = entries[0][2 * N :, :].astype(F32)
+    for entry in entries[1:]:
+        total = total + entry[2 * N :, :].astype(F32)
+    own[...] = total[:, :HALF].astype(BF)
+    other[...] = total[:, HALF:].astype(BF)
+
+
+def probe_sum(entries):
+    shape = jax.ShapeDtypeStruct((HALF, HALF), BF)
+    return pl.pallas_call(
+        probe_sum_kernel,
+        name="probe_sum",
+        out_shape=[shape, shape],
+        in_specs=[VM] * RING,
+        out_specs=[VM, VM],
+        compiler_params=pltpu.CompilerParams(vmem_limit_bytes=VMEM_LIMIT),
+    )(*entries)
+
+
+def pack_kernel(where, grads, own_probe, far_probe, keep, send, summed):
     core, y_at = where[2], where[3]
-    total = jnp.zeros((HALF, HALF), F32)
-    for source in range(DEPTH):
-        total = total + probe[source].astype(F32)
-    summed[...] = total
+
+    @pl.when(where[1] == 0)
+    def _():
+        summed[...] = own_probe[...].astype(F32)
+
+    @pl.when(where[1] == 1)
+    def _():
+        summed[...] = far_probe[...].astype(F32)
+
     for distance in range(RING):
         for x_at in (0, 1):
             for out, core_at in ((keep, core), (send, 1 - core)):
@@ -414,17 +432,17 @@
                     out[distance, x_at, :, half(col)] = jnp.concatenate(pieces, 0).astype(BF)
 
 
-def packed(where, grads, probe):
+def packed(where, grads, own_probe, far_probe):
     shape = jax.ShapeDtypeStruct((RING, 2, CHUNK, PATCH), BF)
     return pl.pallas_call(
         pack_kernel,
         name="pack",
         out_shape=[shape, shape],
-        in_specs=[SM, VM, VM],
+        in_specs=[SM, VM, VM, VM],
         out_specs=[VM, VM],
         scratch_shapes=[pltpu.VMEM((HALF, HALF), F32)],
         compiler_params=pltpu.CompilerParams(vmem_limit_bytes=VMEM_LIMIT),
-    )(where, grads, probe)
+    )(where, grads, own_probe, far_probe)
 
 
 def core_sum_kernel(keep, arrived, *outs):
@@ -498,7 +516,7 @@
 
 
 def order_kernel(where, residual, saved, start, *rest):
-    outs, (first, waves, done, sems, out_sems) = rest[:RING], rest[RING:]
+    outs, (first, begin, waves, sems) = rest[:RING], rest[RING:]
     rank = where[0]
     loads = [pltpu.make_async_copy(residual.at[rank], first, sems.at[RING])]
     for index in range(RING):
@@ -518,17 +536,14 @@
             for parity in (0, 1):
                 target[parity, half(part), :] = ordered[half(parity), :]
 
-    stores = []
     loads[0].wait()
-    reorder(first, start)
+    reorder(first, begin)
+    for parity in (0, 1):
+        start[parity * N : (parity + 1) * N, :] = begin[parity]
     for index in range(RING):
         loads[1 + index].wait()
         for layer in (0, 1):
-            reorder(waves.at[index, layer], done.at[index, layer])
-        stores.append(pltpu.make_async_copy(done.at[index], outs[index], out_sems.at[index]))
-        stores[-1].start()
-    for copy in stores:
-        copy.wait()
+            reorder(waves.at[index, layer], outs[index].at[layer])
 
 
 def row_parity_first(where, residual, saved):
@@ -536,44 +551,18 @@
     return pl.pallas_call(
         order_kernel,
         name="reorder",
-        out_shape=[jax.ShapeDtypeStruct(wave, BF)]
+        out_shape=[jax.ShapeDtypeStruct((2 * N, N), BF)]
         + [jax.ShapeDtypeStruct((2, *wave), BF)] * RING,
         in_specs=[SM, ANY, ANY],
-        out_specs=[VM] + [pl.BlockSpec(memory_space=pltpu.HBM)] * RING,
+        out_specs=[VM] * (RING + 1),
         scratch_shapes=[
             pltpu.VMEM(wave, BF),
-            pltpu.VMEM((RING, 2, *wave), BF),
+            pltpu.VMEM(wave, BF),
             pltpu.VMEM((RING, 2, *wave), BF),
             pltpu.SemaphoreType.DMA((RING + 1,)),
-            pltpu.SemaphoreType.DMA((RING,)),
         ],
         compiler_params=pltpu.CompilerParams(vmem_limit_bytes=VMEM_LIMIT),
     )(where, in_hbm(residual), in_hbm(saved))
-
-
-def pieces_kernel(wave, pieces):
-    width = N // DEPTH
-    lane = lax.broadcasted_iota(jnp.int32, (HALF, HALF), 1) // width
-    for piece in range(DEPTH):
-        per_tile = HALF // width
-        value = jnp.zeros((HALF, HALF), F32)
-        for parity in (0, 1):
-            for part in (0, 1):
-                place = 2 * parity + part
-                source = wave[parity, half(part), half(piece // per_tile)].astype(F32)
-                shift = (place - piece % per_tile) * width % HALF
-                moved = pltpu.roll(source, shift, 1) if shift else source
-                value = jnp.where(lane == place, moved, value)
-        pieces[piece] = value.astype(BF)
-
-
-def column_pieces(wave):
-    return pl.pallas_call(
-        pieces_kernel,
-        name="pieces",
-        out_shape=jax.ShapeDtypeStruct((DEPTH, HALF, HALF), BF),
-        compiler_params=pltpu.CompilerParams(vmem_limit_bytes=VMEM_LIMIT),
-    )(wave)
 
 
 def turned(array, distance):
@@ -589,6 +578,18 @@
     return [arrays[0]] + [turned(arrays[k], k) for k in range(1, RING)]
 
 
+def ring_route(*pairs):
+    return [(RING * ring + a, RING * ring + b) for ring in range(2) for a, b in pairs]
+
+
+def exchanged_windows(own):
+    relay = lax.ppermute(own[2], "depth", ring_route((1, 0), (2, 3)))
+    far = lax.ppermute(own[2], "depth", ring_route((0, 2), (3, 1)))
+    ahead = turned(own[1], 1)
+    back = turned(own[3], 3)
+    return [own[0], ahead, far, back, lax.ppermute(relay, "depth", ring_route((0, 3), (3, 0)))]
+
+
 def shards(residual, saved_waves, object_phase, object_amp, prop_phase, offsets):
     depth_at = lax.axis_index("depth")
     probe_at = lax.axis_index("probe")
@@ -596,23 +597,23 @@
         [depth_at % RING, depth_at // RING, probe_at % 2, probe_at // 2 % RING, probe_at // 8]
     ).astype(jnp.int32)
     own = transmission_windows(where, offsets, object_phase, object_amp)
-    tables = (*transform_tables(N), *filters(prop_phase))
+    tables = filters(prop_phase)
     start, *waves = row_parity_first(where, residual, saved_waves)
-    foreign = exchanged(own)
+    foreign = exchanged_windows(own)
     *deep, leaving = run_chain(True, where, start, foreign, (), tables)
     arrived = lax.ppermute(leaving, "depth", [(RING + i, i) for i in range(RING)])
-    *entries, ending = run_chain(False, where, arrived, foreign, deep, tables)
-    entries = exchanged(entries)
+    entries = exchanged(run_chain(False, where, arrived, foreign, deep, tables))
     grads = None
     for index in (0, 3, 1, 2):
+        if index == 2:
+            *entries, grads = lax.optimization_barrier((*entries, grads))
+            own_probe, other_probe = probe_sum(entries)
+            far_probe = lax.ppermute(other_probe, "depth", [(i, RING + i) for i in range(RING)])
         window = own[(RING - index) % RING]
         grads = visit(
             index, where, offsets, entries[index], window, waves[index], tables, grads
         )
-        if index == 0:
-            ending, grads = lax.optimization_barrier((ending, grads))
-            probe = lax.all_to_all(column_pieces(ending), "depth", 0, 0, tiled=True)
-    keep, send = packed(where, grads, probe)
+    keep, send = packed(where, grads, own_probe, far_probe)
     parts = list(core_sum(keep, moved(send, 0, 0, 1)))
     parts = parts[:1] + [moved(parts[k], 0, k, 0) for k in range(1, RING)]
     keep, send = ring_sum(where, parts)

time: 112 us -> 114 us (1.018)
  waiting for transfers between devices: 38.9 us -> 46.8 us
  starting transfers between devices: 26.7 us -> 34.5 us
  other arithmetic: 4.93 us -> 0 us
  local copies, waits for them, and re-layouts: 5.62 us -> 1.58 us
  Pallas kernels: 33.8 us -> 30.3 us
    ppermute x0 -> x4, starting transfers between devices: none -> 16.8 us  [the longest x1 8.19 us: exchanged_windows(): far = lax.ppermute(own[2], 'depth', ring_route((0, 2), (3, 1)))]
    ppermute x0 -> x4, waiting for transfers between devices: none -> 7.37 us  [the longest x1 3.88 us: exchanged_windows(): relay = lax.ppermute(own[2], 'depth', ring_route((1, 0), (2, 3)))]
    convert_element_type x1 -> x0, other arithmetic: 4.92 us -> none  [build(): return (value * factor).astype(BF)]
    all_to_all x1 -> x0, starting transfers between devices: 4.05 us -> none  [shards(): probe = lax.all_to_all(column_pieces(ending), 'depth', 0, 0, tiled=True)]
    unnamed x25 -> x3, local copies, waits for them, and re-layouts: 4.85 us -> 0.8 us
    ppermute x6 -> x5, starting transfers between devices: 11.5 us -> 7.59 us  [turned(): return lax.ppermute(array, 'depth', route)]
    pallas_call x4, Pallas kernels: 14.1 us -> 10.8 us  [visit(): pl.pallas_call(functools.partial(visit_kernel, index), name=f'visit_{inde...]
    ppermute x6 -> x5, waiting for transfers between devices: 12.9 us -> 13 us  [turned(): return lax.ppermute(array, 'depth', route)]
  transfers between devices with their start and end apart: 13 -> 15, of which waited for: 7 -> 10; matrix products, arithmetic and copies ran while one was open for 4% -> 0% of each run, Pallas kernels for 16% -> 13%
where the time goes in v6:
time: 114 us
  waiting for transfers between devices  46.8 us (41%)
  starting transfers between devices  34.5 us (30%)
  Pallas kernels  30.3 us (27%)
  local copies, waits for them, and re-layouts  1.58 us (1%)
    ppermute x1, waiting for transfers between devices, shards(): lax.ppermute(leaving, 'depth', [(RING + i, i) for i in range(RING)])  14.4 us
    ppermute x5, waiting for transfers between devices, turned(): return lax.ppermute(array, 'depth', route)  13 us
    ppermute x5, waiting for transfers between devices, moved(): return lax.ppermute(array, 'probe', route)  12.1 us
    pallas_call x4, Pallas kernels, visit(): pl.pallas_call(functools.partial(visit_kernel, index), name=f'visit_{inde...  10.8 us
    pallas_call x2, Pallas kernels, run_chain(): pl.pallas_call(functools.partial(chain_kernel, first), name='chain_deep'...  9.46 us
    ppermute x5, starting transfers between devices, moved(): return lax.ppermute(array, 'probe', route)  8.76 us
    ppermute x1, starting transfers between devices, exchanged_windows(): far = lax.ppermute(own[2], 'depth', ring_route((0, 2), (3, 1)))  8.19 us
    ppermute x5, starting transfers between devices, turned(): return lax.ppermute(array, 'depth', route)  7.59 us
  transfers between devices with their start and end apart: 15, of which 10 were waited for; matrix products, arithmetic and copies ran while one was open for 0% of the time, Pallas kernels for 13%

profile of v6, /device:TPU:0, one launch (start us, length us, event | category | flops | bytes accessed | tf_op | source)
XLA Modules:
  0.0 114.0 jit_solution(11841795233542654993)
XLA Ops:
  0.6 0.0 copy-start
  0.7 0.8 copy.15.offsets
  1.5 0.1 stack.23.where
  1.6 3.7 %windows.1 = (bf16[2,2,256,256]{3,2,1,0:T(8,128)(2,1)S(1)}, bf16[2,2,256,256]{3,2,1,0:T(8,128)(2,1)S(1)}, bf16[2,2,256,256]{3,2,1,0:T(8,128)(2,1)S(1)}, bf16[2,2,256,256]{3,2,1,0:T(8,128)(2,1)S(1)}) custom-call(s32[5]{0:T(128)S(1)} %stack.23.where, s32[4,2]{1,0:T(4,128)S(1)} %copy.15.offsets, f32[2,384,384]{2,1,0:T(8,128)} %phase_all.1, f32[2,384,384]{2,1,0:T(8,128)} %amp_all.1), custom_call_target="tpu_custom_call" | custom-call | tf_op jit(solution)/shard_map/windows/pallas_call | solution.py:204
  5.3 1.3 %collective-permute-start.3 = (bf16[2,2,256,256]{3,2,1,0:T(8,128)(2,1)S(1)}, bf16[2,2,256,256]{3,2,1,0:T(8,128)(2,1)S(1)}, u32[]{:S(2)}, u32[]{:S(2)}) collective-permute-start(bf16[2,2,256,256]{3,2,1,0:T(8,128)(2,1)S(1)} %get-tuple-element.45.window), channel_id=1, source_target_pairs={{16,0},{32,48},{80,64},{96,112},{17,1},{33,49},{81,65},{97,113},{1... | collective-permute-start | bytes 1572872 | tf_op jit(solution)/shard_map/ppermute | solution.py:586
  6.6 8.2 %collective-permute-start.1 = (bf16[2,2,256,256]{3,2,1,0:T(8,128)(2,1)S(1)}, bf16[2,2,256,256]{3,2,1,0:T(8,128)(2,1)S(1)}, u32[]{:S(2)}, u32[]{:S(2)}) collective-permute-start(bf16[2,2,256,256]{3,2,1,0:T(8,128)(2,1)S(1)} %get-tuple-element.45.window), channel_id=1, source_target_pairs={{0,32},{48,16},{64,96},{112,80},{1,33},{49,17},{65,97},{113,81},{2... | collective-permute-start | bytes 1572872 | tf_op jit(solution)/shard_map/ppermute | solution.py:587
  14.8 0.1 collective-permute-start
  14.9 3.2 %collective-permute-start.2 = (bf16[2,2,256,256]{3,2,1,0:T(8,128)(2,1)S(1)}, bf16[2,2,256,256]{3,2,1,0:T(8,128)(2,1)S(1)}, u32[]{:S(2)}, u32[]{:S(2)}) collective-permute-start(bf16[2,2,256,256]{3,2,1,0:T(8,128)(2,1)S(1)} %get-tuple-element.46.window), channel_id=1, source_target_pairs={{0,48},{16,0},{32,16},{48,32},{64,112},{80,64},{96,80},{112,96},{1... | collective-permute-start | bytes 1572872 | tf_op jit(solution)/shard_map/ppermute | solution.py:574
  18.1 3.9 %collective-permute-done.3 = bf16[2,2,256,256]{3,2,1,0:T(8,128)(2,1)S(1)} collective-permute-done((bf16[2,2,256,256]{3,2,1,0:T(8,128)(2,1)S(1)}, bf16[2,2,256,256]{3,2,1,0:T(8,128)(2,1)S(1)}, u32[]{:S(2)}, u32[]{:S(2)}) %collective-permute-start.3) | collective-permute-done | bytes 524320 | tf_op jit(solution)/shard_map/ppermute | solution.py:586
  22.0 6.0 %collective-permute-start.4 = (bf16[2,2,256,256]{3,2,1,0:T(8,128)(2,1)S(1)}, bf16[2,2,256,256]{3,2,1,0:T(8,128)(2,1)S(1)}, u32[]{:S(2)}, u32[]{:S(2)}) collective-permute-start(bf16[2,2,256,256]{3,2,1,0:T(8,128)(2,1)S(1)} %collective-permute-done.3), channel_id=1, source_target_pairs={{0,48},{48,0},{64,112},{112,64},{1,49},{49,1},{65,113},{113,65},{2... | collective-permute-start | bytes 1572872 | tf_op jit(solution)/shard_map/ppermute | solution.py:590
  28.0 1.1 filters.1
  29.1 3.0 %reorder.1 = (bf16[512,256]{1,0:T(8,128)(2,1)S(1)}, bf16[2,2,256,256]{3,2,1,0:T(8,128)(2,1)S(1)}, bf16[2,2,256,256]{3,2,1,0:T(8,128)(2,1)S(1)}, bf16[2,2,256,256...) custom-call(s32[5]{0:T(128)S(1)} %stack.23.where, bf16[4,2,256,256]{3,2,1,0:T(8,128)(2,1)} %residual.1, ...), custom_call_target="tpu_custom_call" | custom-call | tf_op jit(solution)/shard_map/reorder/pallas_call | solution.py:551
  32.1 4.8 %collective-permute-done.rest_1_ = bf16[2,2,256,256]{3,2,1,0:T(8,128)(2,1)S(1)} collective-permute-done((bf16[2,2,256,256]{3,2,1,0:T(8,128)(2,1)S(1)}, bf16[2,2,256,256]{3,2,1,0:T(8,128)(2,1)S(1)}, u32[]{:S(2)}, u32[]{:S(2)}) %collective-permute-start) | collective-permute-done | bytes 524320 | tf_op jit(solution)/shard_map/ppermute | solution.py:574
  36.9 0.0 collective-permute-done.2.rest_3_
  36.9 0.0 collective-permute-done.1.rest_2_
  36.9 3.5 %collective-permute-done.4.rest_4_ = bf16[2,2,256,256]{3,2,1,0:T(8,128)(2,1)S(1)} collective-permute-done((bf16[2,2,256,256]{3,2,1,0:T(8,128)(2,1)S(1)}, bf16[2,2,256,256]{3,2,1,0:T(8,128)(2,1)S(1)}, u32[]{:S(2)}, u32[]{:S(2)}) %collective-permute-start.4) | collective-permute-done | bytes 524320 | tf_op jit(solution)/shard_map/ppermute | solution.py:590
  40.4 0.5 chain_deep.1
  41.0 1.3 %collective-permute-start.5 = (bf16[512,256]{1,0:T(8,128)(2,1)S(1)}, bf16[512,256]{1,0:T(8,128)(2,1)S(1)}, u32[]{:S(2)}, u32[]{:S(2)}) collective-permute-start(bf16[512,256]{1,0:T(8,128)(2,1)S(1)} %get-tuple-element.52), channel_id=1, source_target_pairs={{64,0},{80,16},{96,32},{112,48},{65,1},{81,17},{97,33},{113,49},{6... | collective-permute-start | bytes 786440 | tf_op jit(solution)/shard_map/ppermute | solution.py:604
  42.3 14.4 %collective-permute-done.5.start = bf16[512,256]{1,0:T(8,128)(2,1)S(1)} collective-permute-done((bf16[512,256]{1,0:T(8,128)(2,1)S(1)}, bf16[512,256]{1,0:T(8,128)(2,1)S(1)}, u32[]{:S(2)}, u32[]{:S(2)}) %collective-permute-start.5) | collective-permute-done | bytes 262176 | tf_op jit(solution)/shard_map/ppermute | solution.py:604
  56.7 8.9 %chain_top.1 = (bf16[640,256]{1,0:T(8,128)(2,1)S(1)}, bf16[640,256]{1,0:T(8,128)(2,1)S(1)}, bf16[640,256]{1,0:T(8,128)(2,1)S(1)}, bf16[640,256]{1,0:T(8,128)(2,1)S(1)}) custom-call(s32[5]{0:T(128)S(1)} %stack.23.where, bf16[512,256]{1,0:T(8,128)(2,1)S(1)} %collective-permute-done.5.start, bf16[2,2,256,256]{3,2,1,0:T(8,128)(2,1)S(1)} %get-tuple-element.43.rest_0_.window, ...), custom_call_target="tpu_custom_call" | custom-call | tf_op jit(solution)/shard_map/chain_top/pallas_call | solution.py:310
  65.6 2.7 %collective-permute-start.8 = (bf16[640,256]{1,0:T(8,128)(2,1)S(1)}, bf16[640,256]{1,0:T(8,128)(2,1)S(1)}, u32[]{:S(2)}, u32[]{:S(2)}) collective-permute-start(bf16[640,256]{1,0:T(8,128)(2,1)S(1)} %get-tuple-element.60), channel_id=1, source_target_pairs={{0,48},{16,0},{32,16},{48,32},{64,112},{80,64},{96,80},{112,96},{1... | collective-permute-start | bytes 983048 | tf_op jit(solution)/shard_map/ppermute | solution.py:574
  68.3 0.0 collective-permute-start.6
  68.3 1.5 %collective-permute-start.7 = (bf16[640,256]{1,0:T(8,128)(2,1)S(1)}, bf16[640,256]{1,0:T(8,128)(2,1)S(1)}, u32[]{:S(2)}, u32[]{:S(2)}) collective-permute-start(bf16[640,256]{1,0:T(8,128)(2,1)S(1)} %get-tuple-element.59), channel_id=1, source_target_pairs={{0,32},{16,48},{32,0},{48,16},{64,96},{80,112},{96,64},{112,80},{1... | collective-permute-start | bytes 983048 | tf_op jit(solution)/shard_map/ppermute | solution.py:574
  69.9 2.8 %visit_0.1.rest_5_ = f32[2,2,3,384,128]{4,3,2,1,0:T(8,128)S(1)} custom-call(s32[5]{0:T(128)S(1)} %stack.23.where, s32[4,2]{1,0:T(4,128)S(1)} %copy.15.offsets, bf16[640,256]{1,0:T(8,128)(2,1)S(1)} %get-tuple-element.67.entry.refs_0_, bf16[2,2,256,256]{3,2,1,0:T(8,128)(2,1)S(1)} %get-tuple-element.43.rest_0_.window, ...), custom_call_target="tpu_custom_call" | custom-call | tf_op jit(solution)/shard_map/visit_0/pallas_call | solution.py:373
  72.7 7.4 %collective-permute-done.8.entry.refs_3_ = bf16[640,256]{1,0:T(8,128)(2,1)S(1)} collective-permute-done((bf16[640,256]{1,0:T(8,128)(2,1)S(1)}, bf16[640,256]{1,0:T(8,128)(2,1)S(1)}, u32[]{:S(2)}, u32[]{:S(2)}) %collective-permute-start.8) | collective-permute-done | bytes 327712 | tf_op jit(solution)/shard_map/ppermute | solution.py:574
  80.1 2.7 %visit_3.1.rest_5_ = f32[2,2,3,384,128]{4,3,2,1,0:T(8,128)S(1)} custom-call(s32[5]{0:T(128)S(1)} %stack.23.where, s32[4,2]{1,0:T(4,128)S(1)} %copy.15.offsets, bf16[640,256]{1,0:T(8,128)(2,1)S(1)} %collective-permute-done.8.entry.refs_3_, bf16[2,2,256,256]{3,2,1,0:T(8,128)(2,1)S(1)} %get-tuple-element.44.window, ...), custom_call_target="tpu_custom_call", output_to_operand_aliasing={{}: (10, {})} | custom-call | tf_op jit(solution)/shard_map/visit_3/pallas_call | solution.py:373
  82.8 0.7 collective-permute-done.6.entry.refs_1_
  83.5 2.7 %visit_1.1.rest_5_ = f32[2,2,3,384,128]{4,3,2,1,0:T(8,128)S(1)} custom-call(s32[5]{0:T(128)S(1)} %stack.23.where, s32[4,2]{1,0:T(4,128)S(1)} %copy.15.offsets, bf16[640,256]{1,0:T(8,128)(2,1)S(1)} %collective-permute-done.6.entry.refs_1_, bf16[2,2,256,256]{3,2,1,0:T(8,128)(2,1)S(1)} %get-tuple-element.46.window, ...), custom_call_target="tpu_custom_call", output_to_operand_aliasing={{}: (10, {})} | custom-call | tf_op jit(solution)/shard_map/visit_1/pallas_call | solution.py:373
  86.2 0.0 collective-permute-done.7.entry.refs_2_
  86.2 1.3 %collective-permute-start.9 = (bf16[128,128]{1,0:T(8,128)(2,1)S(1)}, bf16[128,128]{1,0:T(8,128)(2,1)S(1)}, u32[]{:S(2)}, u32[]{:S(2)}) collective-permute-start(bf16[128,128]{1,0:T(8,128)(2,1)S(1)} %get-tuple-element.71), channel_id=1, source_target_pairs={{0,64},{16,80},{32,96},{48,112},{1,65},{17,81},{33,97},{49,113},{2... | collective-permute-start | bytes 98312 | tf_op jit(solution)/shard_map/ppermute | solution.py:611
  87.5 2.7 %visit_2.1.grads = f32[2,2,3,384,128]{4,3,2,1,0:T(8,128)S(1)} custom-call(s32[5]{0:T(128)S(1)} %stack.23.where, s32[4,2]{1,0:T(4,128)S(1)} %copy.15.offsets, bf16[640,256]{1,0:T(8,128)(2,1)S(1)} %collective-permute-done.7.entry.refs_2_, bf16[2,2,256,256]{3,2,1,0:T(8,128)(2,1)S(1)} %get-tuple-element.45.window, ...), custom_call_target="tpu_custom_call", output_to_operand_aliasing={{}: (10, {})} | custom-call | tf_op jit(solution)/shard_map/visit_2/pallas_call | solution.py:373
  90.2 0.0 collective-permute-done.9.far_probe
  90.2 0.7 pack.1
  90.9 0.1 collective-permute-start.10
  91.0 2.1 %collective-permute-done.10.arrived = bf16[4,2,112,384]{3,2,1,0:T(8,128)(2,1)S(1)} collective-permute-done((bf16[4,2,112,384]{3,2,1,0:T(8,128)(2,1)S(1)}, bf16[4,2,112,384]{3,2,1,0:T(8,128)(2,1)S(1)}, u32[]{:S(2)}, u32[]{:S(2)}) %collective-permute-start.10) | collective-permute-done | bytes 688160 | tf_op jit(solution)/shard_map/ppermute | solution.py:515
  93.2 0.2 core_sum.1
  93.4 1.6 %collective-permute-start.11 = (bf16[2,112,384]{2,1,0:T(8,128)(2,1)S(1)}, bf16[2,112,384]{2,1,0:T(8,128)(2,1)S(1)}, u32[]{:S(2)}, u32[]{:S(2)}) collective-permute-start(bf16[2,112,384]{2,1,0:T(8,128)(2,1)S(1)} %get-tuple-element.75), channel_id=1, source_target_pairs={{0,2},{1,3},{2,4},{3,5},{4,6},{5,7},{6,0},{7,1},{8,10},{9,11},{10,... | collective-permute-start | bytes 516104 | tf_op jit(solution)/shard_map/ppermute | solution.py:515
  95.0 2.9 %collective-permute-start.12 = (bf16[2,112,384]{2,1,0:T(8,128)(2,1)S(1)}, bf16[2,112,384]{2,1,0:T(8,128)(2,1)S(1)}, u32[]{:S(2)}, u32[]{:S(2)}) collective-permute-start(bf16[2,112,384]{2,1,0:T(8,128)(2,1)S(1)} %get-tuple-element.76), channel_id=1, source_target_pairs={{0,4},{1,5},{2,6},{3,7},{4,0},{5,1},{6,2},{7,3},{8,12},{9,13},{10,... | collective-permute-start | bytes 516104 | tf_op jit(solution)/shard_map/ppermute | solution.py:515
  97.8 1.4 %collective-permute-start.13 = (bf16[2,112,384]{2,1,0:T(8,128)(2,1)S(1)}, bf16[2,112,384]{2,1,0:T(8,128)(2,1)S(1)}, u32[]{:S(2)}, u32[]{:S(2)}) collective-permute-start(bf16[2,112,384]{2,1,0:T(8,128)(2,1)S(1)} %get-tuple-element.77), channel_id=1, source_target_pairs={{0,6},{1,7},{2,0},{3,1},{4,2},{5,3},{6,4},{7,5},{8,14},{9,15},{10,... | collective-permute-start | bytes 516104 | tf_op jit(solution)/shard_map/ppermute | solution.py:515
  99.2 1.8 %collective-permute-done.11.rest_1_ = bf16[2,112,384]{2,1,0:T(8,128)(2,1)S(1)} collective-permute-done((bf16[2,112,384]{2,1,0:T(8,128)(2,1)S(1)}, bf16[2,112,384]{2,1,0:T(8,128)(2,1)S(1)}, u32[]{:S(2)}, u32[]{:S(2)}) %collective-permute-start.11) | collective-permute-done | bytes 172064 | tf_op jit(solution)/shard_map/ppermute | solution.py:515
  101.0 4.8 %collective-permute-done.12.rest_2_ = bf16[2,112,384]{2,1,0:T(8,128)(2,1)S(1)} collective-permute-done((bf16[2,112,384]{2,1,0:T(8,128)(2,1)S(1)}, bf16[2,112,384]{2,1,0:T(8,128)(2,1)S(1)}, u32[]{:S(2)}, u32[]{:S(2)}) %collective-permute-start.12) | collective-permute-done | bytes 172064 | tf_op jit(solution)/shard_map/ppermute | solution.py:515
  105.9 0.0 collective-permute-done.13.rest_3_
  105.9 0.6 ring_sum.1
  106.5 2.8 %collective-permute-start.14 = (bf16[112,384]{1,0:T(8,128)(2,1)S(1)}, bf16[112,384]{1,0:T(8,128)(2,1)S(1)}, u32[]{:S(2)}, u32[]{:S(2)}) collective-permute-start(bf16[112,384]{1,0:T(8,128)(2,1)S(1)} %get-tuple-element.79), channel_id=1, source_target_pairs={{0,8},{1,9},{2,10},{3,11},{4,12},{5,13},{6,14},{7,15},{8,0},{9,1},... | collective-permute-start | bytes 258056 | tf_op jit(solution)/shard_map/ppermute | solution.py:515
  109.4 3.2 %collective-permute-done.14.arrived = bf16[112,384]{1,0:T(8,128)(2,1)S(1)} collective-permute-done((bf16[112,384]{1,0:T(8,128)(2,1)S(1)}, bf16[112,384]{1,0:T(8,128)(2,1)S(1)}, u32[]{:S(2)}, u32[]{:S(2)}) %collective-permute-start.14) | collective-permute-done | bytes 86048 | tf_op jit(solution)/shard_map/ppermute | solution.py:515
  112.6 0.7 last_sum.1
  113.3 0.1 reshape.14
  113.4 0.6 copy.16
  (2 shorter events, 0.0 us)
Async XLA Ops:
  0.6 27.4 %copy-start = (f32[256,256]{1,0:T(8,128)S(1)}, f32[256,256]{1,0:T(8,128)}, u32[]{:S(2)}) copy-start(f32[256,256]{1,0:T(8,128)} %phase.1) | copy-start | bytes 786436
  5.3 16.7 %collective-permute-start.3 = (bf16[2,2,256,256]{3,2,1,0:T(8,128)(2,1)S(1)}, bf16[2,2,256,256]{3,2,1,0:T(8,128)(2,1)S(1)}, u32[]{:S(2)}, u32[]{:S(2)}) collective-permute-start(bf16[2,2,256,256]{3,2,1,0:T(8,128)(2,1)S(1)} %get-tuple-element.45.window), channel_id=1, source_target_pairs={{16,0},{32,48},{80,64},{96,112},{17,1},{33,49},{81,65},{97,113},{1... | collective-permute-start | bytes 1572872 | tf_op jit(solution)/shard_map/ppermute | solution.py:586
  6.6 30.3 %collective-permute-start.1 = (bf16[2,2,256,256]{3,2,1,0:T(8,128)(2,1)S(1)}, bf16[2,2,256,256]{3,2,1,0:T(8,128)(2,1)S(1)}, u32[]{:S(2)}, u32[]{:S(2)}) collective-permute-start(bf16[2,2,256,256]{3,2,1,0:T(8,128)(2,1)S(1)} %get-tuple-element.45.window), channel_id=1, source_target_pairs={{0,32},{48,16},{64,96},{112,80},{1,33},{49,17},{65,97},{113,81},{2... | collective-permute-start | bytes 1572872 | tf_op jit(solution)/shard_map/ppermute | solution.py:587
  14.8 22.1 %collective-permute-start = (bf16[2,2,256,256]{3,2,1,0:T(8,128)(2,1)S(1)}, bf16[2,2,256,256]{3,2,1,0:T(8,128)(2,1)S(1)}, u32[]{:S(2)}, u32[]{:S(2)}) collective-permute-start(bf16[2,2,256,256]{3,2,1,0:T(8,128)(2,1)S(1)} %get-tuple-element.44.window), channel_id=1, source_target_pairs={{0,16},{16,32},{32,48},{48,0},{64,80},{80,96},{96,112},{112,64},{1... | collective-permute-start | bytes 1572872 | tf_op jit(solution)/shard_map/ppermute | solution.py:574
  14.9 22.1 %collective-permute-start.2 = (bf16[2,2,256,256]{3,2,1,0:T(8,128)(2,1)S(1)}, bf16[2,2,256,256]{3,2,1,0:T(8,128)(2,1)S(1)}, u32[]{:S(2)}, u32[]{:S(2)}) collective-permute-start(bf16[2,2,256,256]{3,2,1,0:T(8,128)(2,1)S(1)} %get-tuple-element.46.window), channel_id=1, source_target_pairs={{0,48},{16,0},{32,16},{48,32},{64,112},{80,64},{96,80},{112,96},{1... | collective-permute-start | bytes 1572872 | tf_op jit(solution)/shard_map/ppermute | solution.py:574
  22.0 18.4 %collective-permute-start.4 = (bf16[2,2,256,256]{3,2,1,0:T(8,128)(2,1)S(1)}, bf16[2,2,256,256]{3,2,1,0:T(8,128)(2,1)S(1)}, u32[]{:S(2)}, u32[]{:S(2)}) collective-permute-start(bf16[2,2,256,256]{3,2,1,0:T(8,128)(2,1)S(1)} %collective-permute-done.3), channel_id=1, source_target_pairs={{0,48},{48,0},{64,112},{112,64},{1,49},{49,1},{65,113},{113,65},{2... | collective-permute-start | bytes 1572872 | tf_op jit(solution)/shard_map/ppermute | solution.py:590
  41.0 15.7 %collective-permute-start.5 = (bf16[512,256]{1,0:T(8,128)(2,1)S(1)}, bf16[512,256]{1,0:T(8,128)(2,1)S(1)}, u32[]{:S(2)}, u32[]{:S(2)}) collective-permute-start(bf16[512,256]{1,0:T(8,128)(2,1)S(1)} %get-tuple-element.52), channel_id=1, source_target_pairs={{64,0},{80,16},{96,32},{112,48},{65,1},{81,17},{97,33},{113,49},{6... | collective-permute-start | bytes 786440 | tf_op jit(solution)/shard_map/ppermute | solution.py:604
  65.6 14.5 %collective-permute-start.8 = (bf16[640,256]{1,0:T(8,128)(2,1)S(1)}, bf16[640,256]{1,0:T(8,128)(2,1)S(1)}, u32[]{:S(2)}, u32[]{:S(2)}) collective-permute-start(bf16[640,256]{1,0:T(8,128)(2,1)S(1)} %get-tuple-element.60), channel_id=1, source_target_pairs={{0,48},{16,0},{32,16},{48,32},{64,112},{80,64},{96,80},{112,96},{1... | collective-permute-start | bytes 983048 | tf_op jit(solution)/shard_map/ppermute | solution.py:574
  68.3 15.2 %collective-permute-start.6 = (bf16[640,256]{1,0:T(8,128)(2,1)S(1)}, bf16[640,256]{1,0:T(8,128)(2,1)S(1)}, u32[]{:S(2)}, u32[]{:S(2)}) collective-permute-start(bf16[640,256]{1,0:T(8,128)(2,1)S(1)} %get-tuple-element.58), channel_id=1, source_target_pairs={{0,16},{16,32},{32,48},{48,0},{64,80},{80,96},{96,112},{112,64},{1... | collective-permute-start | bytes 983048 | tf_op jit(solution)/shard_map/ppermute | solution.py:574
  68.3 17.8 %collective-permute-start.7 = (bf16[640,256]{1,0:T(8,128)(2,1)S(1)}, bf16[640,256]{1,0:T(8,128)(2,1)S(1)}, u32[]{:S(2)}, u32[]{:S(2)}) collective-permute-start(bf16[640,256]{1,0:T(8,128)(2,1)S(1)} %get-tuple-element.59), channel_id=1, source_target_pairs={{0,32},{16,48},{32,0},{48,16},{64,96},{80,112},{96,64},{112,80},{1... | collective-permute-start | bytes 983048 | tf_op jit(solution)/shard_map/ppermute | solution.py:574
  86.2 4.0 %collective-permute-start.9 = (bf16[128,128]{1,0:T(8,128)(2,1)S(1)}, bf16[128,128]{1,0:T(8,128)(2,1)S(1)}, u32[]{:S(2)}, u32[]{:S(2)}) collective-permute-start(bf16[128,128]{1,0:T(8,128)(2,1)S(1)} %get-tuple-element.71), channel_id=1, source_target_pairs={{0,64},{16,80},{32,96},{48,112},{1,65},{17,81},{33,97},{49,113},{2... | collective-permute-start | bytes 98312 | tf_op jit(solution)/shard_map/ppermute | solution.py:611
  90.9 2.2 %collective-permute-start.10 = (bf16[4,2,112,384]{3,2,1,0:T(8,128)(2,1)S(1)}, bf16[4,2,112,384]{3,2,1,0:T(8,128)(2,1)S(1)}, u32[]{:S(2)}, u32[]{:S(2)}) collective-permute-start(bf16[4,2,112,384]{3,2,1,0:T(8,128)(2,1)S(1)} %get-tuple-element.73), channel_id=1, source_target_pairs={{0,1},{1,0},{2,3},{3,2},{4,5},{5,4},{6,7},{7,6},{8,9},{9,8},{10,11... | collective-permute-start | bytes 2064392 | tf_op jit(solution)/shard_map/ppermute | solution.py:515
  93.4 7.7 %collective-permute-start.11 = (bf16[2,112,384]{2,1,0:T(8,128)(2,1)S(1)}, bf16[2,112,384]{2,1,0:T(8,128)(2,1)S(1)}, u32[]{:S(2)}, u32[]{:S(2)}) collective-permute-start(bf16[2,112,384]{2,1,0:T(8,128)(2,1)S(1)} %get-tuple-element.75), channel_id=1, source_target_pairs={{0,2},{1,3},{2,4},{3,5},{4,6},{5,7},{6,0},{7,1},{8,10},{9,11},{10,... | collective-permute-start | bytes 516104 | tf_op jit(solution)/shard_map/ppermute | solution.py:515
  95.0 10.9 %collective-permute-start.12 = (bf16[2,112,384]{2,1,0:T(8,128)(2,1)S(1)}, bf16[2,112,384]{2,1,0:T(8,128)(2,1)S(1)}, u32[]{:S(2)}, u32[]{:S(2)}) collective-permute-start(bf16[2,112,384]{2,1,0:T(8,128)(2,1)S(1)} %get-tuple-element.76), channel_id=1, source_target_pairs={{0,4},{1,5},{2,6},{3,7},{4,0},{5,1},{6,2},{7,3},{8,12},{9,13},{10,... | collective-permute-start | bytes 516104 | tf_op jit(solution)/shard_map/ppermute | solution.py:515
  97.8 8.1 %collective-permute-start.13 = (bf16[2,112,384]{2,1,0:T(8,128)(2,1)S(1)}, bf16[2,112,384]{2,1,0:T(8,128)(2,1)S(1)}, u32[]{:S(2)}, u32[]{:S(2)}) collective-permute-start(bf16[2,112,384]{2,1,0:T(8,128)(2,1)S(1)} %get-tuple-element.77), channel_id=1, source_target_pairs={{0,6},{1,7},{2,0},{3,1},{4,2},{5,3},{6,4},{7,5},{8,14},{9,15},{10,... | collective-permute-start | bytes 516104 | tf_op jit(solution)/shard_map/ppermute | solution.py:515
  106.5 6.1 %collective-permute-start.14 = (bf16[112,384]{1,0:T(8,128)(2,1)S(1)}, bf16[112,384]{1,0:T(8,128)(2,1)S(1)}, u32[]{:S(2)}, u32[]{:S(2)}) collective-permute-start(bf16[112,384]{1,0:T(8,128)(2,1)S(1)} %get-tuple-element.79), channel_id=1, source_target_pairs={{0,8},{1,9},{2,10},{3,11},{4,12},{5,13},{6,14},{7,15},{8,0},{9,1},... | collective-permute-start | bytes 258056 | tf_op jit(solution)/shard_map/ppermute | solution.py:515

commit v7 on v6

--- a/solution.py
+++ b/solution.py
@@ -233,15 +233,14 @@
 
 def chain_kernel(first, where, start, *rest):
     count = RING + 1 if first else RING
-    windows = rest[: RING + 1]
-    earlier = () if first else rest[RING + 1 : 2 * RING + 1]
-    rest = rest[RING + 1 + len(earlier) :]
+    windows = rest[:RING]
+    earlier = () if first else rest[RING : 2 * RING]
+    rest = rest[RING + len(earlier) :]
     tables = rest[:5]
     outs = rest[5 : 5 + count]
     trans, waves, middle, mixed, filtered, second = rest[5 + count :]
     rank = where[0]
     active = where[1] == 1 if first else where[1] == 0
-    inner = jnp.logical_or(rank == 1, rank == 2)
 
     @pl.when(active)
     def _():
@@ -266,12 +265,9 @@
 
                 def ready(layer=layer):
                     distance = (rank + RING - pair_at) % RING
-                    index = jnp.where(
-                        jnp.logical_and(distance == 2, jnp.logical_not(inner)), RING, distance
-                    )
-                    for k in range(RING + 1):
-
-                        @pl.when(index == k)
+                    for k in range(RING):
+
+                        @pl.when(distance == k)
                         def _(k=k):
                             for parity in (0, 1):
                                 trans[parity] = windows[k][layer, parity]
@@ -311,7 +307,7 @@
         functools.partial(chain_kernel, first),
         name="chain_deep" if first else "chain_top",
         out_shape=[wave] * count,
-        in_specs=[SM] + [VM] * (RING + 7 + len(earlier)),
+        in_specs=[SM] + [VM] * (RING + 6 + len(earlier)),
         out_specs=[VM] * count,
         scratch_shapes=[
             pltpu.VMEM((2, N, N), BF),
@@ -578,18 +574,6 @@
     return [arrays[0]] + [turned(arrays[k], k) for k in range(1, RING)]
 
 
-def ring_route(*pairs):
-    return [(RING * ring + a, RING * ring + b) for ring in range(2) for a, b in pairs]
-
-
-def exchanged_windows(own):
-    relay = lax.ppermute(own[2], "depth", ring_route((1, 0), (2, 3)))
-    far = lax.ppermute(own[2], "depth", ring_route((0, 2), (3, 1)))
-    ahead = turned(own[1], 1)
-    back = turned(own[3], 3)
-    return [own[0], ahead, far, back, lax.ppermute(relay, "depth", ring_route((0, 3), (3, 0)))]
-
-
 def shards(residual, saved_waves, object_phase, object_amp, prop_phase, offsets):
     depth_at = lax.axis_index("depth")
     probe_at = lax.axis_index("probe")
@@ -599,7 +583,7 @@
     own = transmission_windows(where, offsets, object_phase, object_amp)
     tables = filters(prop_phase)
     start, *waves = row_parity_first(where, residual, saved_waves)
-    foreign = exchanged_windows(own)
+    foreign = exchanged(own)
     *deep, leaving = run_chain(True, where, start, foreign, (), tables)
     arrived = lax.ppermute(leaving, "depth", [(RING + i, i) for i in range(RING)])
     entries = exchanged(run_chain(False, where, arrived, foreign, deep, tables))

time: 114 us -> 111 us (0.974)
  starting transfers between devices: 34.5 us -> 22.8 us
  waiting for transfers between devices: 46.8 us -> 54.9 us
    ppermute x3 -> x0, starting transfers between devices: 15.5 us -> none  [the longest x1 8.19 us: exchanged_windows(): far = lax.ppermute(own[2], 'depth', ring_route((0, 2), (3, 1)))]
    ppermute x5 -> x6, waiting for transfers between devices: 13 us -> 27.8 us  [turned(): return lax.ppermute(array, 'depth', route)]
    ppermute x3 -> x0, waiting for transfers between devices: 7.37 us -> none  [the longest x1 3.88 us: exchanged_windows(): relay = lax.ppermute(own[2], 'depth', ring_route((1, 0), (2, 3)))]
    ppermute x5 -> x6, starting transfers between devices: 7.59 us -> 11.5 us  [turned(): return lax.ppermute(array, 'depth', route)]
  transfers between devices with their start and end apart: 15 -> 13, of which waited for: 10 -> 9; matrix products, arithmetic and copies ran while one was open for 0% -> 0% of each run, Pallas kernels for 13% -> 13%
where the time goes in v7:
time: 111 us; the launch traced here: 110 us
  waiting for transfers between devices  54.9 us (49%)
  Pallas kernels  30.3 us (27%)
  starting transfers between devices  22.8 us (21%)
  local copies, waits for them, and re-layouts  1.58 us (1%)
    ppermute x6, waiting for transfers between devices, turned(): return lax.ppermute(array, 'depth', route)  27.8 us
    ppermute x1, waiting for transfers between devices, shards(): lax.ppermute(leaving, 'depth', [(RING + i, i) for i in range(RING)])  14.9 us
    ppermute x5, waiting for transfers between devices, moved(): return lax.ppermute(array, 'probe', route)  12.1 us
    ppermute x6, starting transfers between devices, turned(): return lax.ppermute(array, 'depth', route)  11.5 us
    pallas_call x4, Pallas kernels, visit(): pl.pallas_call(functools.partial(visit_kernel, index), name=f'visit_{inde...  10.8 us
    pallas_call x2, Pallas kernels, run_chain(): pl.pallas_call(functools.partial(chain_kernel, first), name='chain_deep'...  9.45 us
    ppermute x5, starting transfers between devices, moved(): return lax.ppermute(array, 'probe', route)  8.77 us
    pallas_call x1, Pallas kernels, transmission_windows(): pl.pallas_call(window_kernel, name='windows', out_shape=[shape] * RING, i...  3.7 us
  transfers between devices with their start and end apart: 13, of which 9 were waited for; matrix products, arithmetic and copies ran while one was open for 0% of the time, Pallas kernels for 13%

profile of v7, /device:TPU:0, one launch (start us, length us, event | category | flops | bytes accessed | tf_op | source)
XLA Modules:
  0.0 110.4 jit_solution(16203332337548539787)
XLA Ops:
  0.6 0.0 copy-start
  0.7 0.8 copy.15.offsets
  1.5 0.1 stack.23.where
  1.6 3.7 %windows.1 = (bf16[2,2,256,256]{3,2,1,0:T(8,128)(2,1)S(1)}, bf16[2,2,256,256]{3,2,1,0:T(8,128)(2,1)S(1)}, bf16[2,2,256,256]{3,2,1,0:T(8,128)(2,1)S(1)}, bf16[2,2,256,256]{3,2,1,0:T(8,128)(2,1)S(1)}) custom-call(s32[5]{0:T(128)S(1)} %stack.23.where, s32[4,2]{1,0:T(4,128)S(1)} %copy.15.offsets, f32[2,384,384]{2,1,0:T(8,128)} %phase_all.1, f32[2,384,384]{2,1,0:T(8,128)} %amp_all.1), custom_call_target="tpu_custom_call" | custom-call | tf_op jit(solution)/shard_map/windows/pallas_call | solution.py:204
  5.3 2.1 %collective-permute-start = (bf16[2,2,256,256]{3,2,1,0:T(8,128)(2,1)S(1)}, bf16[2,2,256,256]{3,2,1,0:T(8,128)(2,1)S(1)}, u32[]{:S(2)}, u32[]{:S(2)}) collective-permute-start(bf16[2,2,256,256]{3,2,1,0:T(8,128)(2,1)S(1)} %get-tuple-element.44.window), channel_id=1, source_target_pairs={{0,16},{16,32},{32,48},{48,0},{64,80},{80,96},{96,112},{112,64},{1... | collective-permute-start | bytes 1572872 | tf_op jit(solution)/shard_map/ppermute | solution.py:570
  7.4 3.6 %collective-permute-start.1 = (bf16[2,2,256,256]{3,2,1,0:T(8,128)(2,1)S(1)}, bf16[2,2,256,256]{3,2,1,0:T(8,128)(2,1)S(1)}, u32[]{:S(2)}, u32[]{:S(2)}) collective-permute-start(bf16[2,2,256,256]{3,2,1,0:T(8,128)(2,1)S(1)} %get-tuple-element.45.window), channel_id=1, source_target_pairs={{0,32},{16,48},{32,0},{48,16},{64,96},{80,112},{96,64},{112,80},{1... | collective-permute-start | bytes 1572872 | tf_op jit(solution)/shard_map/ppermute | solution.py:570
  11.0 1.0 collective-permute-start.2
  12.0 0.0 copy-done
  12.0 1.1 filters.1
  13.0 3.0 %reorder.1 = (bf16[512,256]{1,0:T(8,128)(2,1)S(1)}, bf16[2,2,256,256]{3,2,1,0:T(8,128)(2,1)S(1)}, bf16[2,2,256,256]{3,2,1,0:T(8,128)(2,1)S(1)}, bf16[2,2,256,256...) custom-call(s32[5]{0:T(128)S(1)} %stack.23.where, bf16[4,2,256,256]{3,2,1,0:T(8,128)(2,1)} %residual.1, ...), custom_call_target="tpu_custom_call" | custom-call | tf_op jit(solution)/shard_map/reorder/pallas_call | solution.py:547
  16.0 5.4 %collective-permute-done.rest_1_ = bf16[2,2,256,256]{3,2,1,0:T(8,128)(2,1)S(1)} collective-permute-done((bf16[2,2,256,256]{3,2,1,0:T(8,128)(2,1)S(1)}, bf16[2,2,256,256]{3,2,1,0:T(8,128)(2,1)S(1)}, u32[]{:S(2)}, u32[]{:S(2)}) %collective-permute-start) | collective-permute-done | bytes 524320 | tf_op jit(solution)/shard_map/ppermute | solution.py:570
  21.4 12.4 %collective-permute-done.1.rest_2_ = bf16[2,2,256,256]{3,2,1,0:T(8,128)(2,1)S(1)} collective-permute-done((bf16[2,2,256,256]{3,2,1,0:T(8,128)(2,1)S(1)}, bf16[2,2,256,256]{3,2,1,0:T(8,128)(2,1)S(1)}, u32[]{:S(2)}, u32[]{:S(2)}) %collective-permute-start.1) | collective-permute-done | bytes 524320 | tf_op jit(solution)/shard_map/ppermute | solution.py:570
  33.8 0.0 collective-permute-done.2.rest_3_
  33.8 0.5 chain_deep.1
  34.4 1.3 %collective-permute-start.3 = (bf16[512,256]{1,0:T(8,128)(2,1)S(1)}, bf16[512,256]{1,0:T(8,128)(2,1)S(1)}, u32[]{:S(2)}, u32[]{:S(2)}) collective-permute-start(bf16[512,256]{1,0:T(8,128)(2,1)S(1)} %get-tuple-element.52), channel_id=1, source_target_pairs={{64,0},{80,16},{96,32},{112,48},{65,1},{81,17},{97,33},{113,49},{6... | collective-permute-start | bytes 786440 | tf_op jit(solution)/shard_map/ppermute | solution.py:588
  35.7 14.9 %collective-permute-done.3.start = bf16[512,256]{1,0:T(8,128)(2,1)S(1)} collective-permute-done((bf16[512,256]{1,0:T(8,128)(2,1)S(1)}, bf16[512,256]{1,0:T(8,128)(2,1)S(1)}, u32[]{:S(2)}, u32[]{:S(2)}) %collective-permute-start.3) | collective-permute-done | bytes 262176 | tf_op jit(solution)/shard_map/ppermute | solution.py:588
  50.6 8.9 %chain_top.1 = (bf16[640,256]{1,0:T(8,128)(2,1)S(1)}, bf16[640,256]{1,0:T(8,128)(2,1)S(1)}, bf16[640,256]{1,0:T(8,128)(2,1)S(1)}, bf16[640,256]{1,0:T(8,128)(2,1)S(1)}) custom-call(s32[5]{0:T(128)S(1)} %stack.23.where, bf16[512,256]{1,0:T(8,128)(2,1)S(1)} %collective-permute-done.3.start, bf16[2,2,256,256]{3,2,1,0:T(8,128)(2,1)S(1)} %get-tuple-element.43.rest_0_.window, ...), custom_call_target="tpu_custom_call" | custom-call | tf_op jit(solution)/shard_map/chain_top/pallas_call | solution.py:306
  59.5 3.2 %collective-permute-start.6 = (bf16[640,256]{1,0:T(8,128)(2,1)S(1)}, bf16[640,256]{1,0:T(8,128)(2,1)S(1)}, u32[]{:S(2)}, u32[]{:S(2)}) collective-permute-start(bf16[640,256]{1,0:T(8,128)(2,1)S(1)} %get-tuple-element.60), channel_id=1, source_target_pairs={{0,48},{16,0},{32,16},{48,32},{64,112},{80,64},{96,80},{112,96},{1... | collective-permute-start | bytes 983048 | tf_op jit(solution)/shard_map/ppermute | solution.py:570
  62.8 0.0 collective-permute-start.4
  62.8 1.5 %collective-permute-start.5 = (bf16[640,256]{1,0:T(8,128)(2,1)S(1)}, bf16[640,256]{1,0:T(8,128)(2,1)S(1)}, u32[]{:S(2)}, u32[]{:S(2)}) collective-permute-start(bf16[640,256]{1,0:T(8,128)(2,1)S(1)} %get-tuple-element.59), channel_id=1, source_target_pairs={{0,32},{16,48},{32,0},{48,16},{64,96},{80,112},{96,64},{112,80},{1... | collective-permute-start | bytes 983048 | tf_op jit(solution)/shard_map/ppermute | solution.py:570
  64.3 2.8 %visit_0.1.rest_5_ = f32[2,2,3,384,128]{4,3,2,1,0:T(8,128)S(1)} custom-call(s32[5]{0:T(128)S(1)} %stack.23.where, s32[4,2]{1,0:T(4,128)S(1)} %copy.15.offsets, bf16[640,256]{1,0:T(8,128)(2,1)S(1)} %get-tuple-element.67.entry.refs_0_, bf16[2,2,256,256]{3,2,1,0:T(8,128)(2,1)S(1)} %get-tuple-element.43.rest_0_.window, ...), custom_call_target="tpu_custom_call" | custom-call | tf_op jit(solution)/shard_map/visit_0/pallas_call | solution.py:369
  67.1 9.3 %collective-permute-done.6.entry.refs_3_ = bf16[640,256]{1,0:T(8,128)(2,1)S(1)} collective-permute-done((bf16[640,256]{1,0:T(8,128)(2,1)S(1)}, bf16[640,256]{1,0:T(8,128)(2,1)S(1)}, u32[]{:S(2)}, u32[]{:S(2)}) %collective-permute-start.6) | collective-permute-done | bytes 327712 | tf_op jit(solution)/shard_map/ppermute | solution.py:570
  76.4 2.7 %visit_3.1.rest_5_ = f32[2,2,3,384,128]{4,3,2,1,0:T(8,128)S(1)} custom-call(s32[5]{0:T(128)S(1)} %stack.23.where, s32[4,2]{1,0:T(4,128)S(1)} %copy.15.offsets, bf16[640,256]{1,0:T(8,128)(2,1)S(1)} %collective-permute-done.6.entry.refs_3_, bf16[2,2,256,256]{3,2,1,0:T(8,128)(2,1)S(1)} %get-tuple-element.44.window, ...), custom_call_target="tpu_custom_call", output_to_operand_aliasing={{}: (10, {})} | custom-call | tf_op jit(solution)/shard_map/visit_3/pallas_call | solution.py:369
  79.1 0.7 collective-permute-done.4.entry.refs_1_
  79.8 2.7 %visit_1.1.rest_5_ = f32[2,2,3,384,128]{4,3,2,1,0:T(8,128)S(1)} custom-call(s32[5]{0:T(128)S(1)} %stack.23.where, s32[4,2]{1,0:T(4,128)S(1)} %copy.15.offsets, bf16[640,256]{1,0:T(8,128)(2,1)S(1)} %collective-permute-done.4.entry.refs_1_, bf16[2,2,256,256]{3,2,1,0:T(8,128)(2,1)S(1)} %get-tuple-element.46.window, ...), custom_call_target="tpu_custom_call", output_to_operand_aliasing={{}: (10, {})} | custom-call | tf_op jit(solution)/shard_map/visit_1/pallas_call | solution.py:369
  82.5 0.0 collective-permute-done.5.entry.refs_2_
  82.5 1.3 %collective-permute-start.7 = (bf16[128,128]{1,0:T(8,128)(2,1)S(1)}, bf16[128,128]{1,0:T(8,128)(2,1)S(1)}, u32[]{:S(2)}, u32[]{:S(2)}) collective-permute-start(bf16[128,128]{1,0:T(8,128)(2,1)S(1)} %get-tuple-element.71), channel_id=1, source_target_pairs={{0,64},{16,80},{32,96},{48,112},{1,65},{17,81},{33,97},{49,113},{2... | collective-permute-start | bytes 98312 | tf_op jit(solution)/shard_map/ppermute | solution.py:595
  83.8 2.7 %visit_2.1.grads = f32[2,2,3,384,128]{4,3,2,1,0:T(8,128)S(1)} custom-call(s32[5]{0:T(128)S(1)} %stack.23.where, s32[4,2]{1,0:T(4,128)S(1)} %copy.15.offsets, bf16[640,256]{1,0:T(8,128)(2,1)S(1)} %collective-permute-done.5.entry.refs_2_, bf16[2,2,256,256]{3,2,1,0:T(8,128)(2,1)S(1)} %get-tuple-element.45.window, ...), custom_call_target="tpu_custom_call", output_to_operand_aliasing={{}: (10, {})} | custom-call | tf_op jit(solution)/shard_map/visit_2/pallas_call | solution.py:369
  86.5 0.0 collective-permute-done.7.far_probe
  86.5 0.7 pack.1
  87.3 0.1 collective-permute-start.8
  87.3 2.1 %collective-permute-done.8.arrived = bf16[4,2,112,384]{3,2,1,0:T(8,128)(2,1)S(1)} collective-permute-done((bf16[4,2,112,384]{3,2,1,0:T(8,128)(2,1)S(1)}, bf16[4,2,112,384]{3,2,1,0:T(8,128)(2,1)S(1)}, u32[]{:S(2)}, u32[]{:S(2)}) %collective-permute-start.8) | collective-permute-done | bytes 688160 | tf_op jit(solution)/shard_map/ppermute | solution.py:511
  89.5 0.2 core_sum.1
  89.7 1.7 %collective-permute-start.9 = (bf16[2,112,384]{2,1,0:T(8,128)(2,1)S(1)}, bf16[2,112,384]{2,1,0:T(8,128)(2,1)S(1)}, u32[]{:S(2)}, u32[]{:S(2)}) collective-permute-start(bf16[2,112,384]{2,1,0:T(8,128)(2,1)S(1)} %get-tuple-element.75), channel_id=1, source_target_pairs={{0,2},{1,3},{2,4},{3,5},{4,6},{5,7},{6,0},{7,1},{8,10},{9,11},{10,... | collective-permute-start | bytes 516104 | tf_op jit(solution)/shard_map/ppermute | solution.py:511
  91.3 2.9 %collective-permute-start.10 = (bf16[2,112,384]{2,1,0:T(8,128)(2,1)S(1)}, bf16[2,112,384]{2,1,0:T(8,128)(2,1)S(1)}, u32[]{:S(2)}, u32[]{:S(2)}) collective-permute-start(bf16[2,112,384]{2,1,0:T(8,128)(2,1)S(1)} %get-tuple-element.76), channel_id=1, source_target_pairs={{0,4},{1,5},{2,6},{3,7},{4,0},{5,1},{6,2},{7,3},{8,12},{9,13},{10,... | collective-permute-start | bytes 516104 | tf_op jit(solution)/shard_map/ppermute | solution.py:511
  94.2 1.3 %collective-permute-start.11 = (bf16[2,112,384]{2,1,0:T(8,128)(2,1)S(1)}, bf16[2,112,384]{2,1,0:T(8,128)(2,1)S(1)}, u32[]{:S(2)}, u32[]{:S(2)}) collective-permute-start(bf16[2,112,384]{2,1,0:T(8,128)(2,1)S(1)} %get-tuple-element.77), channel_id=1, source_target_pairs={{0,6},{1,7},{2,0},{3,1},{4,2},{5,3},{6,4},{7,5},{8,14},{9,15},{10,... | collective-permute-start | bytes 516104 | tf_op jit(solution)/shard_map/ppermute | solution.py:511
  95.6 1.9 %collective-permute-done.9.rest_1_ = bf16[2,112,384]{2,1,0:T(8,128)(2,1)S(1)} collective-permute-done((bf16[2,112,384]{2,1,0:T(8,128)(2,1)S(1)}, bf16[2,112,384]{2,1,0:T(8,128)(2,1)S(1)}, u32[]{:S(2)}, u32[]{:S(2)}) %collective-permute-start.9) | collective-permute-done | bytes 172064 | tf_op jit(solution)/shard_map/ppermute | solution.py:511
  97.4 4.9 %collective-permute-done.10.rest_2_ = bf16[2,112,384]{2,1,0:T(8,128)(2,1)S(1)} collective-permute-done((bf16[2,112,384]{2,1,0:T(8,128)(2,1)S(1)}, bf16[2,112,384]{2,1,0:T(8,128)(2,1)S(1)}, u32[]{:S(2)}, u32[]{:S(2)}) %collective-permute-start.10) | collective-permute-done | bytes 172064 | tf_op jit(solution)/shard_map/ppermute | solution.py:511
  102.3 0.0 collective-permute-done.11.rest_3_
  102.3 0.6 ring_sum.1
  102.9 2.8 %collective-permute-start.12 = (bf16[112,384]{1,0:T(8,128)(2,1)S(1)}, bf16[112,384]{1,0:T(8,128)(2,1)S(1)}, u32[]{:S(2)}, u32[]{:S(2)}) collective-permute-start(bf16[112,384]{1,0:T(8,128)(2,1)S(1)} %get-tuple-element.79), channel_id=1, source_target_pairs={{0,8},{1,9},{2,10},{3,11},{4,12},{5,13},{6,14},{7,15},{8,0},{9,1},... | collective-permute-start | bytes 258056 | tf_op jit(solution)/shard_map/ppermute | solution.py:511
  105.7 3.3 %collective-permute-done.12.arrived = bf16[112,384]{1,0:T(8,128)(2,1)S(1)} collective-permute-done((bf16[112,384]{1,0:T(8,128)(2,1)S(1)}, bf16[112,384]{1,0:T(8,128)(2,1)S(1)}, u32[]{:S(2)}, u32[]{:S(2)}) %collective-permute-start.12) | collective-permute-done | bytes 86048 | tf_op jit(solution)/shard_map/ppermute | solution.py:511
  109.0 0.7 last_sum.1
  109.7 0.1 reshape.14
  109.8 0.6 copy.16
  (1 shorter events, 0.0 us)
Async XLA Ops:
  0.6 11.3 %copy-start = (f32[256,256]{1,0:T(8,128)S(1)}, f32[256,256]{1,0:T(8,128)}, u32[]{:S(2)}) copy-start(f32[256,256]{1,0:T(8,128)} %phase.1) | copy-start | bytes 786436
  5.3 16.1 %collective-permute-start = (bf16[2,2,256,256]{3,2,1,0:T(8,128)(2,1)S(1)}, bf16[2,2,256,256]{3,2,1,0:T(8,128)(2,1)S(1)}, u32[]{:S(2)}, u32[]{:S(2)}) collective-permute-start(bf16[2,2,256,256]{3,2,1,0:T(8,128)(2,1)S(1)} %get-tuple-element.44.window), channel_id=1, source_target_pairs={{0,16},{16,32},{32,48},{48,0},{64,80},{80,96},{96,112},{112,64},{1... | collective-permute-start | bytes 1572872 | tf_op jit(solution)/shard_map/ppermute | solution.py:570
  7.4 26.5 %collective-permute-start.1 = (bf16[2,2,256,256]{3,2,1,0:T(8,128)(2,1)S(1)}, bf16[2,2,256,256]{3,2,1,0:T(8,128)(2,1)S(1)}, u32[]{:S(2)}, u32[]{:S(2)}) collective-permute-start(bf16[2,2,256,256]{3,2,1,0:T(8,128)(2,1)S(1)} %get-tuple-element.45.window), channel_id=1, source_target_pairs={{0,32},{16,48},{32,0},{48,16},{64,96},{80,112},{96,64},{112,80},{1... | collective-permute-start | bytes 1572872 | tf_op jit(solution)/shard_map/ppermute | solution.py:570
  11.0 22.9 %collective-permute-start.2 = (bf16[2,2,256,256]{3,2,1,0:T(8,128)(2,1)S(1)}, bf16[2,2,256,256]{3,2,1,0:T(8,128)(2,1)S(1)}, u32[]{:S(2)}, u32[]{:S(2)}) collective-permute-start(bf16[2,2,256,256]{3,2,1,0:T(8,128)(2,1)S(1)} %get-tuple-element.46.window), channel_id=1, source_target_pairs={{0,48},{16,0},{32,16},{48,32},{64,112},{80,64},{96,80},{112,96},{1... | collective-permute-start | bytes 1572872 | tf_op jit(solution)/shard_map/ppermute | solution.py:570
  34.4 16.2 %collective-permute-start.3 = (bf16[512,256]{1,0:T(8,128)(2,1)S(1)}, bf16[512,256]{1,0:T(8,128)(2,1)S(1)}, u32[]{:S(2)}, u32[]{:S(2)}) collective-permute-start(bf16[512,256]{1,0:T(8,128)(2,1)S(1)} %get-tuple-element.52), channel_id=1, source_target_pairs={{64,0},{80,16},{96,32},{112,48},{65,1},{81,17},{97,33},{113,49},{6... | collective-permute-start | bytes 786440 | tf_op jit(solution)/shard_map/ppermute | solution.py:588
  59.5 16.9 %collective-permute-start.6 = (bf16[640,256]{1,0:T(8,128)(2,1)S(1)}, bf16[640,256]{1,0:T(8,128)(2,1)S(1)}, u32[]{:S(2)}, u32[]{:S(2)}) collective-permute-start(bf16[640,256]{1,0:T(8,128)(2,1)S(1)} %get-tuple-element.60), channel_id=1, source_target_pairs={{0,48},{16,0},{32,16},{48,32},{64,112},{80,64},{96,80},{112,96},{1... | collective-permute-start | bytes 983048 | tf_op jit(solution)/shard_map/ppermute | solution.py:570
  62.8 17.0 %collective-permute-start.4 = (bf16[640,256]{1,0:T(8,128)(2,1)S(1)}, bf16[640,256]{1,0:T(8,128)(2,1)S(1)}, u32[]{:S(2)}, u32[]{:S(2)}) collective-permute-start(bf16[640,256]{1,0:T(8,128)(2,1)S(1)} %get-tuple-element.58), channel_id=1, source_target_pairs={{0,16},{16,32},{32,48},{48,0},{64,80},{80,96},{96,112},{112,64},{1... | collective-permute-start | bytes 983048 | tf_op jit(solution)/shard_map/ppermute | solution.py:570
  62.8 19.7 %collective-permute-start.5 = (bf16[640,256]{1,0:T(8,128)(2,1)S(1)}, bf16[640,256]{1,0:T(8,128)(2,1)S(1)}, u32[]{:S(2)}, u32[]{:S(2)}) collective-permute-start(bf16[640,256]{1,0:T(8,128)(2,1)S(1)} %get-tuple-element.59), channel_id=1, source_target_pairs={{0,32},{16,48},{32,0},{48,16},{64,96},{80,112},{96,64},{112,80},{1... | collective-permute-start | bytes 983048 | tf_op jit(solution)/shard_map/ppermute | solution.py:570
  82.5 4.0 %collective-permute-start.7 = (bf16[128,128]{1,0:T(8,128)(2,1)S(1)}, bf16[128,128]{1,0:T(8,128)(2,1)S(1)}, u32[]{:S(2)}, u32[]{:S(2)}) collective-permute-start(bf16[128,128]{1,0:T(8,128)(2,1)S(1)} %get-tuple-element.71), channel_id=1, source_target_pairs={{0,64},{16,80},{32,96},{48,112},{1,65},{17,81},{33,97},{49,113},{2... | collective-permute-start | bytes 98312 | tf_op jit(solution)/shard_map/ppermute | solution.py:595
  87.3 2.2 %collective-permute-start.8 = (bf16[4,2,112,384]{3,2,1,0:T(8,128)(2,1)S(1)}, bf16[4,2,112,384]{3,2,1,0:T(8,128)(2,1)S(1)}, u32[]{:S(2)}, u32[]{:S(2)}) collective-permute-start(bf16[4,2,112,384]{3,2,1,0:T(8,128)(2,1)S(1)} %get-tuple-element.73), channel_id=1, source_target_pairs={{0,1},{1,0},{2,3},{3,2},{4,5},{5,4},{6,7},{7,6},{8,9},{9,8},{10,11... | collective-permute-start | bytes 2064392 | tf_op jit(solution)/shard_map/ppermute | solution.py:511
  89.7 7.8 %collective-permute-start.9 = (bf16[2,112,384]{2,1,0:T(8,128)(2,1)S(1)}, bf16[2,112,384]{2,1,0:T(8,128)(2,1)S(1)}, u32[]{:S(2)}, u32[]{:S(2)}) collective-permute-start(bf16[2,112,384]{2,1,0:T(8,128)(2,1)S(1)} %get-tuple-element.75), channel_id=1, source_target_pairs={{0,2},{1,3},{2,4},{3,5},{4,6},{5,7},{6,0},{7,1},{8,10},{9,11},{10,... | collective-permute-start | bytes 516104 | tf_op jit(solution)/shard_map/ppermute | solution.py:511
  91.3 11.0 %collective-permute-start.10 = (bf16[2,112,384]{2,1,0:T(8,128)(2,1)S(1)}, bf16[2,112,384]{2,1,0:T(8,128)(2,1)S(1)}, u32[]{:S(2)}, u32[]{:S(2)}) collective-permute-start(bf16[2,112,384]{2,1,0:T(8,128)(2,1)S(1)} %get-tuple-element.76), channel_id=1, source_target_pairs={{0,4},{1,5},{2,6},{3,7},{4,0},{5,1},{6,2},{7,3},{8,12},{9,13},{10,... | collective-permute-start | bytes 516104 | tf_op jit(solution)/shard_map/ppermute | solution.py:511
  94.2 8.1 %collective-permute-start.11 = (bf16[2,112,384]{2,1,0:T(8,128)(2,1)S(1)}, bf16[2,112,384]{2,1,0:T(8,128)(2,1)S(1)}, u32[]{:S(2)}, u32[]{:S(2)}) collective-permute-start(bf16[2,112,384]{2,1,0:T(8,128)(2,1)S(1)} %get-tuple-element.77), channel_id=1, source_target_pairs={{0,6},{1,7},{2,0},{3,1},{4,2},{5,3},{6,4},{7,5},{8,14},{9,15},{10,... | collective-permute-start | bytes 516104 | tf_op jit(solution)/shard_map/ppermute | solution.py:511
  102.9 6.1 %collective-permute-start.12 = (bf16[112,384]{1,0:T(8,128)(2,1)S(1)}, bf16[112,384]{1,0:T(8,128)(2,1)S(1)}, u32[]{:S(2)}, u32[]{:S(2)}) collective-permute-start(bf16[112,384]{1,0:T(8,128)(2,1)S(1)} %get-tuple-element.79), channel_id=1, source_target_pairs={{0,8},{1,9},{2,10},{3,11},{4,12},{5,13},{6,14},{7,15},{8,0},{9,1},... | collective-permute-start | bytes 258056 | tf_op jit(solution)/shard_map/ppermute | solution.py:511

commit v8 on v7

--- a/solution.py
+++ b/solution.py
@@ -37,7 +37,7 @@
     return jnp.dot(a, b, preferred_element_type=F32)
 
 
-def back_step(source, tables, mixed, filtered, second, finish, ready=None):
+def back_step(source, tables, mixed, filtered, second, finish):
     inward, table, flipped, kernel_cos, kernel_sin = tables
     for part in (0, 1):
         even = dot(inward[0, half(part), :], source[0])
@@ -64,8 +64,6 @@
         for col in (0, 1):
             second[col, half(0), half(part)] = total[:, half(col)]
             second[col, half(1), half(part)] = diff[:, half(col)]
-    if ready is not None:
-        ready()
     totals, diffs = [], []
     for row in (0, 1):
         even = dot(second[0, half(row), :], table[0])
@@ -256,6 +254,7 @@
                 def _(k=k):
                     for parity in (0, 1):
                         outs[k][parity * N : (parity + 1) * N, :] = waves[k, parity]
+                    trans[...] = windows[(RING - k) % RING][...]
 
             source = waves.at[slot]
             target = waves.at[
@@ -263,24 +262,15 @@
             ]
             for layer, begin, end in ((1, source, middle), (0, middle, target)):
 
-                def ready(layer=layer):
-                    distance = (rank + RING - pair_at) % RING
-                    for k in range(RING):
-
-                        @pl.when(distance == k)
-                        def _(k=k):
-                            for parity in (0, 1):
-                                trans[parity] = windows[k][layer, parity]
-
                 def finish(parity, reals, imags, layer=layer, end=end):
                     for col in (0, 1):
-                        tr = trans[parity, half(0), half(col)].astype(F32)
-                        ti = trans[parity, half(1), half(col)].astype(F32)
+                        tr = trans[layer, parity, half(0), half(col)].astype(F32)
+                        ti = trans[layer, parity, half(1), half(col)].astype(F32)
                         qr, qi = reals[col], imags[col]
                         end[parity, half(0), half(col)] = (tr * qr + ti * qi).astype(BF)
                         end[parity, half(1), half(col)] = (tr * qi - ti * qr).astype(BF)
 
-                back_step(begin, tables, mixed, filtered, second, finish, ready)
+                back_step(begin, tables, mixed, filtered, second, finish)
             return carry
 
         lax.fori_loop(0, RING, pair, 0)
@@ -310,7 +300,7 @@
         in_specs=[SM] + [VM] * (RING + 6 + len(earlier)),
         out_specs=[VM] * count,
         scratch_shapes=[
-            pltpu.VMEM((2, N, N), BF),
+            pltpu.VMEM((2, 2, N, N), BF),
             pltpu.VMEM((RING + 1, 2, N, N), BF),
             pltpu.VMEM((2, N, N), BF),
             *step_scratch(),

time: 111 us -> 110 us (level)
  transfers between devices with their start and end apart: 13 -> 13, of which waited for: 9 -> 9; matrix products, arithmetic and copies ran while one was open for 0% -> 0% of each run, Pallas kernels for 13% -> 14%
where the time goes in v8:
time: 110 us; the launch traced here: 109 us
  waiting for transfers between devices  54.3 us (49%)
  Pallas kernels  29.7 us (27%)
  starting transfers between devices  22.9 us (21%)
  local copies, waits for them, and re-layouts  1.58 us (1%)
    ppermute x6, waiting for transfers between devices, turned(): return lax.ppermute(array, 'depth', route)  27.8 us
    ppermute x1, waiting for transfers between devices, shards(): lax.ppermute(leaving, 'depth', [(RING + i, i) for i in range(RING)])  14.4 us
    ppermute x5, waiting for transfers between devices, moved(): return lax.ppermute(array, 'probe', route)  12.1 us
    ppermute x6, starting transfers between devices, turned(): return lax.ppermute(array, 'depth', route)  11.5 us
    pallas_call x4, Pallas kernels, visit(): pl.pallas_call(functools.partial(visit_kernel, index), name=f'visit_{inde...  10.8 us
    pallas_call x2, Pallas kernels, run_chain(): pl.pallas_call(functools.partial(chain_kernel, first), name='chain_deep'...  8.92 us
    ppermute x5, starting transfers between devices, moved(): return lax.ppermute(array, 'probe', route)  8.85 us
    pallas_call x1, Pallas kernels, transmission_windows(): pl.pallas_call(window_kernel, name='windows', out_shape=[shape] * RING, i...  3.7 us
  transfers between devices with their start and end apart: 13, of which 9 were waited for; matrix products, arithmetic and copies ran while one was open for 0% of the time, Pallas kernels for 14%

profile of v8, /device:TPU:0, one launch (start us, length us, event | category | flops | bytes accessed | tf_op | source)
XLA Modules:
  0.0 109.4 jit_solution(9299931913586562079)
XLA Ops:
  0.6 0.0 copy-start
  0.7 0.8 copy.15.offsets
  1.5 0.1 stack.23.where
  1.6 3.7 %windows.1 = (bf16[2,2,256,256]{3,2,1,0:T(8,128)(2,1)S(1)}, bf16[2,2,256,256]{3,2,1,0:T(8,128)(2,1)S(1)}, bf16[2,2,256,256]{3,2,1,0:T(8,128)(2,1)S(1)}, bf16[2,2,256,256]{3,2,1,0:T(8,128)(2,1)S(1)}) custom-call(s32[5]{0:T(128)S(1)} %stack.23.where, s32[4,2]{1,0:T(4,128)S(1)} %copy.15.offsets, f32[2,384,384]{2,1,0:T(8,128)} %phase_all.1, f32[2,384,384]{2,1,0:T(8,128)} %amp_all.1), custom_call_target="tpu_custom_call" | custom-call | tf_op jit(solution)/shard_map/windows/pallas_call | solution.py:202
  5.3 2.1 %collective-permute-start = (bf16[2,2,256,256]{3,2,1,0:T(8,128)(2,1)S(1)}, bf16[2,2,256,256]{3,2,1,0:T(8,128)(2,1)S(1)}, u32[]{:S(2)}, u32[]{:S(2)}) collective-permute-start(bf16[2,2,256,256]{3,2,1,0:T(8,128)(2,1)S(1)} %get-tuple-element.44.window), channel_id=1, source_target_pairs={{0,16},{16,32},{32,48},{48,0},{64,80},{80,96},{96,112},{112,64},{1... | collective-permute-start | bytes 1572872 | tf_op jit(solution)/shard_map/ppermute | solution.py:560
  7.4 3.6 %collective-permute-start.1 = (bf16[2,2,256,256]{3,2,1,0:T(8,128)(2,1)S(1)}, bf16[2,2,256,256]{3,2,1,0:T(8,128)(2,1)S(1)}, u32[]{:S(2)}, u32[]{:S(2)}) collective-permute-start(bf16[2,2,256,256]{3,2,1,0:T(8,128)(2,1)S(1)} %get-tuple-element.45.window), channel_id=1, source_target_pairs={{0,32},{16,48},{32,0},{48,16},{64,96},{80,112},{96,64},{112,80},{1... | collective-permute-start | bytes 1572872 | tf_op jit(solution)/shard_map/ppermute | solution.py:560
  11.0 1.0 collective-permute-start.2
  12.0 0.0 copy-done
  12.0 1.1 filters.1
  13.0 3.0 %reorder.1 = (bf16[512,256]{1,0:T(8,128)(2,1)S(1)}, bf16[2,2,256,256]{3,2,1,0:T(8,128)(2,1)S(1)}, bf16[2,2,256,256]{3,2,1,0:T(8,128)(2,1)S(1)}, bf16[2,2,256,256...) custom-call(s32[5]{0:T(128)S(1)} %stack.23.where, bf16[4,2,256,256]{3,2,1,0:T(8,128)(2,1)} %residual.1, ...), custom_call_target="tpu_custom_call" | custom-call | tf_op jit(solution)/shard_map/reorder/pallas_call | solution.py:537
  16.0 5.4 %collective-permute-done.rest_1_ = bf16[2,2,256,256]{3,2,1,0:T(8,128)(2,1)S(1)} collective-permute-done((bf16[2,2,256,256]{3,2,1,0:T(8,128)(2,1)S(1)}, bf16[2,2,256,256]{3,2,1,0:T(8,128)(2,1)S(1)}, u32[]{:S(2)}, u32[]{:S(2)}) %collective-permute-start) | collective-permute-done | bytes 524320 | tf_op jit(solution)/shard_map/ppermute | solution.py:560
  21.4 12.4 %collective-permute-done.1.rest_2_ = bf16[2,2,256,256]{3,2,1,0:T(8,128)(2,1)S(1)} collective-permute-done((bf16[2,2,256,256]{3,2,1,0:T(8,128)(2,1)S(1)}, bf16[2,2,256,256]{3,2,1,0:T(8,128)(2,1)S(1)}, u32[]{:S(2)}, u32[]{:S(2)}) %collective-permute-start.1) | collective-permute-done | bytes 524320 | tf_op jit(solution)/shard_map/ppermute | solution.py:560
  33.8 0.0 collective-permute-done.2.rest_3_
  33.8 0.5 chain_deep.1
  34.4 1.3 %collective-permute-start.3 = (bf16[512,256]{1,0:T(8,128)(2,1)S(1)}, bf16[512,256]{1,0:T(8,128)(2,1)S(1)}, u32[]{:S(2)}, u32[]{:S(2)}) collective-permute-start(bf16[512,256]{1,0:T(8,128)(2,1)S(1)} %get-tuple-element.52), channel_id=1, source_target_pairs={{64,0},{80,16},{96,32},{112,48},{65,1},{81,17},{97,33},{113,49},{6... | collective-permute-start | bytes 786440 | tf_op jit(solution)/shard_map/ppermute | solution.py:578
  35.7 14.4 %collective-permute-done.3.start = bf16[512,256]{1,0:T(8,128)(2,1)S(1)} collective-permute-done((bf16[512,256]{1,0:T(8,128)(2,1)S(1)}, bf16[512,256]{1,0:T(8,128)(2,1)S(1)}, u32[]{:S(2)}, u32[]{:S(2)}) %collective-permute-start.3) | collective-permute-done | bytes 262176 | tf_op jit(solution)/shard_map/ppermute | solution.py:578
  50.1 8.4 %chain_top.1 = (bf16[640,256]{1,0:T(8,128)(2,1)S(1)}, bf16[640,256]{1,0:T(8,128)(2,1)S(1)}, bf16[640,256]{1,0:T(8,128)(2,1)S(1)}, bf16[640,256]{1,0:T(8,128)(2,1)S(1)}) custom-call(s32[5]{0:T(128)S(1)} %stack.23.where, bf16[512,256]{1,0:T(8,128)(2,1)S(1)} %collective-permute-done.3.start, bf16[2,2,256,256]{3,2,1,0:T(8,128)(2,1)S(1)} %get-tuple-element.43.rest_0_.window, ...), custom_call_target="tpu_custom_call" | custom-call | tf_op jit(solution)/shard_map/chain_top/pallas_call | solution.py:296
  58.5 3.3 %collective-permute-start.6 = (bf16[640,256]{1,0:T(8,128)(2,1)S(1)}, bf16[640,256]{1,0:T(8,128)(2,1)S(1)}, u32[]{:S(2)}, u32[]{:S(2)}) collective-permute-start(bf16[640,256]{1,0:T(8,128)(2,1)S(1)} %get-tuple-element.60), channel_id=1, source_target_pairs={{0,48},{16,0},{32,16},{48,32},{64,112},{80,64},{96,80},{112,96},{1... | collective-permute-start | bytes 983048 | tf_op jit(solution)/shard_map/ppermute | solution.py:560
  61.7 0.0 collective-permute-start.4
  61.7 1.5 %collective-permute-start.5 = (bf16[640,256]{1,0:T(8,128)(2,1)S(1)}, bf16[640,256]{1,0:T(8,128)(2,1)S(1)}, u32[]{:S(2)}, u32[]{:S(2)}) collective-permute-start(bf16[640,256]{1,0:T(8,128)(2,1)S(1)} %get-tuple-element.59), channel_id=1, source_target_pairs={{0,32},{16,48},{32,0},{48,16},{64,96},{80,112},{96,64},{112,80},{1... | collective-permute-start | bytes 983048 | tf_op jit(solution)/shard_map/ppermute | solution.py:560
  63.3 2.8 %visit_0.1.rest_5_ = f32[2,2,3,384,128]{4,3,2,1,0:T(8,128)S(1)} custom-call(s32[5]{0:T(128)S(1)} %stack.23.where, s32[4,2]{1,0:T(4,128)S(1)} %copy.15.offsets, bf16[640,256]{1,0:T(8,128)(2,1)S(1)} %get-tuple-element.67.entry.refs_0_, bf16[2,2,256,256]{3,2,1,0:T(8,128)(2,1)S(1)} %get-tuple-element.43.rest_0_.window, ...), custom_call_target="tpu_custom_call" | custom-call | tf_op jit(solution)/shard_map/visit_0/pallas_call | solution.py:359
  66.1 9.2 %collective-permute-done.6.entry.refs_3_ = bf16[640,256]{1,0:T(8,128)(2,1)S(1)} collective-permute-done((bf16[640,256]{1,0:T(8,128)(2,1)S(1)}, bf16[640,256]{1,0:T(8,128)(2,1)S(1)}, u32[]{:S(2)}, u32[]{:S(2)}) %collective-permute-start.6) | collective-permute-done | bytes 327712 | tf_op jit(solution)/shard_map/ppermute | solution.py:560
  75.3 2.7 %visit_3.1.rest_5_ = f32[2,2,3,384,128]{4,3,2,1,0:T(8,128)S(1)} custom-call(s32[5]{0:T(128)S(1)} %stack.23.where, s32[4,2]{1,0:T(4,128)S(1)} %copy.15.offsets, bf16[640,256]{1,0:T(8,128)(2,1)S(1)} %collective-permute-done.6.entry.refs_3_, bf16[2,2,256,256]{3,2,1,0:T(8,128)(2,1)S(1)} %get-tuple-element.44.window, ...), custom_call_target="tpu_custom_call", output_to_operand_aliasing={{}: (10, {})} | custom-call | tf_op jit(solution)/shard_map/visit_3/pallas_call | solution.py:359
  78.0 0.7 collective-permute-done.4.entry.refs_1_
  78.8 2.7 %visit_1.1.rest_5_ = f32[2,2,3,384,128]{4,3,2,1,0:T(8,128)S(1)} custom-call(s32[5]{0:T(128)S(1)} %stack.23.where, s32[4,2]{1,0:T(4,128)S(1)} %copy.15.offsets, bf16[640,256]{1,0:T(8,128)(2,1)S(1)} %collective-permute-done.4.entry.refs_1_, bf16[2,2,256,256]{3,2,1,0:T(8,128)(2,1)S(1)} %get-tuple-element.46.window, ...), custom_call_target="tpu_custom_call", output_to_operand_aliasing={{}: (10, {})} | custom-call | tf_op jit(solution)/shard_map/visit_1/pallas_call | solution.py:359
  81.4 0.0 collective-permute-done.5.entry.refs_2_
  81.5 1.3 %collective-permute-start.7 = (bf16[128,128]{1,0:T(8,128)(2,1)S(1)}, bf16[128,128]{1,0:T(8,128)(2,1)S(1)}, u32[]{:S(2)}, u32[]{:S(2)}) collective-permute-start(bf16[128,128]{1,0:T(8,128)(2,1)S(1)} %get-tuple-element.71), channel_id=1, source_target_pairs={{0,64},{16,80},{32,96},{48,112},{1,65},{17,81},{33,97},{49,113},{2... | collective-permute-start | bytes 98312 | tf_op jit(solution)/shard_map/ppermute | solution.py:585
  82.8 2.7 %visit_2.1.grads = f32[2,2,3,384,128]{4,3,2,1,0:T(8,128)S(1)} custom-call(s32[5]{0:T(128)S(1)} %stack.23.where, s32[4,2]{1,0:T(4,128)S(1)} %copy.15.offsets, bf16[640,256]{1,0:T(8,128)(2,1)S(1)} %collective-permute-done.5.entry.refs_2_, bf16[2,2,256,256]{3,2,1,0:T(8,128)(2,1)S(1)} %get-tuple-element.45.window, ...), custom_call_target="tpu_custom_call", output_to_operand_aliasing={{}: (10, {})} | custom-call | tf_op jit(solution)/shard_map/visit_2/pallas_call | solution.py:359
  85.5 0.0 collective-permute-done.7.far_probe
  85.5 0.7 pack.1
  86.2 0.1 collective-permute-start.8
  86.3 2.1 %collective-permute-done.8.arrived = bf16[4,2,112,384]{3,2,1,0:T(8,128)(2,1)S(1)} collective-permute-done((bf16[4,2,112,384]{3,2,1,0:T(8,128)(2,1)S(1)}, bf16[4,2,112,384]{3,2,1,0:T(8,128)(2,1)S(1)}, u32[]{:S(2)}, u32[]{:S(2)}) %collective-permute-start.8) | collective-permute-done | bytes 688160 | tf_op jit(solution)/shard_map/ppermute | solution.py:501
  88.4 0.2 core_sum.1
  88.6 1.7 %collective-permute-start.9 = (bf16[2,112,384]{2,1,0:T(8,128)(2,1)S(1)}, bf16[2,112,384]{2,1,0:T(8,128)(2,1)S(1)}, u32[]{:S(2)}, u32[]{:S(2)}) collective-permute-start(bf16[2,112,384]{2,1,0:T(8,128)(2,1)S(1)} %get-tuple-element.75), channel_id=1, source_target_pairs={{0,2},{1,3},{2,4},{3,5},{4,6},{5,7},{6,0},{7,1},{8,10},{9,11},{10,... | collective-permute-start | bytes 516104 | tf_op jit(solution)/shard_map/ppermute | solution.py:501
  90.3 2.9 %collective-permute-start.10 = (bf16[2,112,384]{2,1,0:T(8,128)(2,1)S(1)}, bf16[2,112,384]{2,1,0:T(8,128)(2,1)S(1)}, u32[]{:S(2)}, u32[]{:S(2)}) collective-permute-start(bf16[2,112,384]{2,1,0:T(8,128)(2,1)S(1)} %get-tuple-element.76), channel_id=1, source_target_pairs={{0,4},{1,5},{2,6},{3,7},{4,0},{5,1},{6,2},{7,3},{8,12},{9,13},{10,... | collective-permute-start | bytes 516104 | tf_op jit(solution)/shard_map/ppermute | solution.py:501
  93.2 1.4 %collective-permute-start.11 = (bf16[2,112,384]{2,1,0:T(8,128)(2,1)S(1)}, bf16[2,112,384]{2,1,0:T(8,128)(2,1)S(1)}, u32[]{:S(2)}, u32[]{:S(2)}) collective-permute-start(bf16[2,112,384]{2,1,0:T(8,128)(2,1)S(1)} %get-tuple-element.77), channel_id=1, source_target_pairs={{0,6},{1,7},{2,0},{3,1},{4,2},{5,3},{6,4},{7,5},{8,14},{9,15},{10,... | collective-permute-start | bytes 516104 | tf_op jit(solution)/shard_map/ppermute | solution.py:501
  94.6 1.8 %collective-permute-done.9.rest_1_ = bf16[2,112,384]{2,1,0:T(8,128)(2,1)S(1)} collective-permute-done((bf16[2,112,384]{2,1,0:T(8,128)(2,1)S(1)}, bf16[2,112,384]{2,1,0:T(8,128)(2,1)S(1)}, u32[]{:S(2)}, u32[]{:S(2)}) %collective-permute-start.9) | collective-permute-done | bytes 172064 | tf_op jit(solution)/shard_map/ppermute | solution.py:501
  96.4 4.9 %collective-permute-done.10.rest_2_ = bf16[2,112,384]{2,1,0:T(8,128)(2,1)S(1)} collective-permute-done((bf16[2,112,384]{2,1,0:T(8,128)(2,1)S(1)}, bf16[2,112,384]{2,1,0:T(8,128)(2,1)S(1)}, u32[]{:S(2)}, u32[]{:S(2)}) %collective-permute-start.10) | collective-permute-done | bytes 172064 | tf_op jit(solution)/shard_map/ppermute | solution.py:501
  101.3 0.0 collective-permute-done.11.rest_3_
  101.3 0.6 ring_sum.1
  101.9 2.8 %collective-permute-start.12 = (bf16[112,384]{1,0:T(8,128)(2,1)S(1)}, bf16[112,384]{1,0:T(8,128)(2,1)S(1)}, u32[]{:S(2)}, u32[]{:S(2)}) collective-permute-start(bf16[112,384]{1,0:T(8,128)(2,1)S(1)} %get-tuple-element.79), channel_id=1, source_target_pairs={{0,8},{1,9},{2,10},{3,11},{4,12},{5,13},{6,14},{7,15},{8,0},{9,1},... | collective-permute-start | bytes 258056 | tf_op jit(solution)/shard_map/ppermute | solution.py:501
  104.7 3.2 %collective-permute-done.12.arrived = bf16[112,384]{1,0:T(8,128)(2,1)S(1)} collective-permute-done((bf16[112,384]{1,0:T(8,128)(2,1)S(1)}, bf16[112,384]{1,0:T(8,128)(2,1)S(1)}, u32[]{:S(2)}, u32[]{:S(2)}) %collective-permute-start.12) | collective-permute-done | bytes 86048 | tf_op jit(solution)/shard_map/ppermute | solution.py:501
  108.0 0.7 last_sum.1
  108.7 0.1 reshape.14
  108.7 0.6 copy.16
  (1 shorter events, 0.0 us)
Async XLA Ops:
  0.6 11.3 %copy-start = (f32[256,256]{1,0:T(8,128)S(1)}, f32[256,256]{1,0:T(8,128)}, u32[]{:S(2)}) copy-start(f32[256,256]{1,0:T(8,128)} %phase.1) | copy-start | bytes 786436
  5.3 16.1 %collective-permute-start = (bf16[2,2,256,256]{3,2,1,0:T(8,128)(2,1)S(1)}, bf16[2,2,256,256]{3,2,1,0:T(8,128)(2,1)S(1)}, u32[]{:S(2)}, u32[]{:S(2)}) collective-permute-start(bf16[2,2,256,256]{3,2,1,0:T(8,128)(2,1)S(1)} %get-tuple-element.44.window), channel_id=1, source_target_pairs={{0,16},{16,32},{32,48},{48,0},{64,80},{80,96},{96,112},{112,64},{1... | collective-permute-start | bytes 1572872 | tf_op jit(solution)/shard_map/ppermute | solution.py:560
  7.4 26.5 %collective-permute-start.1 = (bf16[2,2,256,256]{3,2,1,0:T(8,128)(2,1)S(1)}, bf16[2,2,256,256]{3,2,1,0:T(8,128)(2,1)S(1)}, u32[]{:S(2)}, u32[]{:S(2)}) collective-permute-start(bf16[2,2,256,256]{3,2,1,0:T(8,128)(2,1)S(1)} %get-tuple-element.45.window), channel_id=1, source_target_pairs={{0,32},{16,48},{32,0},{48,16},{64,96},{80,112},{96,64},{112,80},{1... | collective-permute-start | bytes 1572872 | tf_op jit(solution)/shard_map/ppermute | solution.py:560
  11.0 22.9 %collective-permute-start.2 = (bf16[2,2,256,256]{3,2,1,0:T(8,128)(2,1)S(1)}, bf16[2,2,256,256]{3,2,1,0:T(8,128)(2,1)S(1)}, u32[]{:S(2)}, u32[]{:S(2)}) collective-permute-start(bf16[2,2,256,256]{3,2,1,0:T(8,128)(2,1)S(1)} %get-tuple-element.46.window), channel_id=1, source_target_pairs={{0,48},{16,0},{32,16},{48,32},{64,112},{80,64},{96,80},{112,96},{1... | collective-permute-start | bytes 1572872 | tf_op jit(solution)/shard_map/ppermute | solution.py:560
  34.4 15.7 %collective-permute-start.3 = (bf16[512,256]{1,0:T(8,128)(2,1)S(1)}, bf16[512,256]{1,0:T(8,128)(2,1)S(1)}, u32[]{:S(2)}, u32[]{:S(2)}) collective-permute-start(bf16[512,256]{1,0:T(8,128)(2,1)S(1)} %get-tuple-element.52), channel_id=1, source_target_pairs={{64,0},{80,16},{96,32},{112,48},{65,1},{81,17},{97,33},{113,49},{6... | collective-permute-start | bytes 786440 | tf_op jit(solution)/shard_map/ppermute | solution.py:578
  58.5 16.9 %collective-permute-start.6 = (bf16[640,256]{1,0:T(8,128)(2,1)S(1)}, bf16[640,256]{1,0:T(8,128)(2,1)S(1)}, u32[]{:S(2)}, u32[]{:S(2)}) collective-permute-start(bf16[640,256]{1,0:T(8,128)(2,1)S(1)} %get-tuple-element.60), channel_id=1, source_target_pairs={{0,48},{16,0},{32,16},{48,32},{64,112},{80,64},{96,80},{112,96},{1... | collective-permute-start | bytes 983048 | tf_op jit(solution)/shard_map/ppermute | solution.py:560
  61.7 17.0 %collective-permute-start.4 = (bf16[640,256]{1,0:T(8,128)(2,1)S(1)}, bf16[640,256]{1,0:T(8,128)(2,1)S(1)}, u32[]{:S(2)}, u32[]{:S(2)}) collective-permute-start(bf16[640,256]{1,0:T(8,128)(2,1)S(1)} %get-tuple-element.58), channel_id=1, source_target_pairs={{0,16},{16,32},{32,48},{48,0},{64,80},{80,96},{96,112},{112,64},{1... | collective-permute-start | bytes 983048 | tf_op jit(solution)/shard_map/ppermute | solution.py:560
  61.7 19.7 %collective-permute-start.5 = (bf16[640,256]{1,0:T(8,128)(2,1)S(1)}, bf16[640,256]{1,0:T(8,128)(2,1)S(1)}, u32[]{:S(2)}, u32[]{:S(2)}) collective-permute-start(bf16[640,256]{1,0:T(8,128)(2,1)S(1)} %get-tuple-element.59), channel_id=1, source_target_pairs={{0,32},{16,48},{32,0},{48,16},{64,96},{80,112},{96,64},{112,80},{1... | collective-permute-start | bytes 983048 | tf_op jit(solution)/shard_map/ppermute | solution.py:560
  81.5 4.0 %collective-permute-start.7 = (bf16[128,128]{1,0:T(8,128)(2,1)S(1)}, bf16[128,128]{1,0:T(8,128)(2,1)S(1)}, u32[]{:S(2)}, u32[]{:S(2)}) collective-permute-start(bf16[128,128]{1,0:T(8,128)(2,1)S(1)} %get-tuple-element.71), channel_id=1, source_target_pairs={{0,64},{16,80},{32,96},{48,112},{1,65},{17,81},{33,97},{49,113},{2... | collective-permute-start | bytes 98312 | tf_op jit(solution)/shard_map/ppermute | solution.py:585
  86.2 2.2 %collective-permute-start.8 = (bf16[4,2,112,384]{3,2,1,0:T(8,128)(2,1)S(1)}, bf16[4,2,112,384]{3,2,1,0:T(8,128)(2,1)S(1)}, u32[]{:S(2)}, u32[]{:S(2)}) collective-permute-start(bf16[4,2,112,384]{3,2,1,0:T(8,128)(2,1)S(1)} %get-tuple-element.73), channel_id=1, source_target_pairs={{0,1},{1,0},{2,3},{3,2},{4,5},{5,4},{6,7},{7,6},{8,9},{9,8},{10,11... | collective-permute-start | bytes 2064392 | tf_op jit(solution)/shard_map/ppermute | solution.py:501
  88.6 7.8 %collective-permute-start.9 = (bf16[2,112,384]{2,1,0:T(8,128)(2,1)S(1)}, bf16[2,112,384]{2,1,0:T(8,128)(2,1)S(1)}, u32[]{:S(2)}, u32[]{:S(2)}) collective-permute-start(bf16[2,112,384]{2,1,0:T(8,128)(2,1)S(1)} %get-tuple-element.75), channel_id=1, source_target_pairs={{0,2},{1,3},{2,4},{3,5},{4,6},{5,7},{6,0},{7,1},{8,10},{9,11},{10,... | collective-permute-start | bytes 516104 | tf_op jit(solution)/shard_map/ppermute | solution.py:501
  90.3 11.0 %collective-permute-start.10 = (bf16[2,112,384]{2,1,0:T(8,128)(2,1)S(1)}, bf16[2,112,384]{2,1,0:T(8,128)(2,1)S(1)}, u32[]{:S(2)}, u32[]{:S(2)}) collective-permute-start(bf16[2,112,384]{2,1,0:T(8,128)(2,1)S(1)} %get-tuple-element.76), channel_id=1, source_target_pairs={{0,4},{1,5},{2,6},{3,7},{4,0},{5,1},{6,2},{7,3},{8,12},{9,13},{10,... | collective-permute-start | bytes 516104 | tf_op jit(solution)/shard_map/ppermute | solution.py:501
  93.2 8.1 %collective-permute-start.11 = (bf16[2,112,384]{2,1,0:T(8,128)(2,1)S(1)}, bf16[2,112,384]{2,1,0:T(8,128)(2,1)S(1)}, u32[]{:S(2)}, u32[]{:S(2)}) collective-permute-start(bf16[2,112,384]{2,1,0:T(8,128)(2,1)S(1)} %get-tuple-element.77), channel_id=1, source_target_pairs={{0,6},{1,7},{2,0},{3,1},{4,2},{5,3},{6,4},{7,5},{8,14},{9,15},{10,... | collective-permute-start | bytes 516104 | tf_op jit(solution)/shard_map/ppermute | solution.py:501
  101.9 6.1 %collective-permute-start.12 = (bf16[112,384]{1,0:T(8,128)(2,1)S(1)}, bf16[112,384]{1,0:T(8,128)(2,1)S(1)}, u32[]{:S(2)}, u32[]{:S(2)}) collective-permute-start(bf16[112,384]{1,0:T(8,128)(2,1)S(1)} %get-tuple-element.79), channel_id=1, source_target_pairs={{0,8},{1,9},{2,10},{3,11},{4,12},{5,13},{6,14},{7,15},{8,0},{9,1},... | collective-permute-start | bytes 258056 | tf_op jit(solution)/shard_map/ppermute | solution.py:501
